TPU v7x, 256 devices: a whole 4x4x8 slice. The times are simulated.
256 devices in a mesh: roll: 16 (over z, x_hi), trans: 4 (over y), case: 4 (over x_lo, core).
Axes of the slice: x: 4 (x_hi: 2, x_lo: 2; x = x_hi * 2 + x_lo), y: 4, z: 8, core: 2. Of those that a mesh axis runs over, the one named last changes fastest.
Arguments:
- ratio_index: int32 [8], P('case'), may hold values from 0 to 15
- shifts: int32 [4], replicated, may hold values from 1 to 8, as said below
- kernel: float32 [31], replicated, may hold values from -0.06 to 0.06
- diagonal: float32 [8, 4096, 2048], P('case', 'roll', 'trans'), may hold values from 4.5 to 6
- flow_x: float32 [8, 4096, 2048], P('case', 'roll', 'trans'), may hold values from 0.1 to 0.5
- flow_y: float32 [8, 4096, 2048], P('case', 'roll', 'trans'), may hold values from 0.1 to 0.5
- pres_source: float32 [8, 4, 4096, 2048], P('case', None, 'roll', 'trans'), may hold values from -6 to 6
- rough_adjoint: float32 [8, 4096, 2048], P('case', 'roll', 'trans'), may hold values from -6 to 6
Outputs:
- pres_adjoint: float32 [8, 4096, 2048], P('case', 'roll', 'trans')
- film_adjoint: float32 [8, 4096, 2048], P('case', 'roll', 'trans')
- rough_gradient: float32 [4096, 2048], P('roll', 'trans')
Inputs may be any that keep to these rules, and one draw needn't show every extreme that they name: Each step's shift is at least 1 and at most 8; some step shifts by exactly 8.
All inputs are finite; a program needn't handle non-finite values.
Results may differ from a plain program's by a relative error of at most 0.00002.
Values sent between devices are 32-bit elements; how exact they have to be, the bound alone decides.
No kernel may reach another device: no remote copies, remote signals or barrier semaphores. Data moves between devices by JAX's collectives and lax.ppermute only.
A program may use at most 128 MiB of HBM per device.

v0:
```python
import jax
import jax.numpy as jnp
from jax import lax
from jax.sharding import PartitionSpec as P

STEPS = 4
SWEEPS = 3
SMAX = 8
NSRR = 16


def with_halo(block, sides, width):
    for axis, dim in sides:
        count = lax.axis_size(axis)
        forward = [(i, i + 1) for i in range(count - 1)]
        backward = [(target, source) for source, target in forward]
        low = lax.ppermute(
            lax.slice_in_dim(block, block.shape[dim] - width, None, axis=dim), axis, forward
        )
        high = lax.ppermute(lax.slice_in_dim(block, 0, width, axis=dim), axis, backward)
        block = jnp.concatenate([low, block, high], axis=dim)
    return block


def passed_along(block, axis, distance):
    devices = range(lax.axis_size(axis))
    route = [(i - distance, i) for i in devices if i - distance in devices]
    return lax.ppermute(block, axis, route)


def relax(lam, rhs, diag, flow_x, flow_y, kernel):
    half = kernel.shape[0] // 2
    rows = lam.shape[1]
    rolled = with_halo(lam, (("roll", 1),), half)
    side = with_halo(lam, (("trans", 2),), 1)
    conv = jnp.zeros(lam.shape, jnp.float32)
    for k in range(kernel.shape[0]):
        conv = conv + kernel[k] * rolled[:, k : k + rows]
    beside = flow_x * (
        rolled[:, half + 1 : half + 1 + rows] + rolled[:, half - 1 : half - 1 + rows]
    )
    beside = beside + flow_y * (side[:, :, 2:] + side[:, :, :-2])
    return lam + 0.8 * (rhs - diag * lam + beside - conv) / diag


def on_device(ratio_index, shifts, kernel, diagonal, flow_x, flow_y, pres_source, rough_adjoint):
    ratio = (0.2 + 1.6 * ratio_index.astype(jnp.float32) / (NSRR - 1)).reshape(-1, 1, 1)
    rows = diagonal.shape[1]
    lam = jnp.zeros(diagonal.shape, jnp.float32)
    film = rough_adjoint
    gradient = jnp.zeros(diagonal.shape[1:], jnp.float32)
    for step in range(STEPS - 1, -1, -1):
        rhs = pres_source[:, step] + ratio * film
        for sweep in range(SWEEPS):
            lam = relax(lam, rhs, diagonal, flow_x, flow_y, kernel)
        term = jnp.sum(lam * film, axis=0)
        gradient = gradient + lax.psum(term, "case")
        incoming = passed_along(film, "roll", -1)[:, :SMAX]
        extended = jnp.concatenate([film, incoming], axis=1)
        moved = lax.dynamic_slice_in_dim(extended, shifts[step], rows, 1)
        film = moved + ratio * lam
    return (lam, film, gradient)


def solution(mesh):
    in_specs = (
        P("case"),
        P(),
        P(),
        P("case", "roll", "trans"),
        P("case", "roll", "trans"),
        P("case", "roll", "trans"),
        P("case", None, "roll", "trans"),
        P("case", "roll", "trans"),
    )
    out_specs = (P("case", "roll", "trans"), P("case", "roll", "trans"), P("roll", "trans"))
    return jax.shard_map(
        on_device, mesh=mesh, in_specs=in_specs, out_specs=out_specs, check_vma=False
    )
```

profile of v0, /device:TPU:1, one launch (start us, length us, event | category | flops | bytes accessed | tf_op | source)
XLA Modules:
  0.0 858.3 jit_solution(7031954421460518734)
XLA Ops:
  25.7 22.6 %fusion.14 = (f32[2,256,512]{2,1,0:T(8,128)S(1)}, f32[2,256,512]{2,1,0:T(8,128)}) fusion(f32[2,256,512]{2,1,0:T(8,128)} %param.11, f32[2,256,512]{2,1,0:T(8,128)} %param.13, f32[2,256,1]{2,1,0:T(8,128)S(1)} %collective-permute-done.2, f32[2,256,1]{2,1,0:T(8,128)S(1)} %collective-permute-done.3, f32[2,15,512]{2,1,0:T(8,128)S(1)} %collective-permute-done, ...), kind=kLoop, calls=%fused_computation.362 | loop fusion | flops 19136512 | bytes 7467140 | tf_op jit(solution)/shard_map/div | solution.py:43
  63.8 45.6 %divide_add_fusion.10 = f32[2,256,512]{2,1,0:T(8,128)} fusion(f32[2,256,512]{2,1,0:T(8,128)} %copy-done.3, f32[2,256,512]{2,1,0:T(8,128)S(1)} %copy-done, f32[2,15,512]{2,1,0:T(8,128)S(1)} %collective-permute-done.4, f32[2,15,512]{2,1,0:T(8,128)S(1)} %collective-permute-done.5, f32[2,256,512]{2,1,0:T(8,128)S(1)} %copy-done.1, ...), kind=kLoop, calls=%fused_computation.1746 | loop fusion | flops 27525120 | bytes 6418556 | tf_op jit(solution)/shard_map/add | solution.py:43
  127.7 44.2 %multiply_reduce_fusion.3 = (f32[256,512]{1,0:T(8,128)}, f32[2,256,512]{2,1,0:T(8,128)}) fusion(f32[2,256,512]{2,1,0:T(8,128)} %param.15, f32[2,256,512]{2,1,0:T(8,128)} %divide_add_fusion.10, f32[2,256,512]{2,1,0:T(8,128)S(1)} %copy-done, f32[2,15,512]{2,1,0:T(8,128)S(1)} %collective-permute-done.8, f32[]{:T(128)} %bitcast.31, f32[]{:T(128)} %bitcast.30, ...), kind=kLoop, calls=%fused_computation.1735 | loop fusion | flops 27918336 | bytes 7991420 | tf_op jit(solution)/shard_map/reduce_sum | solution.py:56
  173.4 5.9 collective-permute-start.14
  183.8 5.6 collective-permute-start.16
  193.0 46.3 %divide_add_fusion.8 = (f32[2,256,512]{2,1,0:T(8,128)}, f32[2,256,512]{2,1,0:T(8,128)}, f32[2,256,512]{2,1,0:T(8,128)}) fusion(f32[2,256,512]{2,1,0:T(8,128)} %get-tuple-element.6, f32[2,256,512]{2,1,0:T(8,128)S(1)} %copy-done, f32[2,15,512]{2,1,0:T(8,128)} %collective-permute-done.13, f32[2,15,512]{2,1,0:T(8,128)S(1)} %collective-permute-done.14, ...), kind=kLoop, calls=%fused_computation.1744 | loop fusion | flops 28835840 | bytes 9597064 | tf_op jit(solution)/shard_map/add | solution.py:43
  240.2 6.2 collective-permute-start.18
  257.5 45.7 %divide_add_fusion.7 = f32[2,256,512]{2,1,0:T(8,128)} fusion(f32[2,256,512]{2,1,0:T(8,128)} %get-tuple-element.17, f32[2,256,512]{2,1,0:T(8,128)S(1)} %copy-done, f32[2,15,512]{2,1,0:T(8,128)S(1)} %collective-permute-done.17, f32[2,15,512]{2,1,0:T(8,128)S(1)} %collective-permute-done.18, f32[2,256,512]{2,1,0:T(8,128)S(1)} %copy-done.1, ...), kind=kLoop, calls=%fused_computation.1743 | loop fusion | flops 27525120 | bytes 6418556 | tf_op jit(solution)/shard_map/add | solution.py:43
  304.1 6.4 collective-permute-start.22
  322.1 46.0 %multiply_reduce_fusion.2 = (f32[256,512]{1,0:T(8,128)}, f32[2,256,512]{2,1,0:T(8,128)}) fusion(f32[2,256,512]{2,1,0:T(8,128)} %get-tuple-element.19, f32[2,256,512]{2,1,0:T(8,128)} %divide_add_fusion.7, f32[2,256,512]{2,1,0:T(8,128)S(1)} %copy-done, f32[2,15,512]{2,1,0:T(8,128)S(1)} %collective-permute-done.21, f32[]{:T(128)} %bitcast.31, f32[]{:T(128)} %bitcast.30, ...), kind=kLoop, calls=%fused_computation.1734 | loop fusion | flops 27918336 | bytes 7991420 | tf_op jit(solution)/shard_map/reduce_sum | solution.py:56
  369.6 6.4 collective-permute-start.27
  388.6 47.3 %divide_add_fusion.5 = (f32[2,256,512]{2,1,0:T(8,128)}, f32[2,256,512]{2,1,0:T(8,128)}, f32[2,256,512]{2,1,0:T(8,128)}) fusion(f32[2,256,512]{2,1,0:T(8,128)} %get-tuple-element.4, f32[2,256,512]{2,1,0:T(8,128)S(1)} %copy-done, f32[2,15,512]{2,1,0:T(8,128)} %collective-permute-done.26, f32[2,15,512]{2,1,0:T(8,128)S(1)} %collective-permute-done.27, ...), kind=kLoop, calls=%fused_computation.1741 | loop fusion | flops 28835840 | bytes 9597064 | tf_op jit(solution)/shard_map/add | solution.py:43
  436.8 6.4 collective-permute-start.31
  446.9 5.6 collective-permute-start.33
  454.7 44.7 %divide_add_fusion.4 = f32[2,256,512]{2,1,0:T(8,128)} fusion(f32[2,256,512]{2,1,0:T(8,128)} %get-tuple-element.14, f32[2,256,512]{2,1,0:T(8,128)S(1)} %copy-done, f32[2,15,512]{2,1,0:T(8,128)S(1)} %collective-permute-done.30, f32[2,15,512]{2,1,0:T(8,128)S(1)} %collective-permute-done.31, f32[2,256,512]{2,1,0:T(8,128)S(1)} %copy-done.1, ...), kind=kLoop, calls=%fused_computation.1740 | loop fusion | flops 27525120 | bytes 6418556 | tf_op jit(solution)/shard_map/add | solution.py:43
  500.3 6.5 collective-permute-start.35
  518.5 46.9 %multiply_reduce_fusion.1 = (f32[256,512]{1,0:T(8,128)}, f32[2,256,512]{2,1,0:T(8,128)}) fusion(f32[2,256,512]{2,1,0:T(8,128)} %get-tuple-element.16, f32[2,256,512]{2,1,0:T(8,128)} %divide_add_fusion.4, f32[2,256,512]{2,1,0:T(8,128)S(1)} %copy-done, f32[2,15,512]{2,1,0:T(8,128)S(1)} %collective-permute-done.34, f32[]{:T(128)} %bitcast.31, f32[]{:T(128)} %bitcast.30, ...), kind=kLoop, calls=%fused_computation.1733 | loop fusion | flops 27918336 | bytes 7991420 | tf_op jit(solution)/shard_map/reduce_sum | solution.py:56
  566.8 6.4 collective-permute-start.40
  585.9 46.4 %divide_add_fusion.2 = (f32[2,256,512]{2,1,0:T(8,128)}, f32[2,256,512]{2,1,0:T(8,128)}, f32[2,256,512]{2,1,0:T(8,128)}) fusion(f32[2,256,512]{2,1,0:T(8,128)} %get-tuple-element.8, f32[2,256,512]{2,1,0:T(8,128)S(1)} %copy-done, f32[2,15,512]{2,1,0:T(8,128)} %collective-permute-done.39, f32[2,15,512]{2,1,0:T(8,128)S(1)} %collective-permute-done.40, ...), kind=kLoop, calls=%fused_computation.1738 | loop fusion | flops 28835840 | bytes 9597064 | tf_op jit(solution)/shard_map/add | solution.py:43
  633.1 6.4 collective-permute-start.44
  651.0 45.6 %divide_add_fusion.1 = f32[2,256,512]{2,1,0:T(8,128)} fusion(f32[2,256,512]{2,1,0:T(8,128)} %get-tuple-element.11, f32[2,256,512]{2,1,0:T(8,128)S(1)} %copy-done, f32[2,15,512]{2,1,0:T(8,128)S(1)} %collective-permute-done.43, f32[2,15,512]{2,1,0:T(8,128)S(1)} %collective-permute-done.44, f32[2,256,512]{2,1,0:T(8,128)S(1)} %copy-done.1, ...), kind=kLoop, calls=%fused_computation.1737 | loop fusion | flops 27525120 | bytes 6418556 | tf_op jit(solution)/shard_map/add | solution.py:43
  697.6 6.4 collective-permute-start.48
  715.6 46.0 %multiply_reduce_fusion = (f32[256,512]{1,0:T(8,128)}, f32[2,256,512]{2,1,0:T(8,128)}) fusion(f32[2,256,512]{2,1,0:T(8,128)} %get-tuple-element.13, f32[2,256,512]{2,1,0:T(8,128)} %divide_add_fusion.1, f32[2,256,512]{2,1,0:T(8,128)S(1)} %copy-done, f32[2,15,512]{2,1,0:T(8,128)S(1)} %collective-permute-done.47, f32[]{:T(128)} %bitcast.31, f32[]{:T(128)} %bitcast.30, ...), kind=kLoop, calls=%fused_computation.1732 | loop fusion | flops 27918336 | bytes 7991420 | tf_op jit(solution)/shard_map/reduce_sum | solution.py:56
  769.4 79.9 %all-reduce.6.cloned.1.call-done = f32[256,512]{1,0:T(8,128)} async-done(((f32[256,512]{1,0:T(8,128)}), f32[256,512]{1,0:T(8,128)}) %all-reduce.6.cloned.1.call-update) | async-done | bytes 524304 | tf_op jit(solution)/shard_map/psum | solution.py:57
  (142 shorter events, 159.7 us)
Async XLA Ops:
  7.2 842.2 %all-reduce.6.cloned.1.call-start = ((), (), s32[]{:S(2)}) async-start(), calls=%async_computation | async-start | bytes 1048576 | tf_op jit(solution)/shard_map/psum | solution.py:57
  7.2 18.5 %collective-permute-start.1 = (f32[2,15,512]{2,1,0:T(8,128)S(1)}, f32[2,15,512]{2,1,0:T(8,128)S(1)}, u32[]{:S(2)}, u32[]{:S(2)}) collective-permute-start(f32[2,15,512]{2,1,0:T(8,128)S(1)} %broadcast.29), channel_id=1, source_target_pairs={{0,16},{16,32},{32,48},{48,64},{64,80},{80,96},{96,112},{112,128},... | collective-permute-start | bytes 184328 | tf_op jit(solution)/shard_map/ppermute | solution.py:17
  12.7 13.0 %collective-permute-start = (f32[2,15,512]{2,1,0:T(8,128)S(1)}, f32[2,15,512]{2,1,0:T(8,128)S(1)}, u32[]{:S(2)}, u32[]{:S(2)}) collective-permute-start(f32[2,15,512]{2,1,0:T(8,128)S(1)} %broadcast.29), channel_id=1, source_target_pairs={{16,0},{32,16},{48,32},{64,48},{80,64},{96,80},{112,96},{128,112},... | collective-permute-start | bytes 184328 | tf_op jit(solution)/shard_map/ppermute | solution.py:20
  48.4 15.4 %collective-permute-start.5 = (f32[2,15,512]{2,1,0:T(8,128)S(1)}, f32[2,15,512]{2,1,0:T(8,128)S(1)}, u32[]{:S(2)}, u32[]{:S(2)}) collective-permute-start(f32[2,15,512]{2,1,0:T(8,128)S(1)} %get-tuple-element.64), channel_id=1, source_target_pairs={{0,16},{16,32},{32,48},{48,64},{64,80},{80,96},{96,112},{112,128},... | collective-permute-start | bytes 184328 | tf_op jit(solution)/shard_map/ppermute | solution.py:17
  110.3 17.3 %collective-permute-start.9 = (f32[2,15,512]{2,1,0:T(8,128)S(1)}, f32[2,15,512]{2,1,0:T(8,128)S(1)}, u32[]{:S(2)}, u32[]{:S(2)}) collective-permute-start(f32[2,15,512]{2,1,0:T(8,128)S(1)} %get-tuple-element.60), channel_id=1, source_target_pairs={{0,16},{16,32},{32,48},{48,64},{64,80},{80,96},{96,112},{112,128},... | collective-permute-start | bytes 184328 | tf_op jit(solution)/shard_map/ppermute | solution.py:17
  115.8 11.8 %collective-permute-start.8 = (f32[2,15,512]{2,1,0:T(8,128)S(1)}, f32[2,15,512]{2,1,0:T(8,128)S(1)}, u32[]{:S(2)}, u32[]{:S(2)}) collective-permute-start(f32[2,15,512]{2,1,0:T(8,128)S(1)} %get-tuple-element.61), channel_id=1, source_target_pairs={{16,0},{32,16},{48,32},{64,48},{80,64},{96,80},{112,96},{128,112},... | collective-permute-start | bytes 184328 | tf_op jit(solution)/shard_map/ppermute | solution.py:20
  125.1 67.1 %collective-permute-start.12 = (f32[2,256,512]{2,1,0:T(8,128)}, f32[2,256,512]{2,1,0:T(8,128)}, u32[]{:S(2)}, u32[]{:S(2)}) collective-permute-start(f32[2,256,512]{2,1,0:T(8,128)} %param.15), channel_id=1, source_target_pairs={{16,0},{32,16},{48,32},{64,48},{80,64},{96,80},{112,96},{128,112},... | collective-permute-start | bytes 3145736 | tf_op jit(solution)/shard_map/ppermute | solution.py:28
  173.4 19.6 %collective-permute-start.14 = (f32[2,15,512]{2,1,0:T(8,128)}, f32[2,15,512]{2,1,0:T(8,128)S(1)}, u32[]{:S(2)}, u32[]{:S(2)}) collective-permute-start(f32[2,15,512]{2,1,0:T(8,128)} %get-tuple-element.56), channel_id=1, source_target_pairs={{0,16},{16,32},{32,48},{48,64},{64,80},{80,96},{96,112},{112,128},... | collective-permute-start | bytes 184328 | tf_op jit(solution)/shard_map/ppermute | solution.py:17
  179.3 13.7 %collective-permute-start.13 = (f32[2,15,512]{2,1,0:T(8,128)}, f32[2,15,512]{2,1,0:T(8,128)}, u32[]{:S(2)}, u32[]{:S(2)}) collective-permute-start(f32[2,15,512]{2,1,0:T(8,128)} %get-tuple-element.57), channel_id=1, source_target_pairs={{16,0},{32,16},{48,32},{64,48},{80,64},{96,80},{112,96},{128,112},... | collective-permute-start | bytes 184328 | tf_op jit(solution)/shard_map/ppermute | solution.py:20
  240.2 17.3 %collective-permute-start.18 = (f32[2,15,512]{2,1,0:T(8,128)S(1)}, f32[2,15,512]{2,1,0:T(8,128)S(1)}, u32[]{:S(2)}, u32[]{:S(2)}) collective-permute-start(f32[2,15,512]{2,1,0:T(8,128)S(1)} %get-tuple-element.52), channel_id=1, source_target_pairs={{0,16},{16,32},{32,48},{48,64},{64,80},{80,96},{96,112},{112,128},... | collective-permute-start | bytes 184328 | tf_op jit(solution)/shard_map/ppermute | solution.py:17
  304.1 18.0 %collective-permute-start.22 = (f32[2,15,512]{2,1,0:T(8,128)S(1)}, f32[2,15,512]{2,1,0:T(8,128)S(1)}, u32[]{:S(2)}, u32[]{:S(2)}) collective-permute-start(f32[2,15,512]{2,1,0:T(8,128)S(1)} %get-tuple-element.48), channel_id=1, source_target_pairs={{0,16},{16,32},{32,48},{48,64},{64,80},{80,96},{96,112},{112,128},... | collective-permute-start | bytes 184328 | tf_op jit(solution)/shard_map/ppermute | solution.py:17
  310.5 11.6 %collective-permute-start.21 = (f32[2,15,512]{2,1,0:T(8,128)S(1)}, f32[2,15,512]{2,1,0:T(8,128)S(1)}, u32[]{:S(2)}, u32[]{:S(2)}) collective-permute-start(f32[2,15,512]{2,1,0:T(8,128)S(1)} %get-tuple-element.49), channel_id=1, source_target_pairs={{16,0},{32,16},{48,32},{64,48},{80,64},{96,80},{112,96},{128,112},... | collective-permute-start | bytes 184328 | tf_op jit(solution)/shard_map/ppermute | solution.py:20
  319.5 68.1 %collective-permute-start.25 = (f32[2,256,512]{2,1,0:T(8,128)}, f32[2,256,512]{2,1,0:T(8,128)}, u32[]{:S(2)}, u32[]{:S(2)}) collective-permute-start(f32[2,256,512]{2,1,0:T(8,128)} %get-tuple-element.19), channel_id=1, source_target_pairs={{16,0},{32,16},{48,32},{64,48},{80,64},{96,80},{112,96},{128,112},... | collective-permute-start | bytes 3145736 | tf_op jit(solution)/shard_map/ppermute | solution.py:28
  369.6 19.0 %collective-permute-start.27 = (f32[2,15,512]{2,1,0:T(8,128)}, f32[2,15,512]{2,1,0:T(8,128)S(1)}, u32[]{:S(2)}, u32[]{:S(2)}) collective-permute-start(f32[2,15,512]{2,1,0:T(8,128)} %get-tuple-element.44), channel_id=1, source_target_pairs={{0,16},{16,32},{32,48},{48,64},{64,80},{80,96},{96,112},{112,128},... | collective-permute-start | bytes 184328 | tf_op jit(solution)/shard_map/ppermute | solution.py:17
  375.9 12.7 %collective-permute-start.26 = (f32[2,15,512]{2,1,0:T(8,128)}, f32[2,15,512]{2,1,0:T(8,128)}, u32[]{:S(2)}, u32[]{:S(2)}) collective-permute-start(f32[2,15,512]{2,1,0:T(8,128)} %get-tuple-element.45), channel_id=1, source_target_pairs={{16,0},{32,16},{48,32},{64,48},{80,64},{96,80},{112,96},{128,112},... | collective-permute-start | bytes 184328 | tf_op jit(solution)/shard_map/ppermute | solution.py:20
  436.8 17.9 %collective-permute-start.31 = (f32[2,15,512]{2,1,0:T(8,128)S(1)}, f32[2,15,512]{2,1,0:T(8,128)S(1)}, u32[]{:S(2)}, u32[]{:S(2)}) collective-permute-start(f32[2,15,512]{2,1,0:T(8,128)S(1)} %get-tuple-element.40), channel_id=1, source_target_pairs={{0,16},{16,32},{32,48},{48,64},{64,80},{80,96},{96,112},{112,128},... | collective-permute-start | bytes 184328 | tf_op jit(solution)/shard_map/ppermute | solution.py:17
  500.3 18.2 %collective-permute-start.35 = (f32[2,15,512]{2,1,0:T(8,128)S(1)}, f32[2,15,512]{2,1,0:T(8,128)S(1)}, u32[]{:S(2)}, u32[]{:S(2)}) collective-permute-start(f32[2,15,512]{2,1,0:T(8,128)S(1)} %get-tuple-element.36), channel_id=1, source_target_pairs={{0,16},{16,32},{32,48},{48,64},{64,80},{80,96},{96,112},{112,128},... | collective-permute-start | bytes 184328 | tf_op jit(solution)/shard_map/ppermute | solution.py:17
  506.8 11.6 %collective-permute-start.34 = (f32[2,15,512]{2,1,0:T(8,128)S(1)}, f32[2,15,512]{2,1,0:T(8,128)S(1)}, u32[]{:S(2)}, u32[]{:S(2)}) collective-permute-start(f32[2,15,512]{2,1,0:T(8,128)S(1)} %get-tuple-element.37), channel_id=1, source_target_pairs={{16,0},{32,16},{48,32},{64,48},{80,64},{96,80},{112,96},{128,112},... | collective-permute-start | bytes 184328 | tf_op jit(solution)/shard_map/ppermute | solution.py:20
  515.9 69.2 %collective-permute-start.38 = (f32[2,256,512]{2,1,0:T(8,128)}, f32[2,256,512]{2,1,0:T(8,128)}, u32[]{:S(2)}, u32[]{:S(2)}) collective-permute-start(f32[2,256,512]{2,1,0:T(8,128)} %get-tuple-element.16), channel_id=1, source_target_pairs={{16,0},{32,16},{48,32},{64,48},{80,64},{96,80},{112,96},{128,112},... | collective-permute-start | bytes 3145736 | tf_op jit(solution)/shard_map/ppermute | solution.py:28
  566.8 19.0 %collective-permute-start.40 = (f32[2,15,512]{2,1,0:T(8,128)}, f32[2,15,512]{2,1,0:T(8,128)S(1)}, u32[]{:S(2)}, u32[]{:S(2)}) collective-permute-start(f32[2,15,512]{2,1,0:T(8,128)} %get-tuple-element.32), channel_id=1, source_target_pairs={{0,16},{16,32},{32,48},{48,64},{64,80},{80,96},{96,112},{112,128},... | collective-permute-start | bytes 184328 | tf_op jit(solution)/shard_map/ppermute | solution.py:17
  573.2 12.7 %collective-permute-start.39 = (f32[2,15,512]{2,1,0:T(8,128)}, f32[2,15,512]{2,1,0:T(8,128)}, u32[]{:S(2)}, u32[]{:S(2)}) collective-permute-start(f32[2,15,512]{2,1,0:T(8,128)} %get-tuple-element.33), channel_id=1, source_target_pairs={{16,0},{32,16},{48,32},{64,48},{80,64},{96,80},{112,96},{128,112},... | collective-permute-start | bytes 184328 | tf_op jit(solution)/shard_map/ppermute | solution.py:20
  633.1 17.9 %collective-permute-start.44 = (f32[2,15,512]{2,1,0:T(8,128)S(1)}, f32[2,15,512]{2,1,0:T(8,128)S(1)}, u32[]{:S(2)}, u32[]{:S(2)}) collective-permute-start(f32[2,15,512]{2,1,0:T(8,128)S(1)} %get-tuple-element.28), channel_id=1, source_target_pairs={{0,16},{16,32},{32,48},{48,64},{64,80},{80,96},{96,112},{112,128},... | collective-permute-start | bytes 184328 | tf_op jit(solution)/shard_map/ppermute | solution.py:17
  697.6 18.0 %collective-permute-start.48 = (f32[2,15,512]{2,1,0:T(8,128)S(1)}, f32[2,15,512]{2,1,0:T(8,128)S(1)}, u32[]{:S(2)}, u32[]{:S(2)}) collective-permute-start(f32[2,15,512]{2,1,0:T(8,128)S(1)} %get-tuple-element.24), channel_id=1, source_target_pairs={{0,16},{16,32},{32,48},{48,64},{64,80},{80,96},{96,112},{112,128},... | collective-permute-start | bytes 184328 | tf_op jit(solution)/shard_map/ppermute | solution.py:17
  713.0 53.1 %collective-permute-start.51 = (f32[2,256,512]{2,1,0:T(8,128)}, f32[2,256,512]{2,1,0:T(8,128)}, u32[]{:S(2)}, u32[]{:S(2)}) collective-permute-start(f32[2,256,512]{2,1,0:T(8,128)} %get-tuple-element.13), channel_id=1, source_target_pairs={{16,0},{32,16},{48,32},{64,48},{80,64},{96,80},{112,96},{128,112},... | collective-permute-start | bytes 3145736 | tf_op jit(solution)/shard_map/ppermute | solution.py:28
  (35 other events, 372.8 us)
Sparse Core Ops, SparseCore 0:
  764.3 84.9 all-reduce.5
where the time goes:
time: 872 us; the launch traced here: 858 us
  other arithmetic  533 us (61%)
  starting transfers between devices  171 us (20%)
  waiting for transfers between devices  96.9 us (11%)
  local copies, waits for them, and re-layouts  34.3 us (4%)
  between operations  23.3 us (3%)
    add x7, other arithmetic, relax(): return lam + 0.8 * (rhs - diag * lam + beside - conv) / diag  322 us
    reduce_sum x4, other arithmetic, on_device(): term = jnp.sum(lam * film, axis=0)  183 us
    ppermute x24, starting transfers between devices, with_halo(): lax.ppermute(lax.slice_in_dim(block, block.shape[dim] - width, None, axis...  134 us
    psum x1, waiting for transfers between devices, on_device(): gradient = gradient + lax.psum(term, 'case')  79.9 us
    ppermute x24, starting transfers between devices, with_halo(): lax.ppermute(lax.slice_in_dim(block, 0, width, axis=dim), axis, backward)  31 us
    div x1, other arithmetic, relax(): return lam + 0.8 * (rhs - diag * lam + beside - conv) / diag  22.6 us
  transfers between devices with their start and end apart: 53, of which 16 were waited for; matrix products, arithmetic and copies ran while one was open for 25% of the time, Pallas kernels for 0%

commit v1 on v0

v1 whole, which is shorter than its diff:
```python
import functools

import jax
import jax.numpy as jnp
from jax import lax
from jax.experimental import pallas as pl
from jax.experimental.pallas import tpu as pltpu
from jax.sharding import PartitionSpec as P

STEPS = 4
SWEEPS = 3
KERN = 31
NSRR = 16
HALO = 48
COEF = 32
COLS = STEPS * SWEEPS - 1
BAND = 16
BLOCK = 128
SLOTS = 8

f32 = jnp.float32
bf16 = jnp.bfloat16


def banded(kern_ref, rows):
    width = rows + 2 * BAND
    shape = (rows, 3 * width)
    lane = lax.broadcasted_iota(jnp.int32, shape, 1)
    part = (lane >= width).astype(jnp.int32) + (lane >= 2 * width).astype(jnp.int32)
    tap = lane - part * width - lax.broadcasted_iota(jnp.int32, shape, 0) - 1
    value = jnp.zeros(shape, f32)
    for k in range(KERN):
        value = jnp.where(tap == k, kern_ref[k], value)
    high = value.astype(bf16).astype(f32)
    return jnp.where(part == 1, value - high, high).astype(bf16)


def pack_kernel(kern_ref, diag, fx, fy, film, src, t_big, t_mid, t_low, left, right):
    t_big[...] = banded(kern_ref, BLOCK)
    t_mid[...] = banded(kern_ref, 64)
    t_low[...] = banded(kern_ref, 32)
    cols = diag.shape[2]
    rows = 32
    lane = lax.broadcasted_iota(jnp.int32, (rows, 128), 1)

    def chunk(i, carry):
        at = pl.ds(pl.multiple_of(i * rows, rows), rows)
        for c in range(2):
            first = jnp.zeros((rows, 128), f32)
            last = jnp.zeros((rows, 128), f32)
            for slot in range(SLOTS):
                if slot < 4:
                    ref = (diag, fx, fy, film)[slot].at[c]
                else:
                    ref = src.at[c, STEPS - 1 - (slot - 4)]
                place = COLS * slot
                here = (lane >= place) & (lane < place + COLS)
                low = ref[at, 0:128]
                high = ref[at, cols - 128 : cols]
                first = jnp.where(here, pltpu.roll(low, place, 1) if place else low, first)
                last = jnp.where(here, pltpu.roll(high, (place + COLS) % 128, 1), last)
            left[c, at, :] = first
            right[c, at, :] = last
        return carry

    lax.fori_loop(0, diag.shape[1] // rows, chunk, 0)


def setup_kernel(
    ratio, flags, diag, fx, fy, film, src, from_left, from_right,
    coef, lam, film_out, extra, up1, down1, up2, down2, up3, down3,
):
    total, cols = diag.shape[1], diag.shape[2]
    rows = 16
    lane = lax.broadcasted_iota(jnp.int32, (rows, 128), 1)
    is_right = lane < COLS
    is_left = lane >= 128 - COLS
    right_ok, left_ok = flags[3], flags[2]
    inside = (is_right & (right_ok > 0)) | (is_left & (left_ok > 0))

    def chunk(i, carry):
        at = pl.ds(pl.multiple_of(i * rows, rows), rows)
        for c in range(2):
            lo = from_left[c, at, :]
            hi = from_right[c, at, :]

            def halo(slot):
                place = COLS * slot
                right = pltpu.roll(hi, (128 - place) % 128, 1) if place else hi
                left = pltpu.roll(lo, (128 - COLS - place) % 128, 1)
                return jnp.where(inside, jnp.where(is_right, right, left), 0.0)

            r = ratio[c]
            for main in (True, False):
                span = slice(0, cols) if main else slice(cols, cols + 128)
                if main:
                    w = 0.8 / diag[c, at, :]
                    x, y, h = fx[c, at, :], fy[c, at, :], film[c, at, :]
                    s = src[c, STEPS - 1, at, :]
                else:
                    d = jnp.where(inside, halo(0), 1.0)
                    w = jnp.where(inside, 0.8 / d, 0.0)
                    x, y, h, s = halo(1), halo(2), halo(3), halo(4)
                    for k in range(STEPS - 1):
                        extra[c, k, at, :] = halo(7 - k)
                coef[c, 0, at, span] = w
                coef[c, 1, at, span] = w * x
                coef[c, 2, at, span] = w * y
                film_out[c, at, span] = h
                lam[c, at, span] = w * (s + r * h)
        return carry

    lax.fori_loop(0, total // rows, chunk, 0)
    for c in range(2):
        end = total
        up1[c, 0:32, :] = lam[c, 0:32, :]
        down1[c, 0:32, :] = lam[c, end - 32 : end, :]
        for k in range(3):
            up1[c, 32 + 16 * k : 48 + 16 * k, :] = coef[c, k, 0:16, :]
            down1[c, 32 + 16 * k : 48 + 16 * k, :] = coef[c, k, end - 16 : end, :]
            up2[c, 16 * k : 16 * k + 16, :] = coef[c, k, 16:32, :]
            down2[c, 16 * k : 16 * k + 16, :] = coef[c, k, end - 32 : end - 16, :]
        up2[c, 80:136, :] = film_out[c, 0:56, :]
        down2[c, 80:112, :] = film_out[c, end - 32 : end, :]
        for ref, other, start, k in ((up2, down2, 48, 2), (up3, down3, 0, 1), (up3, down3, 32, 0)):
            to = slice(start, start + 32)
            ref[c, to, 0:cols] = src[c, k, 0:32, :]
            ref[c, to, cols : cols + 128] = extra[c, k, 0:32, :]
            other[c, to, 0:cols] = src[c, k, end - 32 : end, :]
            other[c, to, cols : cols + 128] = extra[c, k, end - 32 : end, :]


def moved(near, shift):
    stack = jnp.concatenate(near, axis=0)
    size = stack.shape[0]
    return pltpu.roll(stack, size - shift, 0)[0 : size - 8]


def split(value):
    high = value.astype(bf16)
    return high, (value - high.astype(f32)).astype(bf16)


def sweep(old, new, conv, mats, first, last, coefs, emit):
    lam, high, low = old
    start = first
    while start < last:
        size = BLOCK if last - start >= BLOCK else last - start
        near = slice(start - BAND, start + size + BAND)
        top = high[near, :]
        stack = jnp.concatenate([top, top, low[near, :]], axis=0)
        conv[0:size, :] = jnp.dot(mats[size][...], stack, preferred_element_type=f32)
        for row in range(start, start + size, 16):
            w, wx, wy, wr = coefs(row)
            area = lam[row - 8 : row + 24, :]
            mid = area[8:24]
            width = mid.shape[1]
            value = 0.2 * mid + wr
            value = value + wx * (area[7:23] + area[9:25])
            value = value + wy * (pltpu.roll(mid, 1, 1) + pltpu.roll(mid, width - 1, 1))
            value = value - w * conv[row - start : row - start + 16, :]
            emit(row, value, new)
        start += size


def keep(row, value, new):
    lam, high, low = new
    at = slice(row, row + 16)
    lam[at, :] = value
    high[at, :], low[at, :] = split(value)


def first_kernel(
    flags, t_big, t_mid, t_low, coef, lam_in, film, top, bottom,
    lam_out, up, down, grad, la, ha, oa, lb, hb, ob, conv,
):
    mats = {BLOCK: t_big, 64: t_mid, 32: t_low}
    total = lam_in.shape[1]
    cols = grad.shape[1]
    end = HALO + total
    top_ok = flags[0].astype(f32)
    low_ok = flags[1].astype(f32)

    def case(c, carry):
        for row in range(HALO - 32, end + 32, 16):
            if row < HALO:
                value = top[c, row - HALO + 32 : row - HALO + 48, :] * top_ok
            elif row >= end:
                value = bottom[c, row - end : row - end + 16, :] * low_ok
            else:
                value = lam_in[c, row - HALO : row - HALO + 16, :]
            keep(row, value, (la, ha, oa))

        def coefs(row):
            if row < HALO:
                rows = [top[c, 32 + 16 * k : 48 + 16 * k, :] * top_ok for k in range(3)]
                return (*rows, top[c, 16:32, :] * top_ok)
            if row >= end:
                rows = [bottom[c, 32 + 16 * k : 48 + 16 * k, :] * low_ok for k in range(3)]
                return (*rows, bottom[c, 0:16, :] * low_ok)
            at = slice(row - HALO, row - HALO + 16)
            return coef[c, 0, at, :], coef[c, 1, at, :], coef[c, 2, at, :], lam_in[c, at, :]

        sweep((la, ha, oa), (lb, hb, ob), conv, mats, HALO - 16, end + 16, coefs, keep)

        def emit(row, value, new):
            at = slice(row - HALO, row - HALO + 16)
            lam_out[c, at, :] = value
            if row < HALO + HALO:
                up[c, at, :] = value
            if row >= end - HALO:
                down[c, row - end + HALO : row - end + HALO + 16, :] = value
            term = value[:, 0:cols] * film[c, at, 0:cols]
            grad[at, :] = jnp.where(c == 0, term, grad[at, :] + term)

        sweep((lb, hb, ob), None, conv, mats, HALO, end, coefs, emit)
        return carry

    lax.fori_loop(0, 2, case, 0)


def step_kernel(
    step, ratio, shifts, flags, t_big, t_mid, t_low, coef, inner_top, inner_bot, outer_top, outer_bot,
    src, extra, src_top, src_bot, lam_in, lam_top, lam_bot, film, grad_in, *rest,
):
    final = step == 0
    if final:
        lam_out, film_out, grad, film_now, la, ha, oa, lb, hb, ob, wr_ref, conv = rest
    else:
        lam_out, up, down, film_now, grad, la, ha, oa, lb, hb, ob, wr_ref, conv = rest
    mats = {BLOCK: t_big, 64: t_mid, 32: t_low}
    total = lam_in.shape[1]
    cols = grad.shape[1]
    end = HALO + total
    top_ok = flags[0].astype(f32)
    low_ok = flags[1].astype(f32)
    reach = 8 * step
    place = {2: 48, 1: 0, 0: 32}[step]

    def case(c, carry):
        r = ratio[c]

        def old_film(row):
            if step == 2:
                if row < HALO:
                    return outer_top[c, 80 + row - HALO + 32 : 88 + row - HALO + 32, :] * top_ok
                if row >= end:
                    return outer_bot[c, 80 + row - end : 88 + row - end, :] * low_ok
                return film[c, row - HALO : row - HALO + 8, :]
            at = row - (HALO - COEF)
            return film[c, at : at + 8, :]

        def halo_coef(row, k):
            if row < HALO:
                ref, at = (inner_top, 32) if row >= HALO - 16 else (outer_top, 0)
                return ref[c, at + 16 * k : at + 16 * k + 16, :] * top_ok
            ref, at = (inner_bot, 32) if row < end + 16 else (outer_bot, 0)
            return ref[c, at + 16 * k : at + 16 * k + 16, :] * low_ok

        def coef_at(row, k):
            if HALO <= row < end:
                return coef[c, k, row - HALO : row - HALO + 16, :]
            return halo_coef(row, k)

        shift = shifts[step + 1]
        for row in range(0, end + HALO, 16):
            if row < HALO:
                lam = lam_top[c, row : row + 16, :] * top_ok
            elif row >= end:
                lam = lam_bot[c, row - end : row - end + 16, :] * low_ok
            else:
                lam = lam_in[c, row - HALO : row - HALO + 16, :]
            keep(row, lam, (la, ha, oa))
            if row < HALO - COEF or row >= end + COEF + reach:
                continue
            height = 16 if row + 16 <= end + COEF + reach else 8
            near = [old_film(row + k) for k in range(0, height + 8, 8)]
            now = moved(near, shift) + r * lam[0:height]
            film_now[c, row - HALO + COEF : row - HALO + COEF + height, :] = now
            if row >= end + COEF:
                continue
            w = coef_at(row, 0)
            at = row - HALO + COEF
            if row < HALO:
                wr_ref[at : at + 16, :] = w * (src_top[c, place + at : place + at + 16, :] + r * now)
            elif row >= end:
                k = place + row - end
                wr_ref[at : at + 16, :] = w * (src_bot[c, k : k + 16, :] + r * now)
            else:
                k = slice(row - HALO, row - HALO + 16)
                wr_ref[at : at + 16, 0:cols] = w[:, 0:cols] * (src[c, step, k, :] + r * now[:, 0:cols])
                wr_ref[at : at + 16, cols : cols + 128] = w[:, cols : cols + 128] * (
                    extra[c, step, k, :] + r * now[:, cols : cols + 128]
                )

        def coefs(row):
            at = row - HALO + COEF
            return coef_at(row, 0), coef_at(row, 1), coef_at(row, 2), wr_ref[at : at + 16, :]

        a, b = (la, ha, oa), (lb, hb, ob)
        sweep(a, b, conv, mats, HALO - 32, end + 32, coefs, keep)
        sweep(b, a, conv, mats, HALO - 16, end + 16, coefs, keep)

        def emit(row, value, new):
            at = slice(row - HALO, row - HALO + 16)
            here = slice(row - HALO + COEF, row - HALO + COEF + 16)
            term = value[:, 0:cols] * film_now[c, here, 0:cols]
            grad[at, :] = jnp.where(c == 0, grad_in[at, :], grad[at, :]) + term
            if final:
                lam_out[c, at, :] = value[:, 0:cols]
                near = [film_now[c, here.start + k : here.start + k + 8, 0:cols] for k in range(0, 24, 8)]
                film_out[c, at, :] = moved(near, shifts[0]) + r * value[:, 0:cols]
                return
            lam_out[c, at, :] = value
            if row < HALO + HALO:
                up[c, at, :] = value
            if row >= end - HALO:
                down[c, row - end + HALO : row - end + HALO + 16, :] = value

        sweep(a, None, conv, mats, HALO, end, coefs, emit)
        return carry

    lax.fori_loop(0, 2, case, 0)


VM = pl.BlockSpec(memory_space=pltpu.VMEM)
SM = pl.BlockSpec(memory_space=pltpu.SMEM)


def call(body, smem, vmem, outs, scratch=(), flops=0, name=None):
    moved = sum(v.size * 4 for v in vmem) + sum(4 * functools.reduce(lambda a, b: a * b, o.shape) for o in outs)
    return pl.pallas_call(
        body,
        out_shape=tuple(outs),
        in_specs=[SM] * len(smem) + [VM] * len(vmem),
        out_specs=tuple([VM] * len(outs)),
        scratch_shapes=list(scratch),
        cost_estimate=pl.CostEstimate(flops=flops, bytes_accessed=moved, transcendentals=0),
        compiler_params=pltpu.CompilerParams(vmem_limit_bytes=40 << 20),
        name=name,
    )(*smem, *vmem)


def ring(axis, step):
    count = lax.axis_size(axis)
    return [(i, (i + step) % count) for i in range(count)]


def both_ways(up, down, axis):
    from_high = lax.ppermute(up, axis, ring(axis, -1))
    from_low = lax.ppermute(down, axis, ring(axis, 1))
    return from_low, from_high


def after(values, gate):
    return lax.optimization_barrier((tuple(values), tuple(gate)))[0]


def case_sum(part):
    half = part.shape[0] // 2
    core = lax.axis_index("case") % 2
    swap_core = [(i, i ^ 1) for i in range(4)]
    swap_chip = [(i, i ^ 2) for i in range(4)]
    mine = jnp.where(core == 0, part[:half], part[half:])
    other = jnp.where(core == 0, part[half:], part[:half])
    mine = mine + lax.ppermute(other, "case", swap_core)
    mine = mine + lax.ppermute(mine, "case", swap_chip)
    other = lax.ppermute(mine, "case", swap_core)
    return jnp.where(
        core == 0, jnp.concatenate([mine, other], axis=0), jnp.concatenate([other, mine], axis=0)
    )


def on_device(ratio_index, shifts, kernel, diagonal, flow_x, flow_y, pres_source, rough_adjoint):
    ratio = 0.2 + 1.6 * ratio_index.astype(f32) / (NSRR - 1)
    cases, total, cols = diagonal.shape
    wide = cols + 128
    roll, trans = lax.axis_index("roll"), lax.axis_index("trans")
    index = jnp.arange(4)
    flags = jnp.where(
        index == 0,
        roll > 0,
        jnp.where(
            index == 1,
            roll < lax.axis_size("roll") - 1,
            jnp.where(index == 2, trans > 0, trans < lax.axis_size("trans") - 1),
        ),
    ).astype(jnp.int32)

    def shape(*dims, dtype=f32):
        return jax.ShapeDtypeStruct(dims, dtype)

    raw = (diagonal, flow_x, flow_y, rough_adjoint, pres_source)
    t_big, t_mid, t_low, left, right = call(
        pack_kernel,
        (kernel,),
        raw,
        [
            shape(BLOCK, 3 * (BLOCK + 32), dtype=bf16),
            shape(64, 3 * 96, dtype=bf16),
            shape(32, 3 * 64, dtype=bf16),
            shape(cases, total, 128),
            shape(cases, total, 128),
        ],
        name="pack",
    )
    from_left, from_right = both_ways(left, right, "trans")
    coef, lam, film, extra, up1, down1, up2, down2, up3, down3 = call(
        setup_kernel,
        (ratio, flags),
        (*raw, from_left, from_right),
        [
            shape(cases, 3, total, wide),
            shape(cases, total, wide),
            shape(cases, total, wide),
            shape(cases, STEPS - 1, total, 128),
            shape(cases, 80, wide),
            shape(cases, 80, wide),
            shape(cases, 136, wide),
            shape(cases, 112, wide),
            shape(cases, 64, wide),
            shape(cases, 64, wide),
        ],
        name="setup",
    )
    top1, bot1 = both_ways(up1, down1, "roll")
    up2, down2 = after((up2, down2), (top1, bot1))
    top2, bot2 = both_ways(up2, down2, "roll")

    rows = total + 2 * HALO
    fields = [pltpu.VMEM((rows, wide), f32), pltpu.VMEM((rows, wide), bf16), pltpu.VMEM((rows, wide), bf16)]
    conv = pltpu.VMEM((BLOCK, wide), f32)
    work = [*fields, *fields, pltpu.VMEM((total + 2 * COEF, wide), f32), conv]
    mats = (t_big, t_mid, t_low)
    state = [shape(cases, total, wide), shape(cases, HALO, wide), shape(cases, HALO, wide)]
    lam, up, down, grad = call(
        first_kernel,
        (flags,),
        (*mats, coef, lam, film, top1, bot1),
        [*state, shape(total, cols)],
        [*fields, *fields, conv],
        flops=2 << 30,
        name="first",
    )
    for step in range(STEPS - 2, -1, -1):
        lam_top, lam_bot = both_ways(up, down, "roll")
        if step == STEPS - 2:
            up3, down3 = after((up3, down3), (lam_top, lam_bot))
            top3, bot3 = both_ways(up3, down3, "roll")
        src_top, src_bot = (top2, bot2) if step == 2 else (top3, bot3)
        films = shape(cases, total + 2 * COEF + 8 * step, wide)
        if step:
            outs = [*state, films, shape(total, cols)]
            scratch = work
        else:
            outs = [shape(cases, total, cols), shape(cases, total, cols), shape(total, cols)]
            scratch = [pltpu.VMEM(films.shape, f32), *work]
        result = call(
            functools.partial(step_kernel, step),
            (ratio, shifts, flags),
            (*mats, coef, top1, bot1, top2, bot2, pres_source, extra, src_top, src_bot, lam, lam_top, lam_bot, film, grad),
            outs,
            scratch,
            flops=3 << 30,
            name="step" + str(step),
        )
        if step:
            lam, up, down, film, grad = result
        else:
            lam, film, grad = result
    return lam, film, case_sum(grad)


def solution(mesh):
    block = P("case", "roll", "trans")
    in_specs = (P("case"), P(), P(), block, block, block, P("case", None, "roll", "trans"), block)
    out_specs = (block, block, P("roll", "trans"))
    return jax.shard_map(on_device, mesh=mesh, in_specs=in_specs, out_specs=out_specs, check_vma=False)
```

time: 872 us -> 187 us (0.21); the launches traced: 858 us -> 186 us
  other arithmetic: 533 us -> 0.98 us
  starting transfers between devices: 171 us -> 47.3 us
  Pallas kernels: 0 us -> 40.8 us
  waiting for transfers between devices: 96.9 us -> 68.5 us
  between operations: 23.3 us -> 0.78 us
    add x10 -> x3, other arithmetic: 327 us -> 0.1 us  [the longest x1 0.06 us: case_sum(): mine = mine + lax.ppermute(other, 'case', swap_core)]
    reduce_sum x4 -> x0, other arithmetic: 183 us -> none  [on_device(): term = jnp.sum(lam * film, axis=0)]
    ppermute x52 -> x17, starting transfers between devices: 171 us -> 47.3 us  [the longest x7 33.3 us: both_ways(): from_high = lax.ppermute(up, axis, ring(axis, -1))]
    psum x1 -> x0, waiting for transfers between devices: 79.9 us -> none  [on_device(): gradient = gradient + lax.psum(term, 'case')]
    ppermute x52 -> x17, waiting for transfers between devices: 16.9 us -> 68.5 us  [the longest x7 47.5 us: both_ways(): from_low = lax.ppermute(down, axis, ring(axis, 1))]
    pallas_call x0 -> x6, Pallas kernels: none -> 40.8 us  [call(): pl.pallas_call(body, out_shape=tuple(outs), in_specs=[SM] * len(smem) + [...]
    slice x29 -> x0, local copies, waits for them, and re-layouts: 32.4 us -> none  [the longest x11 14 us: with_halo(): lax.slice_in_dim(block, 0, width, axis=dim)]
    unnamed x13 -> x64, local copies, waits for them, and re-layouts: 1.89 us -> 27.6 us
  transfers between devices with their start and end apart: 53 -> 17, of which waited for: 16 -> 12; matrix products, arithmetic and copies ran while one was open for 25% -> 0% of each run, Pallas kernels for 0% -> 7%
where the time goes in v1:
time: 187 us; the launch traced here: 186 us
  waiting for transfers between devices  68.5 us (37%)
  starting transfers between devices  47.3 us (25%)
  Pallas kernels  40.8 us (22%)
  local copies, waits for them, and re-layouts  27.6 us (15%)
    ppermute x7, waiting for transfers between devices, both_ways(): from_low = lax.ppermute(down, axis, ring(axis, 1))  47.5 us
    pallas_call x6, Pallas kernels, call(): pl.pallas_call(body, out_shape=tuple(outs), in_specs=[SM] * len(smem) + [...  40.8 us
    ppermute x7, starting transfers between devices, both_ways(): from_high = lax.ppermute(up, axis, ring(axis, -1))  33.3 us
    unnamed x64, local copies, waits for them, and re-layouts  27.6 us
    ppermute x7, waiting for transfers between devices, both_ways(): from_high = lax.ppermute(up, axis, ring(axis, -1))  11.6 us
    ppermute x7, starting transfers between devices, both_ways(): from_low = lax.ppermute(down, axis, ring(axis, 1))  9.53 us
    ppermute x1, waiting for transfers between devices, case_sum(): mine = mine + lax.ppermute(mine, 'case', swap_chip)  6.99 us
  transfers between devices with their start and end apart: 17, of which 12 were waited for; matrix products, arithmetic and copies ran while one was open for 0% of the time, Pallas kernels for 7%

profile of v1, /device:TPU:1, one launch (start us, length us, event | category | flops | bytes accessed | tf_op | source)
XLA Modules:
  0.0 185.9 jit_solution(8357976744253843113)
XLA Ops:
  8.4 3.3 %pack.1 = (bf16[128,480]{1,0:T(8,128)(2,1)S(1)}, bf16[64,288]{1,0:T(8,128)(2,1)S(1)}, bf16[32,192]{1,0:T(8,128)(2,1)S(1)}, f32[2,256,128]{2,1,0:T(8,128)S(1)}, f32[2,256,128]{2,1,0:T(8,128)S(1)}) custom-call(f32[31]{0:T(128)S(1)} %copy-done.30, f32[2,256,512]{2,1,0:T(8,128)S(1)} %copy-done.3, f32[2,256,512]{2,1,0:T(8,128)S(1)} %copy-done.5, ...), custom_call_target="tpu_custom_call" | custom-call | bytes 9256960 | tf_op jit(solution)/shard_map/pack/pallas_call | solution.py:332
  15.8 3.7 %collective-permute-done.from_left = f32[2,256,128]{2,1,0:T(8,128)S(1)} collective-permute-done((f32[2,256,128]{2,1,0:T(8,128)S(1)}, f32[2,256,128]{2,1,0:T(8,128)S(1)}, u32[]{:S(2)}, u32[]{:S(2)}) %collective-permute-start) | collective-permute-done | bytes 262176 | tf_op jit(solution)/shard_map/ppermute | solution.py:351
  25.2 6.3 %setup.1 = (f32[2,3,256,640]{3,2,1,0:T(8,128)}, f32[2,256,640]{2,1,0:T(8,128)S(1)}, f32[2,256,640]{2,1,0:T(8,128)S(1)}, f32[2,3,256,128]{3,2,1,0:T(8,128)S(1)}, ...) custom-call(f32[2]{0:T(128)S(1)} %multiply_add_fusion.ratio, ...), custom_call_target="tpu_custom_call" | custom-call | bytes 18997248 | tf_op jit(solution)/shard_map/setup/pallas_call | solution.py:332
  31.4 3.3 %collective-permute-start.2 = (f32[2,80,640]{2,1,0:T(8,128)S(1)}, f32[2,80,640]{2,1,0:T(8,128)S(1)}, u32[]{:S(2)}, u32[]{:S(2)}) collective-permute-start(f32[2,80,640]{2,1,0:T(8,128)S(1)} %get-tuple-element.45), channel_id=1, source_target_pairs={{0,16},{16,32},{32,48},{48,64},{64,80},{80,96},{96,112},{112,128},... | collective-permute-start | bytes 1228808 | tf_op jit(solution)/shard_map/ppermute | solution.py:351
  34.7 5.3 %collective-permute-start.3 = (f32[2,80,640]{2,1,0:T(8,128)S(1)}, f32[2,80,640]{2,1,0:T(8,128)S(1)}, u32[]{:S(2)}, u32[]{:S(2)}) collective-permute-start(f32[2,80,640]{2,1,0:T(8,128)S(1)} %get-tuple-element.46), channel_id=1, source_target_pairs={{0,240},{16,0},{32,16},{48,32},{64,48},{80,64},{96,80},{112,96},{1... | collective-permute-start | bytes 1228808 | tf_op jit(solution)/shard_map/ppermute | solution.py:350
  40.0 10.7 %collective-permute-done.2.top.inner_top = f32[2,80,640]{2,1,0:T(8,128)S(1)} collective-permute-done((f32[2,80,640]{2,1,0:T(8,128)S(1)}, f32[2,80,640]{2,1,0:T(8,128)S(1)}, u32[]{:S(2)}, u32[]{:S(2)}) %collective-permute-start.2) | collective-permute-done | bytes 409632 | tf_op jit(solution)/shard_map/ppermute | solution.py:351
  50.8 3.4 %collective-permute-done.3.bottom.inner_bot = f32[2,80,640]{2,1,0:T(8,128)S(1)} collective-permute-done((f32[2,80,640]{2,1,0:T(8,128)S(1)}, f32[2,80,640]{2,1,0:T(8,128)S(1)}, u32[]{:S(2)}, u32[]{:S(2)}) %collective-permute-start.3) | collective-permute-done | bytes 409632 | tf_op jit(solution)/shard_map/ppermute | solution.py:350
  54.2 5.6 %collective-permute-start.5 = (f32[2,136,640]{2,1,0:T(8,128)S(1)}, f32[2,136,640]{2,1,0:T(8,128)S(1)}, u32[]{:S(2)}, u32[]{:S(2)}) collective-permute-start(f32[2,136,640]{2,1,0:T(8,128)S(1)} %get-tuple-element.50), channel_id=1, source_target_pairs={{0,240},{16,0},{32,16},{48,32},{64,48},{80,64},{96,80},{112,96},{1... | collective-permute-start | bytes 2088968 | tf_op jit(solution)/shard_map/ppermute | solution.py:350
  61.9 3.9 %first.1 = (f32[2,256,640]{2,1,0:T(8,128)S(1)}, f32[2,48,640]{2,1,0:T(8,128)S(1)}, f32[2,48,640]{2,1,0:T(8,128)S(1)}, f32[256,512]{1,0:T(8,128)S(1)}) custom-call(s32[4]{0:T(128)S(1)} %select_convert_fusion.flags, bf16[128,480]{1,0:T(8,128)(2,1)S(1)} %get-tuple-element.39.t_big, bf16[64,288]{1,0:T(8,128)(2,1)S(1)} %get-tuple-element.40.t_mid, ...), custom_call_target="tpu_custom_call" | custom-call | flops 2147483648 | bytes 10043392 | tf_op jit(solution)/shard_map/first/pallas_call | solution.py:332
  65.9 5.1 %collective-permute-start.7 = (f32[2,48,640]{2,1,0:T(8,128)S(1)}, f32[2,48,640]{2,1,0:T(8,128)S(1)}, u32[]{:S(2)}, u32[]{:S(2)}) collective-permute-start(f32[2,48,640]{2,1,0:T(8,128)S(1)} %get-tuple-element.57), channel_id=1, source_target_pairs={{0,240},{16,0},{32,16},{48,32},{64,48},{80,64},{96,80},{112,96},{1... | collective-permute-start | bytes 737288 | tf_op jit(solution)/shard_map/ppermute | solution.py:350
  71.0 23.1 %collective-permute-done.6.lam_top = f32[2,48,640]{2,1,0:T(8,128)S(1)} collective-permute-done((f32[2,48,640]{2,1,0:T(8,128)S(1)}, f32[2,48,640]{2,1,0:T(8,128)S(1)}, u32[]{:S(2)}, u32[]{:S(2)}) %collective-permute-start.6) | collective-permute-done | bytes 245792 | tf_op jit(solution)/shard_map/ppermute | solution.py:351
  94.1 3.7 %collective-permute-start.8 = (f32[2,64,640]{2,1,0:T(8,128)S(1)}, f32[2,64,640]{2,1,0:T(8,128)S(1)}, u32[]{:S(2)}, u32[]{:S(2)}) collective-permute-start(f32[2,64,640]{2,1,0:T(8,128)S(1)} %get-tuple-element.58), channel_id=1, source_target_pairs={{0,16},{16,32},{32,48},{48,64},{64,80},{80,96},{96,112},{112,128},... | collective-permute-start | bytes 983048 | tf_op jit(solution)/shard_map/ppermute | solution.py:351
  97.8 6.0 %collective-permute-start.9 = (f32[2,64,640]{2,1,0:T(8,128)S(1)}, f32[2,64,640]{2,1,0:T(8,128)S(1)}, u32[]{:S(2)}, u32[]{:S(2)}) collective-permute-start(f32[2,64,640]{2,1,0:T(8,128)S(1)} %get-tuple-element.59), channel_id=1, source_target_pairs={{0,240},{16,0},{32,16},{48,32},{64,48},{80,64},{96,80},{112,96},{1... | collective-permute-start | bytes 983048 | tf_op jit(solution)/shard_map/ppermute | solution.py:350
  105.5 8.8 %step2.1 = (f32[2,256,640]{2,1,0:T(8,128)S(1)}, f32[2,48,640]{2,1,0:T(8,128)S(1)}, f32[2,48,640]{2,1,0:T(8,128)S(1)}, f32[2,336,640]{2,1,0:T(8,128)S(1)}, f32[256,512]{1,0:T(8,128)S(1)}) custom-call(f32[2]{0:T(128)S(1)} %multiply_add_fusion.ratio, s32[4]{0:T(128)S(1)} %copy-done.28, s32[4]{0:T(128)S(1)} %select_convert_fusion.flags, ...), custom_call_target="tpu_custom_call" | custom-call | flops 3221225472 | bytes 20299776 | tf_op jit(solution)/shard_map/step2/pallas_call | solution.py:332
  114.3 5.1 %collective-permute-start.11 = (f32[2,48,640]{2,1,0:T(8,128)S(1)}, f32[2,48,640]{2,1,0:T(8,128)S(1)}, u32[]{:S(2)}, u32[]{:S(2)}) collective-permute-start(f32[2,48,640]{2,1,0:T(8,128)S(1)} %get-tuple-element.64), channel_id=1, source_target_pairs={{0,240},{16,0},{32,16},{48,32},{64,48},{80,64},{96,80},{112,96},{1... | collective-permute-start | bytes 737288 | tf_op jit(solution)/shard_map/ppermute | solution.py:350
  119.4 5.3 %collective-permute-done.10.lam_top = f32[2,48,640]{2,1,0:T(8,128)S(1)} collective-permute-done((f32[2,48,640]{2,1,0:T(8,128)S(1)}, f32[2,48,640]{2,1,0:T(8,128)S(1)}, u32[]{:S(2)}, u32[]{:S(2)}) %collective-permute-start.10) | collective-permute-done | bytes 245792 | tf_op jit(solution)/shard_map/ppermute | solution.py:351
  124.7 3.2 %collective-permute-done.11.lam_bot = f32[2,48,640]{2,1,0:T(8,128)S(1)} collective-permute-done((f32[2,48,640]{2,1,0:T(8,128)S(1)}, f32[2,48,640]{2,1,0:T(8,128)S(1)}, u32[]{:S(2)}, u32[]{:S(2)}) %collective-permute-start.11) | collective-permute-done | bytes 245792 | tf_op jit(solution)/shard_map/ppermute | solution.py:350
  127.9 9.4 %step1.1 = (f32[2,256,640]{2,1,0:T(8,128)S(1)}, f32[2,48,640]{2,1,0:T(8,128)}, f32[2,48,640]{2,1,0:T(8,128)}, f32[2,328,640]{2,1,0:T(8,128)S(1)}, f32[256,512]{1,0:T(8,128)S(1)}) custom-call(f32[2]{0:T(128)S(1)} %multiply_add_fusion.ratio, s32[4]{0:T(128)S(1)} %copy-done.28, s32[4]{0:T(128)S(1)} %select_convert_fusion.flags, ...), custom_call_target="tpu_custom_call" | custom-call | flops 3221225472 | bytes 20054016 | tf_op jit(solution)/shard_map/step1/pallas_call | solution.py:332
  140.7 4.8 %collective-permute-start.13 = (f32[2,48,640]{2,1,0:T(8,128)}, f32[2,48,640]{2,1,0:T(8,128)}, u32[]{:S(2)}, u32[]{:S(2)}) collective-permute-start(f32[2,48,640]{2,1,0:T(8,128)} %get-tuple-element.69), channel_id=1, source_target_pairs={{0,240},{16,0},{32,16},{48,32},{64,48},{80,64},{96,80},{112,96},{1... | collective-permute-start | bytes 737288 | tf_op jit(solution)/shard_map/ppermute | solution.py:350
  145.5 4.7 %collective-permute-done.12.lam_top = f32[2,48,640]{2,1,0:T(8,128)} collective-permute-done((f32[2,48,640]{2,1,0:T(8,128)}, f32[2,48,640]{2,1,0:T(8,128)}, u32[]{:S(2)}, u32[]{:S(2)}) %collective-permute-start.12) | collective-permute-done | bytes 245792 | tf_op jit(solution)/shard_map/ppermute | solution.py:351
  150.2 3.5 %collective-permute-done.13.lam_bot = f32[2,48,640]{2,1,0:T(8,128)} collective-permute-done((f32[2,48,640]{2,1,0:T(8,128)}, f32[2,48,640]{2,1,0:T(8,128)}, u32[]{:S(2)}, u32[]{:S(2)}) %collective-permute-start.13) | collective-permute-done | bytes 245792 | tf_op jit(solution)/shard_map/ppermute | solution.py:350
  162.0 9.3 %step0.1 = (f32[2,256,512]{2,1,0:T(8,128)}, f32[2,256,512]{2,1,0:T(8,128)}, f32[256,512]{1,0:T(8,128)S(1)}) custom-call(f32[2]{0:T(128)S(1)} %multiply_add_fusion.ratio, s32[4]{0:T(128)S(1)} %copy-done.29, s32[4]{0:T(128)S(1)} %select_convert_fusion.flags, bf16[128,480]{1,0:T(8,128)(2,1)S(1)} %copy-done.17, bf16[64,288]{1,0:T(8,128)(2,1)S(1)} %copy-done.22, ...), custom_call_target="tpu_custom_call" | custom-call | flops 3221225472 | bytes 18628608 | tf_op jit(solution)/shard_map/step0/pallas_call | solution.py:332
  171.3 2.5 %collective-permute-start.14 = (f32[128,512]{1,0:T(8,128)S(1)}, f32[128,512]{1,0:T(8,128)S(1)}, u32[]{:S(2)}, u32[]{:S(2)}) collective-permute-start(f32[128,512]{1,0:T(8,128)S(1)} %slice_select_fusion), channel_id=1, source_target_pairs={{0,1},{1,0},{2,3},{3,2},{4,5},{5,4},{6,7},{7,6},{8,9},{9,8},{10,11... | collective-permute-start | bytes 786440 | tf_op jit(solution)/shard_map/ppermute | solution.py:366
  175.6 7.0 %collective-permute-done.15 = f32[128,512]{1,0:T(8,128)S(1)} collective-permute-done((f32[128,512]{1,0:T(8,128)S(1)}, f32[128,512]{1,0:T(8,128)S(1)}, u32[]{:S(2)}, u32[]{:S(2)}) %collective-permute-start.15) | collective-permute-done | bytes 262176 | tf_op jit(solution)/shard_map/ppermute | solution.py:367
  (86 shorter events, 38.3 us)
Async XLA Ops:
  8.4 13.4 %copy-start.4 = (f32[2,256,512]{2,1,0:T(8,128)S(1)}, f32[2,256,512]{2,1,0:T(8,128)}, u32[]{:S(2)}) copy-start(f32[2,256,512]{2,1,0:T(8,128)} %diag.3) | copy-start | bytes 3145732
  8.4 13.4 %copy-start.6 = (f32[2,256,512]{2,1,0:T(8,128)S(1)}, f32[2,256,512]{2,1,0:T(8,128)}, u32[]{:S(2)}) copy-start(f32[2,256,512]{2,1,0:T(8,128)} %fx.3) | copy-start | bytes 3145732
  12.3 47.5 %copy-start.15 = (bf16[128,480]{1,0:T(8,128)(2,1)}, bf16[128,480]{1,0:T(8,128)(2,1)S(1)}, u32[]{:S(2)}) copy-start(bf16[128,480]{1,0:T(8,128)(2,1)S(1)} %get-tuple-element.39.t_big) | copy-start | bytes 368644
  12.3 47.5 %copy-start.20 = (bf16[64,288]{1,0:T(8,128)(2,1)}, bf16[64,288]{1,0:T(8,128)(2,1)S(1)}, u32[]{:S(2)}) copy-start(bf16[64,288]{1,0:T(8,128)(2,1)S(1)} %get-tuple-element.40.t_mid) | copy-start | bytes 110596
  12.3 7.3 %collective-permute-start = (f32[2,256,128]{2,1,0:T(8,128)S(1)}, f32[2,256,128]{2,1,0:T(8,128)S(1)}, u32[]{:S(2)}, u32[]{:S(2)}) collective-permute-start(f32[2,256,128]{2,1,0:T(8,128)S(1)} %get-tuple-element.42), channel_id=1, source_target_pairs={{0,4},{4,8},{8,12},{12,0},{1,5},{5,9},{9,13},{13,1},{2,6},{6,10},{... | collective-permute-start | bytes 786440 | tf_op jit(solution)/shard_map/ppermute | solution.py:351
  14.4 6.7 %collective-permute-start.1 = (f32[2,256,128]{2,1,0:T(8,128)S(1)}, f32[2,256,128]{2,1,0:T(8,128)S(1)}, u32[]{:S(2)}, u32[]{:S(2)}) collective-permute-start(f32[2,256,128]{2,1,0:T(8,128)S(1)} %get-tuple-element.43), channel_id=1, source_target_pairs={{0,12},{4,0},{8,4},{12,8},{1,13},{5,1},{9,5},{13,9},{2,14},{6,2},{... | collective-permute-start | bytes 786440 | tf_op jit(solution)/shard_map/ppermute | solution.py:350
  25.2 34.6 %copy-start.26 = (bf16[32,192]{1,0:T(8,128)(2,1)S(1)}, bf16[32,192]{1,0:T(8,128)(2,1)}, u32[]{:S(2)}) copy-start(bf16[32,192]{1,0:T(8,128)(2,1)} %copy-done.25) | copy-start | bytes 36868
  31.4 19.3 %collective-permute-start.2 = (f32[2,80,640]{2,1,0:T(8,128)S(1)}, f32[2,80,640]{2,1,0:T(8,128)S(1)}, u32[]{:S(2)}, u32[]{:S(2)}) collective-permute-start(f32[2,80,640]{2,1,0:T(8,128)S(1)} %get-tuple-element.45), channel_id=1, source_target_pairs={{0,16},{16,32},{32,48},{48,64},{64,80},{80,96},{96,112},{112,128},... | collective-permute-start | bytes 1228808 | tf_op jit(solution)/shard_map/ppermute | solution.py:351
  34.7 19.5 %collective-permute-start.3 = (f32[2,80,640]{2,1,0:T(8,128)S(1)}, f32[2,80,640]{2,1,0:T(8,128)S(1)}, u32[]{:S(2)}, u32[]{:S(2)}) collective-permute-start(f32[2,80,640]{2,1,0:T(8,128)S(1)} %get-tuple-element.46), channel_id=1, source_target_pairs={{0,240},{16,0},{32,16},{48,32},{64,48},{80,64},{96,80},{112,96},{1... | collective-permute-start | bytes 1228808 | tf_op jit(solution)/shard_map/ppermute | solution.py:350
  54.2 49.6 %collective-permute-start.5 = (f32[2,136,640]{2,1,0:T(8,128)S(1)}, f32[2,136,640]{2,1,0:T(8,128)S(1)}, u32[]{:S(2)}, u32[]{:S(2)}) collective-permute-start(f32[2,136,640]{2,1,0:T(8,128)S(1)} %get-tuple-element.50), channel_id=1, source_target_pairs={{0,240},{16,0},{32,16},{48,32},{64,48},{80,64},{96,80},{112,96},{1... | collective-permute-start | bytes 2088968 | tf_op jit(solution)/shard_map/ppermute | solution.py:350
  59.8 44.0 %collective-permute-start.4 = (f32[2,112,640]{2,1,0:T(8,128)S(1)}, f32[2,112,640]{2,1,0:T(8,128)S(1)}, u32[]{:S(2)}, u32[]{:S(2)}) collective-permute-start(f32[2,112,640]{2,1,0:T(8,128)S(1)} %get-tuple-element.49), channel_id=1, source_target_pairs={{0,16},{16,32},{32,48},{48,64},{64,80},{80,96},{96,112},{112,128},... | collective-permute-start | bytes 1720328 | tf_op jit(solution)/shard_map/ppermute | solution.py:351
  61.9 41.8 %copy-start.28 = (s32[4]{0:T(128)S(1)}, s32[4]{0:T(128)}, u32[]{:S(2)}) copy-start(s32[4]{0:T(128)} %shifts.5) | copy-start | bytes 52
  65.8 28.3 %collective-permute-start.6 = (f32[2,48,640]{2,1,0:T(8,128)S(1)}, f32[2,48,640]{2,1,0:T(8,128)S(1)}, u32[]{:S(2)}, u32[]{:S(2)}) collective-permute-start(f32[2,48,640]{2,1,0:T(8,128)S(1)} %get-tuple-element.56), channel_id=1, source_target_pairs={{0,16},{16,32},{32,48},{48,64},{64,80},{80,96},{96,112},{112,128},... | collective-permute-start | bytes 737288 | tf_op jit(solution)/shard_map/ppermute | solution.py:351
  65.9 28.2 %collective-permute-start.7 = (f32[2,48,640]{2,1,0:T(8,128)S(1)}, f32[2,48,640]{2,1,0:T(8,128)S(1)}, u32[]{:S(2)}, u32[]{:S(2)}) collective-permute-start(f32[2,48,640]{2,1,0:T(8,128)S(1)} %get-tuple-element.57), channel_id=1, source_target_pairs={{0,240},{16,0},{32,16},{48,32},{64,48},{80,64},{96,80},{112,96},{1... | collective-permute-start | bytes 737288 | tf_op jit(solution)/shard_map/ppermute | solution.py:350
  94.1 25.3 %collective-permute-start.8 = (f32[2,64,640]{2,1,0:T(8,128)S(1)}, f32[2,64,640]{2,1,0:T(8,128)S(1)}, u32[]{:S(2)}, u32[]{:S(2)}) collective-permute-start(f32[2,64,640]{2,1,0:T(8,128)S(1)} %get-tuple-element.58), channel_id=1, source_target_pairs={{0,16},{16,32},{32,48},{48,64},{64,80},{80,96},{96,112},{112,128},... | collective-permute-start | bytes 983048 | tf_op jit(solution)/shard_map/ppermute | solution.py:351
  97.8 21.6 %collective-permute-start.9 = (f32[2,64,640]{2,1,0:T(8,128)S(1)}, f32[2,64,640]{2,1,0:T(8,128)S(1)}, u32[]{:S(2)}, u32[]{:S(2)}) collective-permute-start(f32[2,64,640]{2,1,0:T(8,128)S(1)} %get-tuple-element.59), channel_id=1, source_target_pairs={{0,240},{16,0},{32,16},{48,32},{64,48},{80,64},{96,80},{112,96},{1... | collective-permute-start | bytes 983048 | tf_op jit(solution)/shard_map/ppermute | solution.py:350
  114.2 10.5 %collective-permute-start.10 = (f32[2,48,640]{2,1,0:T(8,128)S(1)}, f32[2,48,640]{2,1,0:T(8,128)S(1)}, u32[]{:S(2)}, u32[]{:S(2)}) collective-permute-start(f32[2,48,640]{2,1,0:T(8,128)S(1)} %get-tuple-element.63), channel_id=1, source_target_pairs={{0,16},{16,32},{32,48},{48,64},{64,80},{80,96},{96,112},{112,128},... | collective-permute-start | bytes 737288 | tf_op jit(solution)/shard_map/ppermute | solution.py:351
  114.3 13.6 %collective-permute-start.11 = (f32[2,48,640]{2,1,0:T(8,128)S(1)}, f32[2,48,640]{2,1,0:T(8,128)S(1)}, u32[]{:S(2)}, u32[]{:S(2)}) collective-permute-start(f32[2,48,640]{2,1,0:T(8,128)S(1)} %get-tuple-element.64), channel_id=1, source_target_pairs={{0,240},{16,0},{32,16},{48,32},{64,48},{80,64},{96,80},{112,96},{1... | collective-permute-start | bytes 737288 | tf_op jit(solution)/shard_map/ppermute | solution.py:350
  127.9 25.8 %copy-start.27 = (bf16[32,192]{1,0:T(8,128)(2,1)S(1)}, bf16[32,192]{1,0:T(8,128)(2,1)}, u32[]{:S(2)}) copy-start(bf16[32,192]{1,0:T(8,128)(2,1)} %copy-done.25) | copy-start | bytes 36868
  140.4 9.8 %collective-permute-start.12 = (f32[2,48,640]{2,1,0:T(8,128)}, f32[2,48,640]{2,1,0:T(8,128)}, u32[]{:S(2)}, u32[]{:S(2)}) collective-permute-start(f32[2,48,640]{2,1,0:T(8,128)} %get-tuple-element.68), channel_id=1, source_target_pairs={{0,16},{16,32},{32,48},{48,64},{64,80},{80,96},{96,112},{112,128},... | collective-permute-start | bytes 737288 | tf_op jit(solution)/shard_map/ppermute | solution.py:351
  140.7 13.0 %collective-permute-start.13 = (f32[2,48,640]{2,1,0:T(8,128)}, f32[2,48,640]{2,1,0:T(8,128)}, u32[]{:S(2)}, u32[]{:S(2)}) collective-permute-start(f32[2,48,640]{2,1,0:T(8,128)} %get-tuple-element.69), channel_id=1, source_target_pairs={{0,240},{16,0},{32,16},{48,32},{64,48},{80,64},{96,80},{112,96},{1... | collective-permute-start | bytes 737288 | tf_op jit(solution)/shard_map/ppermute | solution.py:350
  171.3 3.7 %collective-permute-start.14 = (f32[128,512]{1,0:T(8,128)S(1)}, f32[128,512]{1,0:T(8,128)S(1)}, u32[]{:S(2)}, u32[]{:S(2)}) collective-permute-start(f32[128,512]{1,0:T(8,128)S(1)} %slice_select_fusion), channel_id=1, source_target_pairs={{0,1},{1,0},{2,3},{3,2},{4,5},{5,4},{6,7},{7,6},{8,9},{9,8},{10,11... | collective-permute-start | bytes 786440 | tf_op jit(solution)/shard_map/ppermute | solution.py:366
  175.0 7.6 %collective-permute-start.15 = (f32[128,512]{1,0:T(8,128)S(1)}, f32[128,512]{1,0:T(8,128)S(1)}, u32[]{:S(2)}, u32[]{:S(2)}) collective-permute-start(f32[128,512]{1,0:T(8,128)S(1)} %select_add_fusion), channel_id=1, source_target_pairs={{0,2},{1,3},{2,0},{3,1},{4,6},{5,7},{6,4},{7,5},{8,10},{9,11},{10,... | collective-permute-start | bytes 786440 | tf_op jit(solution)/shard_map/ppermute | solution.py:367
  182.6 2.5 %collective-permute-start.16 = (f32[128,512]{1,0:T(8,128)S(1)}, f32[128,512]{1,0:T(8,128)S(1)}, u32[]{:S(2)}, u32[]{:S(2)}) collective-permute-start(f32[128,512]{1,0:T(8,128)S(1)} %add.16), channel_id=1, source_target_pairs={{0,1},{1,0},{2,3},{3,2},{4,5},{5,4},{6,7},{7,6},{8,9},{9,8},{10,11... | collective-permute-start | bytes 786440 | tf_op jit(solution)/shard_map/ppermute | solution.py:368
  (25 other events, 35.1 us)

commit v2 on v1

v2 whole, which is shorter than its diff:
```python
import functools

import jax
import jax.numpy as jnp
from jax import lax
from jax.experimental import pallas as pl
from jax.experimental.pallas import tpu as pltpu
from jax.sharding import PartitionSpec as P

STEPS = 4
SWEEPS = 3
KERN = 31
NSRR = 16
HALO = 48
COEF = 32
COLS = STEPS * SWEEPS - 1
BAND = 16
BLOCK = 128
SLOTS = 8

f32 = jnp.float32
bf16 = jnp.bfloat16


def banded(kern_ref, rows):
    width = rows + 2 * BAND
    shape = (rows, 3 * width)
    lane = lax.broadcasted_iota(jnp.int32, shape, 1)
    part = (lane >= width).astype(jnp.int32) + (lane >= 2 * width).astype(jnp.int32)
    tap = lane - part * width - lax.broadcasted_iota(jnp.int32, shape, 0) - 1
    value = jnp.zeros(shape, f32)
    for k in range(KERN):
        value = jnp.where(tap == k, kern_ref[k], value)
    high = value.astype(bf16).astype(f32)
    return jnp.where(part == 1, value - high, high).astype(bf16)


def bands_kernel(kern_ref, gate, mats):
    mats[:, 0:480] = banded(kern_ref, BLOCK)
    mats[0:64, 512:800] = banded(kern_ref, 64)
    mats[0:32, 896:1088] = banded(kern_ref, 32)


def run_copies(pairs, sems):
    copies = [pltpu.make_async_copy(a, b, sems.at[i]) for i, (a, b) in enumerate(pairs)]
    for copy in copies:
        copy.start()
    for copy in copies:
        copy.wait()


def edges_kernel(scal, diag, fx, fy, film, src, up_a, down_a, up_b, down_b, up_c, down_c, sems):
    total = diag.shape[1]
    low, high = slice(0, COEF), slice(total - COEF, total)
    pairs = []
    for edge, a, b, c in ((low, up_a, up_b, up_c), (high, down_a, down_b, down_c)):
        for k, ref in enumerate((diag, fx, fy, src.at[:, STEPS - 1], film)):
            pairs.append((ref.at[:, edge], a.at[:, 32 * k : 32 * k + 32]))
        pairs.append((src.at[:, 2, edge], b.at[:, 0:32]))
        pairs.append((src.at[:, 1, edge], c.at[:, 0:32]))
        pairs.append((src.at[:, 0, edge], c.at[:, 32:64]))
    pairs.append((film.at[:, 32:56], up_b.at[:, 32:56]))
    run_copies(pairs, sems)


def pack_kernel(scal, diag, fx, fy, film, src, left, right, low, high, sems):
    total, cols = diag.shape[1], diag.shape[2]
    refs = [diag, fx, fy, film] + [src.at[:, s] for s in (3, 2, 1, 0)]
    pairs = []
    for slot, ref in enumerate(refs):
        pairs.append((ref.at[:, :, 0:128], low.at[slot]))
        pairs.append((ref.at[:, :, cols - 128 : cols], high.at[slot]))
    run_copies(pairs, sems)
    rows = 32
    lane = lax.broadcasted_iota(jnp.int32, (rows, 128), 1)

    def chunk(i, carry):
        at = pl.ds(pl.multiple_of(i * rows, rows), rows)
        for c in range(2):
            first = jnp.zeros((rows, 128), f32)
            last = jnp.zeros((rows, 128), f32)
            for slot in range(SLOTS):
                place = COLS * slot
                here = (lane >= place) & (lane < place + COLS)
                a, b = low[slot, c, at, :], high[slot, c, at, :]
                first = jnp.where(here, pltpu.roll(a, place, 1) if place else a, first)
                last = jnp.where(here, pltpu.roll(b, (place + COLS) % 128, 1), last)
            left[c, at, :] = first
            right[c, at, :] = last
        return carry

    lax.fori_loop(0, total // rows, chunk, 0)


def ratio_of(scal, c):
    return 0.2 + 1.6 * scal[4 + c].astype(f32) / (NSRR - 1)


def main_kernel(scal, diag, fx, fy, film, src, coef, lam):
    rows = 16

    def chunk(i, carry):
        at = pl.ds(pl.multiple_of(i * rows, rows), rows)
        for c in range(2):
            w = 0.8 / diag[c, at, :]
            coef[c, 0, at, :] = w
            coef[c, 1, at, :] = w * fx[c, at, :]
            coef[c, 2, at, :] = w * fy[c, at, :]
            lam[c, at, :] = w * (src[c, STEPS - 1, at, :] + ratio_of(scal, c) * film[c, at, :])
        return carry

    lax.fori_loop(0, diag.shape[1] // rows, chunk, 0)


def side_kernel(scal, from_left, from_right, side, up, down):
    total = side.shape[2]
    rows = 32
    lane = lax.broadcasted_iota(jnp.int32, (rows, 128), 1)
    is_right = lane < COLS
    inside = (is_right & (scal[9] > 0)) | ((lane >= 128 - COLS) & (scal[8] > 0))

    def chunk(i, carry):
        at = pl.ds(pl.multiple_of(i * rows, rows), rows)
        for c in range(2):
            lo = from_left[c, at, :]
            hi = from_right[c, at, :]

            def halo(slot):
                place = COLS * slot
                right = pltpu.roll(hi, (128 - place) % 128, 1) if place else hi
                left = pltpu.roll(lo, (128 - COLS - place) % 128, 1)
                return jnp.where(inside, jnp.where(is_right, right, left), 0.0)

            w = jnp.where(inside, 0.8 / jnp.where(inside, halo(0), 1.0), 0.0)
            film = halo(3)
            side[c, 0, at, :] = w
            side[c, 1, at, :] = w * halo(1)
            side[c, 2, at, :] = w * halo(2)
            side[c, 3, at, :] = w * (halo(4) + ratio_of(scal, c) * film)
            side[c, 4, at, :] = halo(7)
            side[c, 5, at, :] = halo(6)
            side[c, 6, at, :] = halo(5)
            side[c, 7, at, :] = film
        return carry

    lax.fori_loop(0, total // rows, chunk, 0)

    def packed(c, first, at, count=4):
        result = jnp.zeros((at.stop - at.start, 128), f32)
        place = lax.broadcasted_iota(jnp.int32, result.shape, 1)
        for k in range(count):
            moved_in = pltpu.roll(side[c, first + k, at, :], 32 * k + COLS, 1)
            result = jnp.where((place >= 32 * k) & (place < 32 * k + 2 * COLS), moved_in, result)
        return result

    for c in range(2):
        for ref, at in ((up, slice(0, 32)), (down, slice(total - 32, total))):
            ref[c, 0:32, :] = packed(c, 0, at)
            ref[c, 32:64, :] = packed(c, 4, at)
            ref[c, 64:88, :] = packed(c, 7, slice(32, 56), 1)


def corner(ref, c, which, row, size):
    base, group = (64, 0) if which == 8 else (32 * (which // 4), which % 4)
    tile = ref[c, base + row : base + row + size, :]
    lane = lax.broadcasted_iota(jnp.int32, tile.shape, 1)
    tile = pltpu.roll(tile, 128 - COLS - 32 * group, 1)
    return jnp.where((lane < COLS) | (lane >= 128 - COLS), tile, 0.0)


def beside(main, extra):
    return jnp.concatenate([main, extra], axis=1)


def moved(near, shift):
    stack = jnp.concatenate(near, axis=0)
    size = stack.shape[0]
    return pltpu.roll(stack, size - shift, 0)[0 : size - 8]


def split(value):
    high = value.astype(bf16)
    return high, (value - high.astype(f32)).astype(bf16)


def matrix(mats, size):
    if size == BLOCK:
        return mats[:, 0:480]
    return mats[0:64, 512:800] if size == 64 else mats[0:32, 896:1088]


def sweep(old, new, conv, mats, first, last, coefs, emit):
    lam, high, low = old
    start = first
    while start < last:
        size = BLOCK if last - start >= BLOCK else last - start
        near = slice(start - BAND, start + size + BAND)
        top = high[near, :]
        stack = jnp.concatenate([top, top, low[near, :]], axis=0)
        conv[0:size, :] = jnp.dot(matrix(mats, size), stack, preferred_element_type=f32)
        for row in range(start, start + size, 16):
            w, wx, wy, wr = coefs(row)
            area = lam[row - 8 : row + 24, :]
            mid = area[8:24]
            width = mid.shape[1]
            value = 0.2 * mid + wr
            value = value + wx * (area[7:23] + area[9:25])
            value = value + wy * (pltpu.roll(mid, 1, 1) + pltpu.roll(mid, width - 1, 1))
            value = value - w * conv[row - start : row - start + 16, :]
            emit(row, value, new)
        start += size


def keep(row, value, new):
    lam, high, low = new
    at = slice(row, row + 16)
    lam[at, :] = value
    high[at, :], low[at, :] = split(value)


def first_kernel(
    scal, mats, coef, side, lam_in, film, top, bot, top_corner, bot_corner,
    lam_out, up, down, grad, coef_top, coef_bot, la, ha, oa, lb, hb, ob, conv,
):
    total = lam_in.shape[1]
    cols = grad.shape[1]
    end = HALO + total
    top_ok = scal[6].astype(f32)
    low_ok = scal[7].astype(f32)

    def case(c, carry):
        r = ratio_of(scal, c)
        for ref, edge, ok, out, base in (
            (top, top_corner, top_ok, coef_top, HALO - COEF),
            (bot, bot_corner, low_ok, coef_bot, end),
        ):
            for row in range(0, COEF, 16):
                w = ok * (0.8 / ref[c, row : row + 16, :])
                fx = w * ref[c, 32 + row : 48 + row, :]
                fy = w * ref[c, 64 + row : 80 + row, :]
                lam = w * (ref[c, 96 + row : 112 + row, :] + r * ref[c, 128 + row : 144 + row, :])
                for k, main in enumerate((w, fx, fy)):
                    out[c, k, row : row + 16, :] = beside(main, ok * corner(edge, c, k, row, 16))
                keep(base + row, beside(lam, ok * corner(edge, c, 3, row, 16)), (la, ha, oa))
        for row in range(HALO, end, 16):
            at = slice(row - HALO, row - HALO + 16)
            keep(row, beside(lam_in[c, at, :], side[c, 3, at, :]), (la, ha, oa))

        def coefs(row):
            if row < HALO:
                at = slice(row - HALO + COEF, row - HALO + COEF + 16)
                return (*[coef_top[c, k, at, :] for k in range(3)], None)
            if row >= end:
                at = slice(row - end, row - end + 16)
                return (*[coef_bot[c, k, at, :] for k in range(3)], None)
            at = slice(row - HALO, row - HALO + 16)
            return (*[beside(coef[c, k, at, :], side[c, k, at, :]) for k in range(3)], None)

        def with_rhs(row):
            if HALO <= row < end:
                at = slice(row - HALO, row - HALO + 16)
                return (*coefs(row)[:3], beside(lam_in[c, at, :], side[c, 3, at, :]))
            return (*coefs(row)[:3], la[row : row + 16, :])

        sweep((la, ha, oa), (lb, hb, ob), conv, mats, HALO - 16, end + 16, with_rhs, keep)

        def emit(row, value, new):
            at = slice(row - HALO, row - HALO + 16)
            lam_out[c, at, :] = value
            if row < HALO + HALO:
                up[c, at, :] = value
            if row >= end - HALO:
                down[c, row - end + HALO : row - end + HALO + 16, :] = value
            term = value[:, 0:cols] * film[c, at, :]
            grad[at, :] = jnp.where(c == 0, term, grad[at, :] + term)

        sweep((lb, hb, ob), None, conv, mats, HALO, end, with_rhs, emit)
        return carry

    lax.fori_loop(0, 2, case, 0)


def step_kernel(
    step, scal, mats, coef, side, coef_top, coef_bot, top_corner, bot_corner,
    src, src_top, src_bot, lam_in, lam_top, lam_bot, film, *rest,
):
    final = step == 0
    if step == 2:
        film_top, film_bot, *rest = rest
    grad_in, *rest = rest
    if final:
        lam_out, film_out, mine, other, film_now, grad, *rest = rest
    else:
        lam_out, up, down, film_now, grad, *rest = rest
    la, ha, oa, lb, hb, ob, wr_ref, conv = rest
    total = lam_in.shape[1]
    cols = grad.shape[1]
    end = HALO + total
    top_ok = scal[6].astype(f32)
    low_ok = scal[7].astype(f32)
    reach = 8 * step
    place = {2: 0, 1: 0, 0: 32}[step]

    def case(c, carry):
        r = ratio_of(scal, c)

        def old_film(row):
            if step < 2:
                at = row - (HALO - COEF)
                return film[c, at : at + 8, :]
            if row < HALO:
                at = row - HALO + COEF
                return top_ok * beside(film_top[c, 128 + at : 136 + at, :], corner(top_corner, c, 7, at, 8))
            if row < end:
                at = slice(row - HALO, row - HALO + 8)
                return beside(film[c, at, :], side[c, 7, at, :])
            at = row - end
            if at < 32:
                return low_ok * beside(film_bot[c, 128 + at : 136 + at, :], corner(bot_corner, c, 7, at, 8))
            return low_ok * beside(src_bot[c, at : at + 8, :], corner(bot_corner, c, 8, at - 32, 8))

        def coef_at(row, k):
            if row < HALO:
                return coef_top[c, k, row - HALO + COEF : row - HALO + COEF + 16, :]
            if row >= end:
                return coef_bot[c, k, row - end : row - end + 16, :]
            at = slice(row - HALO, row - HALO + 16)
            return beside(coef[c, k, at, :], side[c, k, at, :])

        def source(row):
            if row < HALO:
                at = row - HALO + COEF
                return beside(src_top[c, place + at : place + at + 16, :], corner(top_corner, c, 4 + step, at, 16))
            if row >= end:
                at = row - end
                return beside(src_bot[c, place + at : place + at + 16, :], corner(bot_corner, c, 4 + step, at, 16))
            at = slice(row - HALO, row - HALO + 16)
            return beside(src[c, step, at, :], side[c, 4 + step, at, :])

        shift = scal[step + 1]
        for row in range(0, end + HALO, 16):
            if row < HALO:
                lam = lam_top[c, row : row + 16, :] * top_ok
            elif row >= end:
                lam = lam_bot[c, row - end : row - end + 16, :] * low_ok
            else:
                lam = lam_in[c, row - HALO : row - HALO + 16, :]
            keep(row, lam, (la, ha, oa))
            if row < HALO - COEF or row >= end + COEF + reach:
                continue
            height = 16 if row + 16 <= end + COEF + reach else 8
            near = [old_film(row + k) for k in range(0, height + 8, 8)]
            now = moved(near, shift) + r * lam[0:height]
            at = row - HALO + COEF
            film_now[c, at : at + height, :] = now
            if row < end + COEF:
                wr_ref[at : at + 16, :] = coef_at(row, 0) * (source(row) + r * now)

        def coefs(row):
            at = row - HALO + COEF
            return coef_at(row, 0), coef_at(row, 1), coef_at(row, 2), wr_ref[at : at + 16, :]

        a, b = (la, ha, oa), (lb, hb, ob)
        sweep(a, b, conv, mats, HALO - 32, end + 32, coefs, keep)
        sweep(b, a, conv, mats, HALO - 16, end + 16, coefs, keep)

        def emit(row, value, new):
            at = slice(row - HALO, row - HALO + 16)
            here = slice(row - HALO + COEF, row - HALO + COEF + 16)
            term = value[:, 0:cols] * film_now[c, here, 0:cols]
            grad[at, :] = jnp.where(c == 0, grad_in[at, :], grad[at, :]) + term
            if final:
                lam_out[c, at, :] = value[:, 0:cols]
                near = [film_now[c, here.start + k : here.start + k + 8, 0:cols] for k in range(0, 24, 8)]
                film_out[c, at, :] = moved(near, scal[0]) + r * value[:, 0:cols]
                return
            lam_out[c, at, :] = value
            if row < HALO + HALO:
                up[c, at, :] = value
            if row >= end - HALO:
                down[c, row - end + HALO : row - end + HALO + 16, :] = value

        sweep(a, None, conv, mats, HALO, end, coefs, emit)
        return carry

    lax.fori_loop(0, 2, case, 0)
    if final:
        half = total // 2
        first = pl.multiple_of(scal[10] * half, half)
        mine[...] = grad[pl.ds(first, half), :]
        other[...] = grad[pl.ds(pl.multiple_of(half - first, half), half), :]


VM = pl.BlockSpec(memory_space=pltpu.VMEM)
SM = pl.BlockSpec(memory_space=pltpu.SMEM)
HB = pl.BlockSpec(memory_space=pltpu.HBM)


def call(body, smem, vmem, outs, scratch=(), flops=0, name=None, space=VM, limit=12):
    moved_bytes = sum(v.size * 4 for v in vmem) + sum(4 * functools.reduce(lambda a, b: a * b, o.shape) for o in outs)
    return pl.pallas_call(
        body,
        out_shape=tuple(outs),
        in_specs=[SM] * len(smem) + [space] * len(vmem),
        out_specs=tuple([VM] * len(outs)),
        scratch_shapes=list(scratch),
        cost_estimate=pl.CostEstimate(flops=flops, bytes_accessed=moved_bytes, transcendentals=0),
        compiler_params=pltpu.CompilerParams(vmem_limit_bytes=limit << 20),
        name=name,
    )(*smem, *[pltpu.with_memory_space_constraint(v, pltpu.HBM) for v in vmem] if space is HB else vmem)


def ring(axis, step):
    count = lax.axis_size(axis)
    return [(i, (i + step) % count) for i in range(count)]


def both_ways(up, down, axis):
    from_high = lax.ppermute(up, axis, ring(axis, -1))
    from_low = lax.ppermute(down, axis, ring(axis, 1))
    return from_low, from_high


def after(values, gate):
    return lax.optimization_barrier((tuple(values), tuple(gate)))[0]


def case_sum(mine, other, core):
    swap_core = [(i, i ^ 1) for i in range(4)]
    swap_chip = [(i, i ^ 2) for i in range(4)]
    mine = mine + lax.ppermute(other, "case", swap_core)
    mine = mine + lax.ppermute(mine, "case", swap_chip)
    other = lax.ppermute(mine, "case", swap_core)
    return jnp.where(
        core == 0, jnp.concatenate([mine, other], axis=0), jnp.concatenate([other, mine], axis=0)
    )


def on_device(ratio_index, shifts, kernel, diagonal, flow_x, flow_y, pres_source, rough_adjoint):
    cases, total, cols = diagonal.shape
    wide = cols + 128
    roll, trans = lax.axis_index("roll"), lax.axis_index("trans")
    core = lax.axis_index("case") % 2
    scal = jnp.concatenate(
        [
            shifts,
            ratio_index,
            jnp.stack(
                [
                    (roll > 0).astype(jnp.int32),
                    (roll < lax.axis_size("roll") - 1).astype(jnp.int32),
                    (trans > 0).astype(jnp.int32),
                    (trans < lax.axis_size("trans") - 1).astype(jnp.int32),
                    core,
                ]
            ),
        ]
    )

    def shape(*dims, dtype=f32):
        return jax.ShapeDtypeStruct(dims, dtype)

    raw = (diagonal, flow_x, flow_y, rough_adjoint, pres_source)
    up_a, down_a, up_b, down_b, up_c, down_c = call(
        edges_kernel,
        (scal,),
        raw,
        [shape(cases, rows, cols) for rows in (160, 160, 56, 32, 64, 64)],
        [pltpu.SemaphoreType.DMA((17,))],
        name="edges",
        space=HB,
    )
    top_a, bot_a = both_ways(up_a, down_a, "roll")
    tile = pltpu.VMEM((SLOTS, cases, total, 128), f32)
    left, right = call(
        pack_kernel,
        (scal,),
        raw,
        [shape(cases, total, 128)] * 2,
        [tile, tile, pltpu.SemaphoreType.DMA((2 * SLOTS,))],
        name="pack",
        space=HB,
    )
    from_left, from_right = both_ways(left, right, "trans")
    (mats,) = call(bands_kernel, (kernel,), (left,), [shape(BLOCK, 1152, dtype=bf16)], name="bands")
    coef, lam = call(
        main_kernel,
        (scal,),
        raw,
        [shape(cases, 3, total, cols), shape(cases, total, cols)],
        name="main",
    )
    from_left, from_right = after((from_left, from_right), (coef, mats))
    side, up, down = call(
        side_kernel,
        (scal,),
        (from_left, from_right),
        [shape(cases, 8, total, 128), shape(cases, 88, 128), shape(cases, 88, 128)],
        name="side",
    )
    top_corner, bot_corner = both_ways(up, down, "roll")
    up_b, down_b = after((up_b, down_b), (top_a, bot_a))
    top_b, bot_b = both_ways(up_b, down_b, "roll")

    rows = total + 2 * HALO
    fields = [pltpu.VMEM((rows, wide), f32), pltpu.VMEM((rows, wide), bf16), pltpu.VMEM((rows, wide), bf16)]
    conv = pltpu.VMEM((BLOCK, wide), f32)
    work = [*fields, *fields, pltpu.VMEM((total + 2 * COEF, wide), f32), conv]
    state = [shape(cases, total, wide), shape(cases, HALO, wide), shape(cases, HALO, wide)]
    lam, up, down, grad, coef_top, coef_bot = call(
        first_kernel,
        (scal,),
        (mats, coef, side, lam, rough_adjoint, top_a, bot_a, top_corner, bot_corner),
        [*state, shape(total, cols), shape(cases, 3, COEF, wide), shape(cases, 3, COEF, wide)],
        [*fields, *fields, conv],
        flops=2 << 30,
        name="first",
    )
    film = rough_adjoint
    for step in range(STEPS - 2, -1, -1):
        lam_top, lam_bot = both_ways(up, down, "roll")
        if step == STEPS - 2:
            up_c, down_c = after((up_c, down_c), (lam_top, lam_bot))
            top_c, bot_c = both_ways(up_c, down_c, "roll")
        src_top, src_bot = (top_b, bot_b) if step == 2 else (top_c, bot_c)
        films = shape(cases, total + 2 * COEF + 8 * step, wide)
        half = shape(total // 2, cols)
        if step:
            outs = [*state, films, shape(total, cols)]
            scratch = work
        else:
            outs = [shape(cases, total, cols), shape(cases, total, cols), half, half]
            scratch = [pltpu.VMEM(films.shape, f32), pltpu.VMEM((total, cols), f32), *work]
        more = (top_a, bot_a) if step == 2 else ()
        result = call(
            functools.partial(step_kernel, step),
            (scal,),
            (
                mats, coef, side, coef_top, coef_bot, top_corner, bot_corner, pres_source, src_top, src_bot,
                lam, lam_top, lam_bot, film, *more, grad,
            ),
            outs,
            scratch,
            flops=3 << 30,
            name="step" + str(step),
        )
        if step:
            lam, up, down, film, grad = result
        else:
            lam, film, mine, other = result
    return lam, film, case_sum(mine, other, core)


def solution(mesh):
    block = P("case", "roll", "trans")
    in_specs = (P("case"), P(), P(), block, block, block, P("case", None, "roll", "trans"), block)
    out_specs = (block, block, P("roll", "trans"))
    return jax.shard_map(on_device, mesh=mesh, in_specs=in_specs, out_specs=out_specs, check_vma=False)
```

time: 187 us -> 133 us (0.71)
  local copies, waits for them, and re-layouts: 27.6 us -> 0.77 us
  waiting for transfers between devices: 68.5 us -> 46.3 us
  Pallas kernels: 40.8 us -> 35.6 us
    ppermute x7 -> x8, waiting for transfers between devices: 47.5 us -> 17.6 us  [both_ways(): from_low = lax.ppermute(down, axis, ring(axis, 1))]
    unnamed x64 -> x12, local copies, waits for them, and re-layouts: 27.6 us -> 0.02 us
    ppermute x7 -> x8, waiting for transfers between devices: 11.6 us -> 20.1 us  [both_ways(): from_high = lax.ppermute(up, axis, ring(axis, -1))]
    ppermute x7 -> x8, starting transfers between devices: 33.3 us -> 39.8 us  [both_ways(): from_high = lax.ppermute(up, axis, ring(axis, -1))]
    pallas_call x6 -> x9, Pallas kernels: 40.8 us -> 35.6 us  [call(): pl.pallas_call(body, out_shape=tuple(outs), in_specs=[SM] * len(smem) + [...]
    ppermute x7 -> x8, starting transfers between devices: 9.53 us -> 5.68 us  [both_ways(): from_low = lax.ppermute(down, axis, ring(axis, 1))]
    ppermute x1, starting transfers between devices: 2.51 us -> 0.5 us  [case_sum(): mine = mine + lax.ppermute(other, 'case', swap_core)]
  transfers between devices with their start and end apart: 17 -> 19, of which waited for: 12 -> 12; matrix products, arithmetic and copies ran while one was open for 0% -> 0% of each run, Pallas kernels for 7% -> 12%
where the time goes in v2:
time: 133 us
  starting transfers between devices  48.6 us (37%)
  waiting for transfers between devices  46.3 us (35%)
  Pallas kernels  35.6 us (27%)
    ppermute x8, starting transfers between devices, both_ways(): from_high = lax.ppermute(up, axis, ring(axis, -1))  39.8 us
    pallas_call x9, Pallas kernels, call(): pl.pallas_call(body, out_shape=tuple(outs), in_specs=[SM] * len(smem) + [...  35.6 us
    ppermute x8, waiting for transfers between devices, both_ways(): from_high = lax.ppermute(up, axis, ring(axis, -1))  20.1 us
    ppermute x8, waiting for transfers between devices, both_ways(): from_low = lax.ppermute(down, axis, ring(axis, 1))  17.6 us
    ppermute x1, waiting for transfers between devices, case_sum(): mine = mine + lax.ppermute(mine, 'case', swap_chip)  6.29 us
    ppermute x8, starting transfers between devices, both_ways(): from_low = lax.ppermute(down, axis, ring(axis, 1))  5.68 us
  transfers between devices with their start and end apart: 19, of which 12 were waited for; matrix products, arithmetic and copies ran while one was open for 0% of the time, Pallas kernels for 12%

profile of v2, /device:TPU:1, one launch (start us, length us, event | category | flops | bytes accessed | tf_op | source)
XLA Modules:
  0.0 132.9 jit_solution(2769112864339181075)
XLA Ops:
  1.4 2.3 %edges.1 = (f32[2,160,512]{2,1,0:T(8,128)S(1)}, f32[2,160,512]{2,1,0:T(8,128)S(1)}, f32[2,56,512]{2,1,0:T(8,128)S(1)}, f32[2,32,512]{2,1,0:T(8,128)S(1)}, f32[2,...) custom-call(s32[11]{0:T(128)S(1)} %concatenate.9.scal, f32[2,256,512]{2,1,0:T(8,128)} %diag.5, f32[2,256,512]{2,1,0:T(8,128)} %fx.5, ...), custom_call_target="tpu_custom_call" | custom-call | bytes 10584064 | tf_op jit(solution)/shard_map/edges/pallas_call | solution.py:401
  3.7 3.7 %collective-permute-start.2 = (f32[2,160,512]{2,1,0:T(8,128)S(1)}, f32[2,160,512]{2,1,0:T(8,128)S(1)}, u32[]{:S(2)}, u32[]{:S(2)}) collective-permute-start(f32[2,160,512]{2,1,0:T(8,128)S(1)} %get-tuple-element.49), channel_id=1, source_target_pairs={{0,16},{16,32},{32,48},{48,64},{64,80},{80,96},{96,112},{112,128},... | collective-permute-start | bytes 1966088 | tf_op jit(solution)/shard_map/ppermute | solution.py:420
  7.4 5.4 %collective-permute-start.3 = (f32[2,160,512]{2,1,0:T(8,128)S(1)}, f32[2,160,512]{2,1,0:T(8,128)S(1)}, u32[]{:S(2)}, u32[]{:S(2)}) collective-permute-start(f32[2,160,512]{2,1,0:T(8,128)S(1)} %get-tuple-element.50), channel_id=1, source_target_pairs={{0,240},{16,0},{32,16},{48,32},{64,48},{80,64},{96,80},{112,96},{1... | collective-permute-start | bytes 1966088 | tf_op jit(solution)/shard_map/ppermute | solution.py:419
  12.8 4.7 %pack.1 = (f32[2,256,128]{2,1,0:T(8,128)S(1)}, f32[2,256,128]{2,1,0:T(8,128)S(1)}) custom-call(s32[11]{0:T(128)S(1)} %concatenate.9.scal, f32[2,256,512]{2,1,0:T(8,128)} %diag.5, f32[2,256,512]{2,1,0:T(8,128)} %fx.5, f32[2,256,512]{2,1,0:T(8,128)} %fy.5, f32[2,256,512]{2,1,0:T(8,128)} %film.9, f32[2,4,256,512]{3,2,1,0:T(8,128)} %src.11), custom_call_target="tpu_custom_call" | custom-call | bytes 8912896 | tf_op jit(solution)/shard_map/pack/pallas_call | solution.py:401
  23.2 2.6 %collective-permute-done.from_left = f32[2,256,128]{2,1,0:T(8,128)S(1)} collective-permute-done((f32[2,256,128]{2,1,0:T(8,128)S(1)}, f32[2,256,128]{2,1,0:T(8,128)S(1)}, u32[]{:S(2)}, u32[]{:S(2)}) %collective-permute-start) | collective-permute-done | bytes 262176 | tf_op jit(solution)/shard_map/ppermute | solution.py:420
  25.8 2.3 %side.1 = (f32[2,8,256,128]{3,2,1,0:T(8,128)S(1)}, f32[2,88,128]{2,1,0:T(8,128)S(1)}, f32[2,88,128]{2,1,0:T(8,128)S(1)}) custom-call(s32[11]{0:T(128)S(1)} %concatenate.9.scal, f32[2,256,128]{2,1,0:T(8,128)S(1)} %collective-permute-done.from_left, f32[2,256,128]{2,1,0:T(8,128)S(1)} %collective-permute-done.1.from_right), custom_call_target="tpu_custom_call" | custom-call | bytes 2801664 | tf_op jit(solution)/shard_map/side/pallas_call | solution.py:401
  28.2 5.1 %collective-permute-start.5 = (f32[2,88,128]{2,1,0:T(8,128)S(1)}, f32[2,88,128]{2,1,0:T(8,128)S(1)}, u32[]{:S(2)}, u32[]{:S(2)}) collective-permute-start(f32[2,88,128]{2,1,0:T(8,128)S(1)} %get-tuple-element.52), channel_id=1, source_target_pairs={{0,240},{16,0},{32,16},{48,32},{64,48},{80,64},{96,80},{112,96},{1... | collective-permute-start | bytes 270344 | tf_op jit(solution)/shard_map/ppermute | solution.py:419
  33.3 5.4 %collective-permute-done.4.top_corner = f32[2,88,128]{2,1,0:T(8,128)S(1)} collective-permute-done((f32[2,88,128]{2,1,0:T(8,128)S(1)}, f32[2,88,128]{2,1,0:T(8,128)S(1)}, u32[]{:S(2)}, u32[]{:S(2)}) %collective-permute-start.4) | collective-permute-done | bytes 90144 | tf_op jit(solution)/shard_map/ppermute | solution.py:420
  38.7 3.5 %collective-permute-done.5.bot_corner = f32[2,88,128]{2,1,0:T(8,128)S(1)} collective-permute-done((f32[2,88,128]{2,1,0:T(8,128)S(1)}, f32[2,88,128]{2,1,0:T(8,128)S(1)}, u32[]{:S(2)}, u32[]{:S(2)}) %collective-permute-start.5) | collective-permute-done | bytes 90144 | tf_op jit(solution)/shard_map/ppermute | solution.py:419
  42.2 3.8 %first.1 = (f32[2,256,640]{2,1,0:T(8,128)S(1)}, f32[2,48,640]{2,1,0:T(8,128)S(1)}, f32[2,48,640]{2,1,0:T(8,128)S(1)}, f32[256,512]{1,0:T(8,128)S(1)}, f32[2,3,32...) custom-call(s32[11]{0:T(128)S(1)} %concatenate.9.scal, bf16[128,1152]{1,0:T(8,128)(2,1)S(1)} %bands.1.mats, ...), custom_call_target="tpu_custom_call" | custom-call | flops 2147483648 | bytes 12730368 | tf_op jit(solution)/shard_map/first/pallas_call | solution.py:401
  46.3 5.4 %collective-permute-start.7 = (f32[2,48,640]{2,1,0:T(8,128)S(1)}, f32[2,48,640]{2,1,0:T(8,128)S(1)}, u32[]{:S(2)}, u32[]{:S(2)}) collective-permute-start(f32[2,48,640]{2,1,0:T(8,128)S(1)} %get-tuple-element.58), channel_id=1, source_target_pairs={{0,240},{16,0},{32,16},{48,32},{64,48},{80,64},{96,80},{112,96},{1... | collective-permute-start | bytes 737288 | tf_op jit(solution)/shard_map/ppermute | solution.py:419
  51.7 2.9 %collective-permute-start.11 = (f32[2,56,512]{2,1,0:T(8,128)S(1)}, f32[2,56,512]{2,1,0:T(8,128)S(1)}, u32[]{:S(2)}, u32[]{:S(2)}) collective-permute-start(f32[2,56,512]{2,1,0:T(8,128)S(1)} %get-tuple-element.64), channel_id=1, source_target_pairs={{0,240},{16,0},{32,16},{48,32},{64,48},{80,64},{96,80},{112,96},{1... | collective-permute-start | bytes 688136 | tf_op jit(solution)/shard_map/ppermute | solution.py:419
  56.2 3.6 %collective-permute-done.7.lam_bot = f32[2,48,640]{2,1,0:T(8,128)S(1)} collective-permute-done((f32[2,48,640]{2,1,0:T(8,128)S(1)}, f32[2,48,640]{2,1,0:T(8,128)S(1)}, u32[]{:S(2)}, u32[]{:S(2)}) %collective-permute-start.7) | collective-permute-done | bytes 245792 | tf_op jit(solution)/shard_map/ppermute | solution.py:419
  59.8 9.4 %collective-permute-start.9 = (f32[2,64,512]{2,1,0:T(8,128)S(1)}, f32[2,64,512]{2,1,0:T(8,128)S(1)}, u32[]{:S(2)}, u32[]{:S(2)}) collective-permute-start(f32[2,64,512]{2,1,0:T(8,128)S(1)} %get-tuple-element.60), channel_id=1, source_target_pairs={{0,240},{16,0},{32,16},{48,32},{64,48},{80,64},{96,80},{112,96},{1... | collective-permute-start | bytes 786440 | tf_op jit(solution)/shard_map/ppermute | solution.py:419
  69.2 6.2 %step2.1 = (f32[2,256,640]{2,1,0:T(8,128)S(1)}, f32[2,48,640]{2,1,0:T(8,128)S(1)}, f32[2,48,640]{2,1,0:T(8,128)S(1)}, f32[2,336,640]{2,1,0:T(8,128)S(1)}, f32[256,512]{1,0:T(8,128)S(1)}) custom-call(s32[11]{0:T(128)S(1)} %concatenate.9.scal, bf16[128,1152]{1,0:T(8,128)(2,1)S(1)} %bands.1.mats, f32[2,3,256,512]{3,2,1,0:T(8,128)S(1)} %get-tuple-element.43.coef, ...), custom_call_target="tpu_custom_call" | custom-call | flops 3221225472 | bytes 20283392 | tf_op jit(solution)/shard_map/step2/pallas_call | solution.py:401
  75.5 5.1 %collective-permute-start.13 = (f32[2,48,640]{2,1,0:T(8,128)S(1)}, f32[2,48,640]{2,1,0:T(8,128)S(1)}, u32[]{:S(2)}, u32[]{:S(2)}) collective-permute-start(f32[2,48,640]{2,1,0:T(8,128)S(1)} %get-tuple-element.69), channel_id=1, source_target_pairs={{0,240},{16,0},{32,16},{48,32},{64,48},{80,64},{96,80},{112,96},{1... | collective-permute-start | bytes 737288 | tf_op jit(solution)/shard_map/ppermute | solution.py:419
  80.6 3.7 %collective-permute-done.12.lam_top = f32[2,48,640]{2,1,0:T(8,128)S(1)} collective-permute-done((f32[2,48,640]{2,1,0:T(8,128)S(1)}, f32[2,48,640]{2,1,0:T(8,128)S(1)}, u32[]{:S(2)}, u32[]{:S(2)}) %collective-permute-start.12) | collective-permute-done | bytes 245792 | tf_op jit(solution)/shard_map/ppermute | solution.py:420
  84.3 5.6 %collective-permute-done.13.lam_bot = f32[2,48,640]{2,1,0:T(8,128)S(1)} collective-permute-done((f32[2,48,640]{2,1,0:T(8,128)S(1)}, f32[2,48,640]{2,1,0:T(8,128)S(1)}, u32[]{:S(2)}, u32[]{:S(2)}) %collective-permute-start.13) | collective-permute-done | bytes 245792 | tf_op jit(solution)/shard_map/ppermute | solution.py:419
  89.9 6.1 %step1.1 = (f32[2,256,640]{2,1,0:T(8,128)S(1)}, f32[2,48,640]{2,1,0:T(8,128)S(1)}, f32[2,48,640]{2,1,0:T(8,128)S(1)}, f32[2,328,640]{2,1,0:T(8,128)S(1)}, f32[256,512]{1,0:T(8,128)S(1)}) custom-call(s32[11]{0:T(128)S(1)} %concatenate.9.scal, bf16[128,1152]{1,0:T(8,128)(2,1)S(1)} %bands.1.mats, f32[2,3,256,512]{3,2,1,0:T(8,128)S(1)} %get-tuple-element.43.coef, ...), custom_call_target="tpu_custom_call" | custom-call | flops 3221225472 | bytes 19767296 | tf_op jit(solution)/shard_map/step1/pallas_call | solution.py:401
  96.2 5.1 %collective-permute-start.15 = (f32[2,48,640]{2,1,0:T(8,128)S(1)}, f32[2,48,640]{2,1,0:T(8,128)S(1)}, u32[]{:S(2)}, u32[]{:S(2)}) collective-permute-start(f32[2,48,640]{2,1,0:T(8,128)S(1)} %get-tuple-element.74), channel_id=1, source_target_pairs={{0,240},{16,0},{32,16},{48,32},{64,48},{80,64},{96,80},{112,96},{1... | collective-permute-start | bytes 737288 | tf_op jit(solution)/shard_map/ppermute | solution.py:419
  101.2 4.3 %collective-permute-done.14.lam_top = f32[2,48,640]{2,1,0:T(8,128)S(1)} collective-permute-done((f32[2,48,640]{2,1,0:T(8,128)S(1)}, f32[2,48,640]{2,1,0:T(8,128)S(1)}, u32[]{:S(2)}, u32[]{:S(2)}) %collective-permute-start.14) | collective-permute-done | bytes 245792 | tf_op jit(solution)/shard_map/ppermute | solution.py:420
  105.6 7.4 %collective-permute-done.15.lam_bot = f32[2,48,640]{2,1,0:T(8,128)S(1)} collective-permute-done((f32[2,48,640]{2,1,0:T(8,128)S(1)}, f32[2,48,640]{2,1,0:T(8,128)S(1)}, u32[]{:S(2)}, u32[]{:S(2)}) %collective-permute-start.15) | collective-permute-done | bytes 245792 | tf_op jit(solution)/shard_map/ppermute | solution.py:419
  112.9 7.4 %step0.1 = (f32[2,256,512]{2,1,0:T(8,128)}, f32[2,256,512]{2,1,0:T(8,128)}, f32[128,512]{1,0:T(8,128)S(1)}, f32[128,512]{1,0:T(8,128)S(1)}) custom-call(s32[11]{0:T(128)S(1)} %concatenate.9.scal, bf16[128,1152]{1,0:T(8,128)(2,1)S(1)} %bands.1.mats, f32[2,3,256,512]{3,2,1,0:T(8,128)S(1)} %get-tuple-element.43.coef, ...), custom_call_target="tpu_custom_call" | custom-call | flops 3221225472 | bytes 18341888 | tf_op jit(solution)/shard_map/step0/pallas_call | solution.py:401
  123.3 6.3 %collective-permute-done.17 = f32[128,512]{1,0:T(8,128)S(1)} collective-permute-done((f32[128,512]{1,0:T(8,128)S(1)}, f32[128,512]{1,0:T(8,128)S(1)}, u32[]{:S(2)}, u32[]{:S(2)}) %collective-permute-start.17) | collective-permute-done | bytes 262176 | tf_op jit(solution)/shard_map/ppermute | solution.py:432
  (39 shorter events, 15.0 us)
Async XLA Ops:
  3.7 38.4 %collective-permute-start.2 = (f32[2,160,512]{2,1,0:T(8,128)S(1)}, f32[2,160,512]{2,1,0:T(8,128)S(1)}, u32[]{:S(2)}, u32[]{:S(2)}) collective-permute-start(f32[2,160,512]{2,1,0:T(8,128)S(1)} %get-tuple-element.49), channel_id=1, source_target_pairs={{0,16},{16,32},{32,48},{48,64},{64,80},{80,96},{96,112},{112,128},... | collective-permute-start | bytes 1966088 | tf_op jit(solution)/shard_map/ppermute | solution.py:420
  7.4 13.1 %copy-start.1 = (f32[2,256,512]{2,1,0:T(8,128)S(1)}, f32[2,256,512]{2,1,0:T(8,128)}, u32[]{:S(2)}) copy-start(f32[2,256,512]{2,1,0:T(8,128)} %film.9) | copy-start | bytes 3145732
  7.4 13.1 %copy-start.2 = (f32[2,256,512]{2,1,0:T(8,128)S(1)}, f32[2,256,512]{2,1,0:T(8,128)}, u32[]{:S(2)}) copy-start(f32[2,256,512]{2,1,0:T(8,128)} %diag.5) | copy-start | bytes 3145732
  7.4 13.1 %copy-start.3 = (f32[2,256,512]{2,1,0:T(8,128)S(1)}, f32[2,256,512]{2,1,0:T(8,128)}, u32[]{:S(2)}) copy-start(f32[2,256,512]{2,1,0:T(8,128)} %fx.5) | copy-start | bytes 3145732
  7.4 13.1 %copy-start.4 = (f32[2,256,512]{2,1,0:T(8,128)S(1)}, f32[2,256,512]{2,1,0:T(8,128)}, u32[]{:S(2)}) copy-start(f32[2,256,512]{2,1,0:T(8,128)} %fy.5) | copy-start | bytes 3145732
  7.4 34.8 %collective-permute-start.3 = (f32[2,160,512]{2,1,0:T(8,128)S(1)}, f32[2,160,512]{2,1,0:T(8,128)S(1)}, u32[]{:S(2)}, u32[]{:S(2)}) collective-permute-start(f32[2,160,512]{2,1,0:T(8,128)S(1)} %get-tuple-element.50), channel_id=1, source_target_pairs={{0,240},{16,0},{32,16},{48,32},{64,48},{80,64},{96,80},{112,96},{1... | collective-permute-start | bytes 1966088 | tf_op jit(solution)/shard_map/ppermute | solution.py:419
  12.8 7.6 %copy-start = (f32[2,4,256,512]{3,2,1,0:T(8,128)S(1)}, f32[2,4,256,512]{3,2,1,0:T(8,128)}, u32[]{:S(2)}) copy-start(f32[2,4,256,512]{3,2,1,0:T(8,128)} %src.11) | copy-start | bytes 12582916
  17.5 8.3 %collective-permute-start = (f32[2,256,128]{2,1,0:T(8,128)S(1)}, f32[2,256,128]{2,1,0:T(8,128)S(1)}, u32[]{:S(2)}, u32[]{:S(2)}) collective-permute-start(f32[2,256,128]{2,1,0:T(8,128)S(1)} %get-tuple-element.44), channel_id=1, source_target_pairs={{0,4},{4,8},{8,12},{12,0},{1,5},{5,9},{9,13},{13,1},{2,6},{6,10},{... | collective-permute-start | bytes 786440 | tf_op jit(solution)/shard_map/ppermute | solution.py:420
  18.9 6.9 %collective-permute-start.1 = (f32[2,256,128]{2,1,0:T(8,128)S(1)}, f32[2,256,128]{2,1,0:T(8,128)S(1)}, u32[]{:S(2)}, u32[]{:S(2)}) collective-permute-start(f32[2,256,128]{2,1,0:T(8,128)S(1)} %get-tuple-element.42.gate), channel_id=1, source_target_pairs={{0,12},{4,0},{8,4},{12,8},{1,13},{5,1},{9,5},{13,9},{2,14},{6,2},{... | collective-permute-start | bytes 786440 | tf_op jit(solution)/shard_map/ppermute | solution.py:419
  28.1 10.6 %collective-permute-start.4 = (f32[2,88,128]{2,1,0:T(8,128)S(1)}, f32[2,88,128]{2,1,0:T(8,128)S(1)}, u32[]{:S(2)}, u32[]{:S(2)}) collective-permute-start(f32[2,88,128]{2,1,0:T(8,128)S(1)} %get-tuple-element.51), channel_id=1, source_target_pairs={{0,16},{16,32},{32,48},{48,64},{64,80},{80,96},{96,112},{112,128},... | collective-permute-start | bytes 270344 | tf_op jit(solution)/shard_map/ppermute | solution.py:420
  28.2 14.0 %collective-permute-start.5 = (f32[2,88,128]{2,1,0:T(8,128)S(1)}, f32[2,88,128]{2,1,0:T(8,128)S(1)}, u32[]{:S(2)}, u32[]{:S(2)}) collective-permute-start(f32[2,88,128]{2,1,0:T(8,128)S(1)} %get-tuple-element.52), channel_id=1, source_target_pairs={{0,240},{16,0},{32,16},{48,32},{64,48},{80,64},{96,80},{112,96},{1... | collective-permute-start | bytes 270344 | tf_op jit(solution)/shard_map/ppermute | solution.py:419
  46.0 10.2 %collective-permute-start.6 = (f32[2,48,640]{2,1,0:T(8,128)S(1)}, f32[2,48,640]{2,1,0:T(8,128)S(1)}, u32[]{:S(2)}, u32[]{:S(2)}) collective-permute-start(f32[2,48,640]{2,1,0:T(8,128)S(1)} %get-tuple-element.57), channel_id=1, source_target_pairs={{0,16},{16,32},{32,48},{48,64},{64,80},{80,96},{96,112},{112,128},... | collective-permute-start | bytes 737288 | tf_op jit(solution)/shard_map/ppermute | solution.py:420
  46.3 13.5 %collective-permute-start.7 = (f32[2,48,640]{2,1,0:T(8,128)S(1)}, f32[2,48,640]{2,1,0:T(8,128)S(1)}, u32[]{:S(2)}, u32[]{:S(2)}) collective-permute-start(f32[2,48,640]{2,1,0:T(8,128)S(1)} %get-tuple-element.58), channel_id=1, source_target_pairs={{0,240},{16,0},{32,16},{48,32},{64,48},{80,64},{96,80},{112,96},{1... | collective-permute-start | bytes 737288 | tf_op jit(solution)/shard_map/ppermute | solution.py:419
  51.7 17.5 %collective-permute-start.11 = (f32[2,56,512]{2,1,0:T(8,128)S(1)}, f32[2,56,512]{2,1,0:T(8,128)S(1)}, u32[]{:S(2)}, u32[]{:S(2)}) collective-permute-start(f32[2,56,512]{2,1,0:T(8,128)S(1)} %get-tuple-element.64), channel_id=1, source_target_pairs={{0,240},{16,0},{32,16},{48,32},{64,48},{80,64},{96,80},{112,96},{1... | collective-permute-start | bytes 688136 | tf_op jit(solution)/shard_map/ppermute | solution.py:419
  54.6 14.6 %collective-permute-start.10 = (f32[2,32,512]{2,1,0:T(8,128)S(1)}, f32[2,32,512]{2,1,0:T(8,128)S(1)}, u32[]{:S(2)}, u32[]{:S(2)}) collective-permute-start(f32[2,32,512]{2,1,0:T(8,128)S(1)} %get-tuple-element.63), channel_id=1, source_target_pairs={{0,16},{16,32},{32,48},{48,64},{64,80},{80,96},{96,112},{112,128},... | collective-permute-start | bytes 393224 | tf_op jit(solution)/shard_map/ppermute | solution.py:420
  59.8 30.1 %collective-permute-start.8 = (f32[2,64,512]{2,1,0:T(8,128)S(1)}, f32[2,64,512]{2,1,0:T(8,128)S(1)}, u32[]{:S(2)}, u32[]{:S(2)}) collective-permute-start(f32[2,64,512]{2,1,0:T(8,128)S(1)} %get-tuple-element.59), channel_id=1, source_target_pairs={{0,16},{16,32},{32,48},{48,64},{64,80},{80,96},{96,112},{112,128},... | collective-permute-start | bytes 786440 | tf_op jit(solution)/shard_map/ppermute | solution.py:420
  59.8 30.1 %collective-permute-start.9 = (f32[2,64,512]{2,1,0:T(8,128)S(1)}, f32[2,64,512]{2,1,0:T(8,128)S(1)}, u32[]{:S(2)}, u32[]{:S(2)}) collective-permute-start(f32[2,64,512]{2,1,0:T(8,128)S(1)} %get-tuple-element.60), channel_id=1, source_target_pairs={{0,240},{16,0},{32,16},{48,32},{64,48},{80,64},{96,80},{112,96},{1... | collective-permute-start | bytes 786440 | tf_op jit(solution)/shard_map/ppermute | solution.py:419
  75.4 8.8 %collective-permute-start.12 = (f32[2,48,640]{2,1,0:T(8,128)S(1)}, f32[2,48,640]{2,1,0:T(8,128)S(1)}, u32[]{:S(2)}, u32[]{:S(2)}) collective-permute-start(f32[2,48,640]{2,1,0:T(8,128)S(1)} %get-tuple-element.68), channel_id=1, source_target_pairs={{0,16},{16,32},{32,48},{48,64},{64,80},{80,96},{96,112},{112,128},... | collective-permute-start | bytes 737288 | tf_op jit(solution)/shard_map/ppermute | solution.py:420
  75.5 14.4 %collective-permute-start.13 = (f32[2,48,640]{2,1,0:T(8,128)S(1)}, f32[2,48,640]{2,1,0:T(8,128)S(1)}, u32[]{:S(2)}, u32[]{:S(2)}) collective-permute-start(f32[2,48,640]{2,1,0:T(8,128)S(1)} %get-tuple-element.69), channel_id=1, source_target_pairs={{0,240},{16,0},{32,16},{48,32},{64,48},{80,64},{96,80},{112,96},{1... | collective-permute-start | bytes 737288 | tf_op jit(solution)/shard_map/ppermute | solution.py:419
  96.1 9.5 %collective-permute-start.14 = (f32[2,48,640]{2,1,0:T(8,128)S(1)}, f32[2,48,640]{2,1,0:T(8,128)S(1)}, u32[]{:S(2)}, u32[]{:S(2)}) collective-permute-start(f32[2,48,640]{2,1,0:T(8,128)S(1)} %get-tuple-element.73), channel_id=1, source_target_pairs={{0,16},{16,32},{32,48},{48,64},{64,80},{80,96},{96,112},{112,128},... | collective-permute-start | bytes 737288 | tf_op jit(solution)/shard_map/ppermute | solution.py:420
  96.2 16.7 %collective-permute-start.15 = (f32[2,48,640]{2,1,0:T(8,128)S(1)}, f32[2,48,640]{2,1,0:T(8,128)S(1)}, u32[]{:S(2)}, u32[]{:S(2)}) collective-permute-start(f32[2,48,640]{2,1,0:T(8,128)S(1)} %get-tuple-element.74), channel_id=1, source_target_pairs={{0,240},{16,0},{32,16},{48,32},{64,48},{80,64},{96,80},{112,96},{1... | collective-permute-start | bytes 737288 | tf_op jit(solution)/shard_map/ppermute | solution.py:419
  120.3 1.7 %collective-permute-start.16 = (f32[128,512]{1,0:T(8,128)S(1)}, f32[128,512]{1,0:T(8,128)S(1)}, u32[]{:S(2)}, u32[]{:S(2)}) collective-permute-start(f32[128,512]{1,0:T(8,128)S(1)} %get-tuple-element.80), channel_id=1, source_target_pairs={{0,1},{1,0},{2,3},{3,2},{4,5},{5,4},{6,7},{7,6},{8,9},{9,8},{10,11... | collective-permute-start | bytes 786440 | tf_op jit(solution)/shard_map/ppermute | solution.py:431
  122.0 7.6 %collective-permute-start.17 = (f32[128,512]{1,0:T(8,128)S(1)}, f32[128,512]{1,0:T(8,128)S(1)}, u32[]{:S(2)}, u32[]{:S(2)}) collective-permute-start(f32[128,512]{1,0:T(8,128)S(1)} %add.11), channel_id=1, source_target_pairs={{0,2},{1,3},{2,0},{3,1},{4,6},{5,7},{6,4},{7,5},{8,10},{9,11},{10,... | collective-permute-start | bytes 786440 | tf_op jit(solution)/shard_map/ppermute | solution.py:432
  129.6 2.5 %collective-permute-start.18 = (f32[128,512]{1,0:T(8,128)S(1)}, f32[128,512]{1,0:T(8,128)S(1)}, u32[]{:S(2)}, u32[]{:S(2)}) collective-permute-start(f32[128,512]{1,0:T(8,128)S(1)} %add.12), channel_id=1, source_target_pairs={{0,1},{1,0},{2,3},{3,2},{4,5},{5,4},{6,7},{7,6},{8,9},{9,8},{10,11... | collective-permute-start | bytes 786440 | tf_op jit(solution)/shard_map/ppermute | solution.py:433
  (1 other events, 2.6 us)

commit v3 on v2

v3 whole, which is shorter than its diff:
```python
import functools

import jax
import jax.numpy as jnp
from jax import lax
from jax.experimental import pallas as pl
from jax.experimental.pallas import tpu as pltpu
from jax.sharding import PartitionSpec as P

STEPS = 4
SWEEPS = 3
KERN = 31
NSRR = 16
HALO = 48
COEF = 32
COLS = STEPS * SWEEPS - 1
BAND = 16
BLOCK = 128
SLOTS = 8

f32 = jnp.float32
bf16 = jnp.bfloat16


def banded(kern_ref, rows):
    width = rows + 2 * BAND
    shape = (rows, 3 * width)
    lane = lax.broadcasted_iota(jnp.int32, shape, 1)
    part = (lane >= width).astype(jnp.int32) + (lane >= 2 * width).astype(jnp.int32)
    tap = lane - part * width - lax.broadcasted_iota(jnp.int32, shape, 0) - 1
    value = jnp.zeros(shape, f32)
    for k in range(KERN):
        value = jnp.where(tap == k, kern_ref[k], value)
    high = value.astype(bf16).astype(f32)
    return jnp.where(part == 1, value - high, high).astype(bf16)


def bands_kernel(kern_ref, gate, mats):
    mats[:, 0:480] = banded(kern_ref, BLOCK)
    mats[0:64, 512:800] = banded(kern_ref, 64)
    mats[0:32, 896:1088] = banded(kern_ref, 32)


def run_copies(pairs, sems):
    copies = [pltpu.make_async_copy(a, b, sems.at[i]) for i, (a, b) in enumerate(pairs)]
    for copy in copies:
        copy.start()
    for copy in copies:
        copy.wait()


def edges_kernel(scal, diag, fx, fy, film, src, *rest):
    *outs, sems = rest
    total = diag.shape[1]
    low, high = slice(0, COEF), slice(total - COEF, total)
    pairs = []
    for c in range(2):
        up_a, down_a, up_b, down_b = [ref.at[c] for ref in outs]
        for edge, a, b in ((low, up_a, up_b), (high, down_a, down_b)):
            for k, ref in enumerate((diag.at[c], fx.at[c], fy.at[c], src.at[c, STEPS - 1], film.at[c])):
                pairs.append((ref.at[edge], a.at[32 * k : 32 * k + 32]))
            for k in range(STEPS - 1):
                pairs.append((src.at[c, k, edge], b.at[32 * k : 32 * k + 32]))
        pairs.append((film.at[c, 32:56], up_b.at[96:120]))
    run_copies(pairs, sems)


def pack_kernel(scal, diag, fx, fy, film, src, left, right, low, high, sems):
    total, cols = diag.shape[1], diag.shape[2]
    refs = [diag, fx, fy, film] + [src.at[:, s] for s in (3, 2, 1, 0)]
    pairs = []
    for slot, ref in enumerate(refs):
        pairs.append((ref.at[:, :, 0:128], low.at[slot]))
        pairs.append((ref.at[:, :, cols - 128 : cols], high.at[slot]))
    run_copies(pairs, sems)
    rows = 32
    lane = lax.broadcasted_iota(jnp.int32, (rows, 128), 1)

    def chunk(i, carry):
        at = pl.ds(pl.multiple_of(i * rows, rows), rows)
        for c in range(2):
            first = jnp.zeros((rows, 128), f32)
            last = jnp.zeros((rows, 128), f32)
            for slot in range(SLOTS):
                place = COLS * slot
                here = (lane >= place) & (lane < place + COLS)
                a, b = low[slot, c, at, :], high[slot, c, at, :]
                first = jnp.where(here, pltpu.roll(a, place, 1) if place else a, first)
                last = jnp.where(here, pltpu.roll(b, (place + COLS) % 128, 1), last)
            left[c, at, :] = first
            right[c, at, :] = last
        return carry

    lax.fori_loop(0, total // rows, chunk, 0)


def ratio_of(scal, c):
    return 0.2 + 1.6 * scal[4 + c].astype(f32) / (NSRR - 1)


def main_kernel(scal, diag, fx, fy, film, src, coef, lam):
    rows = 16

    def chunk(i, carry):
        at = pl.ds(pl.multiple_of(i * rows, rows), rows)
        for c in range(2):
            w = 0.8 / diag[c, at, :]
            coef[c, 0, at, :] = w
            coef[c, 1, at, :] = w * fx[c, at, :]
            coef[c, 2, at, :] = w * fy[c, at, :]
            lam[c, at, :] = w * (src[c, STEPS - 1, at, :] + ratio_of(scal, c) * film[c, at, :])
        return carry

    lax.fori_loop(0, diag.shape[1] // rows, chunk, 0)


def side_kernel(scal, from_left, from_right, side, up, down):
    total = side.shape[2]
    rows = 32
    lane = lax.broadcasted_iota(jnp.int32, (rows, 128), 1)
    is_right = lane < COLS
    inside = (is_right & (scal[9] > 0)) | ((lane >= 128 - COLS) & (scal[8] > 0))

    def chunk(i, carry):
        at = pl.ds(pl.multiple_of(i * rows, rows), rows)
        for c in range(2):
            lo = from_left[c, at, :]
            hi = from_right[c, at, :]

            def halo(slot):
                place = COLS * slot
                right = pltpu.roll(hi, (128 - place) % 128, 1) if place else hi
                left = pltpu.roll(lo, (128 - COLS - place) % 128, 1)
                return jnp.where(inside, jnp.where(is_right, right, left), 0.0)

            w = jnp.where(inside, 0.8 / jnp.where(inside, halo(0), 1.0), 0.0)
            film = halo(3)
            side[c, 0, at, :] = w
            side[c, 1, at, :] = w * halo(1)
            side[c, 2, at, :] = w * halo(2)
            side[c, 3, at, :] = w * (halo(4) + ratio_of(scal, c) * film)
            side[c, 4, at, :] = halo(7)
            side[c, 5, at, :] = halo(6)
            side[c, 6, at, :] = halo(5)
            side[c, 7, at, :] = film
        return carry

    lax.fori_loop(0, total // rows, chunk, 0)

    def packed(c, first, at, count=4):
        result = jnp.zeros((at.stop - at.start, 128), f32)
        place = lax.broadcasted_iota(jnp.int32, result.shape, 1)
        for k in range(count):
            moved_in = pltpu.roll(side[c, first + k, at, :], 32 * k + COLS, 1)
            result = jnp.where((place >= 32 * k) & (place < 32 * k + 2 * COLS), moved_in, result)
        return result

    for c in range(2):
        for ref, at in ((up, slice(0, 32)), (down, slice(total - 32, total))):
            ref[c, 0:32, :] = packed(c, 0, at)
            ref[c, 32:64, :] = packed(c, 4, at)
            ref[c, 64:88, :] = packed(c, 7, slice(32, 56), 1)


def corner(ref, c, which, row, size):
    base, group = (64, 0) if which == 8 else (32 * (which // 4), which % 4)
    tile = ref[c, base + row : base + row + size, :]
    lane = lax.broadcasted_iota(jnp.int32, tile.shape, 1)
    tile = pltpu.roll(tile, 128 - COLS - 32 * group, 1)
    return jnp.where((lane < COLS) | (lane >= 128 - COLS), tile, 0.0)


def beside(main, extra):
    return jnp.concatenate([main, extra], axis=1)


def moved(stack, shift):
    size = stack.shape[0]
    return pltpu.roll(stack, size - shift, 0)[0 : size - 8]


def span(row, size):
    return slice(row, row + size) if isinstance(row, int) else pl.ds(pl.multiple_of(row, 8), size)


def chunks(first, last, body):
    count = (last - first) // 16

    def step(i, carry):
        body(first + pl.multiple_of(i * 16, 16))
        return carry

    lax.fori_loop(0, count, step, 0, unroll=2 if count % 2 == 0 else 1)


def split(value):
    high = value.astype(bf16)
    return high, (value - high.astype(f32)).astype(bf16)


def matrix(mats, size):
    if size == BLOCK:
        return mats[:, 0:480]
    return mats[0:64, 512:800] if size == 64 else mats[0:32, 896:1088]


def sweep(old, new, conv, mats, first, last, end, coefs, emit):
    lam, high, low = old
    start = first
    while start < last:
        size = BLOCK if last - start >= BLOCK else last - start
        near = slice(start - BAND, start + size + BAND)
        top = high[near, :]
        stack = jnp.concatenate([top, top, low[near, :]], axis=0)
        conv[0:size, :] = jnp.dot(matrix(mats, size), stack, preferred_element_type=f32)

        def chunk(row, start=start):
            w, wx, wy, wr = coefs(row)
            area = lam[span(row - 8, 32), :]
            mid = area[8:24]
            width = mid.shape[1]
            value = 0.2 * mid + wr
            value = value + wx * (area[7:23] + area[9:25])
            value = value + wy * (pltpu.roll(mid, 1, 1) + pltpu.roll(mid, width - 1, 1))
            value = value - w * conv[span(row - start, 16), :]
            emit(row, value, new)

        inner, outer = max(start, HALO), min(start + size, end)
        for row in range(start, min(start + size, HALO), 16):
            chunk(row)
        if inner < outer:
            chunks(inner, outer, chunk)
        for row in range(max(start, end), start + size, 16):
            chunk(row)
        start += size


def keep(row, value, new):
    lam, high, low = new
    at = span(row, 16)
    lam[at, :] = value
    high[at, :], low[at, :] = split(value)


def send_edges(lam_out, up, down):
    total = lam_out.shape[0]
    up[...] = lam_out[0:HALO, :]
    down[...] = lam_out[total - HALO : total, :]


def first_kernel(c, scal, mats, coef, side, lam_in, film, top, bot, top_corner, bot_corner, *rest):
    if c:
        grad_in, *rest = rest
    lam_out, up, down, grad, coef_top, coef_bot, la, ha, oa, lb, hb, ob, conv = rest
    total = lam_in.shape[1]
    cols = grad.shape[1]
    end = HALO + total
    top_ok = scal[6].astype(f32)
    low_ok = scal[7].astype(f32)
    r = ratio_of(scal, c)
    for ref, edge, ok, out, base in (
        (top, top_corner, top_ok, coef_top, HALO - COEF),
        (bot, bot_corner, low_ok, coef_bot, end),
    ):
        for row in range(0, COEF, 16):
            w = ok * (0.8 / ref[c, row : row + 16, :])
            fx = w * ref[c, 32 + row : 48 + row, :]
            fy = w * ref[c, 64 + row : 80 + row, :]
            lam = w * (ref[c, 96 + row : 112 + row, :] + r * ref[c, 128 + row : 144 + row, :])
            for k, main in enumerate((w, fx, fy)):
                out[k, row : row + 16, :] = beside(main, ok * corner(edge, c, k, row, 16))
            keep(base + row, beside(lam, ok * corner(edge, c, 3, row, 16)), (la, ha, oa))

    def load(row):
        at = span(row - HALO, 16)
        keep(row, beside(lam_in[c, at, :], side[c, 3, at, :]), (la, ha, oa))

    chunks(HALO, end, load)

    def coefs(row):
        if isinstance(row, int) and not HALO <= row < end:
            ref, at = (coef_top, row - HALO + COEF) if row < HALO else (coef_bot, row - end)
            return (*[ref[k, at : at + 16, :] for k in range(3)], la[row : row + 16, :])
        at = span(row - HALO, 16)
        parts = [beside(coef[c, k, at, :], side[c, k, at, :]) for k in range(3)]
        return (*parts, beside(lam_in[c, at, :], side[c, 3, at, :]))

    sweep((la, ha, oa), (lb, hb, ob), conv, mats, HALO - 16, end + 16, end, coefs, keep)

    def emit(row, value, new):
        at = span(row - HALO, 16)
        lam_out[at, :] = value
        term = value[:, 0:cols] * film[c, at, :]
        grad[at, :] = grad_in[at, :] + term if c else term

    sweep((lb, hb, ob), None, conv, mats, HALO, end, end, coefs, emit)
    send_edges(lam_out, up, down)


def step_kernel(
    step, c, scal, mats, coef, side, coef_top, coef_bot, top_corner, bot_corner,
    src, src_top, src_bot, lam_in, lam_top, lam_bot, film, grad_in, *rest,
):
    final = step == 0
    if step == 2:
        film_top, film_bot, *rest = rest
    if final:
        if c:
            _, _, *rest = rest
            lam_full, film_full, mine, other, film_now, lam_out, film_out, grad, *rest = rest
        else:
            lam_full, film_full, grad, film_now, lam_out, film_out, *rest = rest
        sems, *rest = rest
    else:
        lam_out, up, down, film_now, grad, *rest = rest
    la, ha, oa, lb, hb, ob, wr_ref, conv = rest
    total = lam_in.shape[0]
    cols = grad.shape[1]
    end = HALO + total
    top_ok = scal[6].astype(f32)
    low_ok = scal[7].astype(f32)
    reach = 8 * step
    r = ratio_of(scal, c)

    def old_film(row, size):
        if step < 2:
            return film[span(row - (HALO - COEF), size), :]
        if not isinstance(row, int):
            at = span(row - HALO, size)
            return beside(film[c, at, :], side[c, 7, at, :])
        parts = []
        for k in range(row, row + size, 8):
            if k < HALO:
                at = k - HALO + COEF
                part = top_ok * beside(film_top[c, 128 + at : 136 + at, :], corner(top_corner, c, 7, at, 8))
            elif k < end:
                at = slice(k - HALO, k - HALO + 8)
                part = beside(film[c, at, :], side[c, 7, at, :])
            elif k < end + 32:
                at = k - end
                part = low_ok * beside(film_bot[c, 128 + at : 136 + at, :], corner(bot_corner, c, 7, at, 8))
            else:
                at = k - end - 32
                part = low_ok * beside(src_bot[c, 96 + at : 104 + at, :], corner(bot_corner, c, 8, at, 8))
            parts.append(part)
        return jnp.concatenate(parts, axis=0)

    def coef_at(row, k):
        if isinstance(row, int) and not HALO <= row < end:
            ref, at = (coef_top, row - HALO + COEF) if row < HALO else (coef_bot, row - end)
            return ref[k, at : at + 16, :]
        at = span(row - HALO, 16)
        return beside(coef[c, k, at, :], side[c, k, at, :])

    def source(row):
        if isinstance(row, int) and not HALO <= row < end:
            ref, edge, at = (src_top, top_corner, row - HALO + COEF) if row < HALO else (src_bot, bot_corner, row - end)
            here = 32 * step + at
            return beside(ref[c, here : here + 16, :], corner(edge, c, 4 + step, at, 16))
        at = span(row - HALO, 16)
        return beside(src[c, step, at, :], side[c, 4 + step, at, :])

    shift = scal[step + 1]

    def begin(row):
        if isinstance(row, int) and row < HALO:
            lam = lam_top[row : row + 16, :] * top_ok
        elif isinstance(row, int) and row >= end:
            lam = lam_bot[row - end : row - end + 16, :] * low_ok
        else:
            lam = lam_in[span(row - HALO, 16), :]
        keep(row, lam, (la, ha, oa))
        height = 16
        if isinstance(row, int):
            if row < HALO - COEF or row >= end + COEF + reach:
                return
            height = min(16, end + COEF + reach - row)
        now = moved(old_film(row, height + 8), shift) + r * lam[0:height]
        at = row - HALO + COEF
        film_now[span(at, height), :] = now
        if not isinstance(row, int) or row < end + COEF:
            wr_ref[span(at, 16), :] = coef_at(row, 0) * (source(row) + r * now)

    for row in range(0, HALO, 16):
        begin(row)
    chunks(HALO, end - 32, begin)
    for row in range(end - 32, end + HALO, 16):
        begin(row)

    def coefs(row):
        return coef_at(row, 0), coef_at(row, 1), coef_at(row, 2), wr_ref[span(row - HALO + COEF, 16), :]

    a, b = (la, ha, oa), (lb, hb, ob)
    sweep(a, b, conv, mats, HALO - 32, end + 32, end, coefs, keep)
    sweep(b, a, conv, mats, HALO - 16, end + 16, end, coefs, keep)

    def emit(row, value, new):
        at = span(row - HALO, 16)
        here = row - HALO + COEF
        grad[at, :] = grad_in[at, :] + value[:, 0:cols] * film_now[span(here, 16), 0:cols]
        if final:
            lam_out[at, :] = value[:, 0:cols]
            film_out[at, :] = moved(film_now[span(here, 24), 0:cols], scal[0]) + r * value[:, 0:cols]
        else:
            lam_out[at, :] = value

    sweep(a, None, conv, mats, HALO, end, end, coefs, emit)
    if final:
        run_copies([(lam_out, lam_full.at[c]), (film_out, film_full.at[c])], sems)
        if c:
            half = total // 2
            first = pl.multiple_of(scal[10] * half, half)
            mine[...] = grad[pl.ds(first, half), :]
            other[...] = grad[pl.ds(pl.multiple_of(half - first, half), half), :]
    else:
        send_edges(lam_out, up, down)


VM = pl.BlockSpec(memory_space=pltpu.VMEM)
SM = pl.BlockSpec(memory_space=pltpu.SMEM)
HB = pl.BlockSpec(memory_space=pltpu.HBM)


def call(body, smem, vmem, outs, scratch=(), flops=0, name=None, space=VM, limit=12, hbm_outs=0, hbm_ins=0):
    moved_bytes = sum(v.size * 4 for v in vmem) + sum(4 * functools.reduce(lambda a, b: a * b, o.shape) for o in outs)
    return pl.pallas_call(
        body,
        out_shape=tuple(outs),
        in_specs=[SM] * len(smem) + [space] * (len(vmem) - hbm_ins) + [HB] * hbm_ins,
        out_specs=tuple([HB] * hbm_outs + [VM] * (len(outs) - hbm_outs)),
        input_output_aliases={len(smem) + len(vmem) - hbm_ins + i: i for i in range(hbm_ins)},
        scratch_shapes=list(scratch),
        cost_estimate=pl.CostEstimate(flops=flops, bytes_accessed=moved_bytes, transcendentals=0),
        compiler_params=pltpu.CompilerParams(vmem_limit_bytes=limit << 20),
        name=name,
    )(*smem, *[pltpu.with_memory_space_constraint(v, pltpu.HBM) for v in vmem] if space is HB else vmem)


def ring(axis, step):
    count = lax.axis_size(axis)
    return [(i, (i + step) % count) for i in range(count)]


def both_ways(up, down, axis):
    from_high = lax.ppermute(up, axis, ring(axis, -1))
    from_low = lax.ppermute(down, axis, ring(axis, 1))
    return from_low, from_high


def after(values, gate):
    return lax.optimization_barrier((tuple(values), tuple(gate)))[0]


def case_sum(mine, other, core):
    swap_core = [(i, i ^ 1) for i in range(4)]
    swap_chip = [(i, i ^ 2) for i in range(4)]
    mine = mine + lax.ppermute(other, "case", swap_core)
    mine = mine + lax.ppermute(mine, "case", swap_chip)
    other = lax.ppermute(mine, "case", swap_core)
    return jnp.where(
        core == 0, jnp.concatenate([mine, other], axis=0), jnp.concatenate([other, mine], axis=0)
    )


def on_device(ratio_index, shifts, kernel, diagonal, flow_x, flow_y, pres_source, rough_adjoint):
    cases, total, cols = diagonal.shape
    wide = cols + 128
    roll, trans = lax.axis_index("roll"), lax.axis_index("trans")
    core = lax.axis_index("case") % 2
    scal = jnp.concatenate(
        [
            shifts,
            ratio_index,
            jnp.stack(
                [
                    (roll > 0).astype(jnp.int32),
                    (roll < lax.axis_size("roll") - 1).astype(jnp.int32),
                    (trans > 0).astype(jnp.int32),
                    (trans < lax.axis_size("trans") - 1).astype(jnp.int32),
                    core,
                ]
            ),
        ]
    )

    def shape(*dims, dtype=f32):
        return jax.ShapeDtypeStruct(dims, dtype)

    raw = (diagonal, flow_x, flow_y, rough_adjoint, pres_source)
    edges = call(
        edges_kernel,
        (scal,),
        raw,
        [shape(cases, rows, cols) for rows in (160, 160, 120, 96)],
        [pltpu.SemaphoreType.DMA((34,))],
        name="edges",
        space=HB,
    )
    near = both_ways(edges[0], edges[1], "roll")
    (scal,) = after((scal,), (edges[0],))
    tile = pltpu.VMEM((SLOTS, cases, total, 128), f32)
    left, right = call(
        pack_kernel,
        (scal,),
        raw,
        [shape(cases, total, 128)] * 2,
        [tile, tile, pltpu.SemaphoreType.DMA((2 * SLOTS,))],
        name="pack",
        space=HB,
    )
    from_left, from_right = both_ways(left, right, "trans")
    (mats,) = call(bands_kernel, (kernel,), (left,), [shape(BLOCK, 1152, dtype=bf16)], name="bands")
    coef, lam = call(
        main_kernel,
        (scal,),
        raw,
        [shape(cases, 3, total, cols), shape(cases, total, cols)],
        name="main",
    )
    from_left, from_right = after((from_left, from_right), (coef, mats))
    side, up, down = call(
        side_kernel,
        (scal,),
        (from_left, from_right),
        [shape(cases, 8, total, 128), shape(cases, 88, 128), shape(cases, 88, 128)],
        name="side",
    )
    top_corner, bot_corner = both_ways(up, down, "roll")
    rows = total + 2 * HALO
    fields = [pltpu.VMEM((rows, wide), f32), pltpu.VMEM((rows, wide), bf16), pltpu.VMEM((rows, wide), bf16)]
    conv = pltpu.VMEM((BLOCK, wide), f32)
    work = [*fields, *fields, pltpu.VMEM((total + 2 * COEF, wide), f32), conv]
    state = [shape(total, wide), shape(HALO, wide), shape(HALO, wide)]
    halo = shape(3, COEF, wide)
    block = shape(total, cols)
    grad = None
    lams, ends, coefs, films = [None] * 2, [None] * 2, [None] * 2, [rough_adjoint] * 2
    later = both_ways(*after(edges[2:4], near), "roll")
    for c in range(2):
        lams[c], up, down, grad, *coefs[c] = call(
            functools.partial(first_kernel, c),
            (scal,),
            (mats, coef, side, lam, rough_adjoint, *near, top_corner, bot_corner, *([grad] if c else [])),
            [*state, block, halo, halo],
            [*fields, *fields, conv],
            flops=1 << 30,
            name="first" + str(c),
        )
        ends[c] = both_ways(up, down, "roll")
    out = ()
    for step in range(STEPS - 2, -1, -1):
        for c in range(2):
            film = shape(total + 2 * COEF + 8 * step, wide)
            scratch = work
            hbm_outs = hbm_ins = 0
            if step:
                outs = [*state, film, block]
            else:
                full = shape(cases, total, cols)
                half = shape(total // 2, cols)
                outs = [full, full, half, half] if c else [full, full, block]
                kept = [film, block, block] + ([block] if c else [])
                scratch = [*[pltpu.VMEM(k.shape, f32) for k in kept], pltpu.SemaphoreType.DMA((2,)), *work]
                hbm_outs, hbm_ins = 2, 2 * c
            more = near if step == 2 else out
            result = call(
                functools.partial(step_kernel, step, c),
                (scal,),
                (
                    mats, coef, side, *coefs[c], top_corner, bot_corner, pres_source, *later,
                    lams[c], *ends[c], films[c], grad, *more,
                ),
                outs,
                scratch,
                flops=3 << 29,
                name="step" + str(step) + "case" + str(c),
                hbm_outs=hbm_outs,
                hbm_ins=hbm_ins,
            )
            if step:
                lams[c], up, down, films[c], grad = result
                ends[c] = both_ways(up, down, "roll")
            elif c == 0:
                *out, grad = result
            else:
                lam, film, mine, other = result
    return lam, film, case_sum(mine, other, core)


def solution(mesh):
    block = P("case", "roll", "trans")
    in_specs = (P("case"), P(), P(), block, block, block, P("case", None, "roll", "trans"), block)
    out_specs = (block, block, P("roll", "trans"))
    return jax.shard_map(on_device, mesh=mesh, in_specs=in_specs, out_specs=out_specs, check_vma=False)
```

time: 133 us -> 160 us (1.20)
  Pallas kernels: 35.6 us -> 57 us
  starting transfers between devices: 48.6 us -> 64.1 us
  waiting for transfers between devices: 46.3 us -> 36.5 us
    pallas_call x9 -> x13, Pallas kernels: 35.6 us -> 57 us  [call(): pl.pallas_call(body, out_shape=tuple(outs), in_specs=[SM] * len(smem) + [...]
    ppermute x8 -> x10, waiting for transfers between devices: 20.1 us -> 3.8 us  [both_ways(): from_high = lax.ppermute(up, axis, ring(axis, -1))]
    ppermute x8 -> x10, starting transfers between devices: 39.8 us -> 49.5 us  [both_ways(): from_high = lax.ppermute(up, axis, ring(axis, -1))]
    ppermute x8 -> x10, waiting for transfers between devices: 17.6 us -> 23.1 us  [both_ways(): from_low = lax.ppermute(down, axis, ring(axis, 1))]
    ppermute x8 -> x10, starting transfers between devices: 5.68 us -> 9.2 us  [both_ways(): from_low = lax.ppermute(down, axis, ring(axis, 1))]
    ppermute x1, starting transfers between devices: 0.5 us -> 3.67 us  [case_sum(): mine = mine + lax.ppermute(other, 'case', swap_core)]
  transfers between devices with their start and end apart: 19 -> 23, of which waited for: 12 -> 7; matrix products, arithmetic and copies ran while one was open for 0% -> 0% of each run, Pallas kernels for 12% -> 30%
where the time goes in v3:
time: 160 us
  starting transfers between devices  64.1 us (40%)
  Pallas kernels  57 us (36%)
  waiting for transfers between devices  36.5 us (23%)
    pallas_call x13, Pallas kernels, call(): pl.pallas_call(body, out_shape=tuple(outs), in_specs=[SM] * len(smem) + [...  57 us
    ppermute x10, starting transfers between devices, both_ways(): from_high = lax.ppermute(up, axis, ring(axis, -1))  49.5 us
    ppermute x10, waiting for transfers between devices, both_ways(): from_low = lax.ppermute(down, axis, ring(axis, 1))  23.1 us
    ppermute x10, starting transfers between devices, both_ways(): from_low = lax.ppermute(down, axis, ring(axis, 1))  9.2 us
    ppermute x1, waiting for transfers between devices, case_sum(): mine = mine + lax.ppermute(mine, 'case', swap_chip)  7.21 us
    ppermute x10, waiting for transfers between devices, both_ways(): from_high = lax.ppermute(up, axis, ring(axis, -1))  3.8 us
    ppermute x1, starting transfers between devices, case_sum(): mine = mine + lax.ppermute(other, 'case', swap_core)  3.67 us
  transfers between devices with their start and end apart: 23, of which 7 were waited for; matrix products, arithmetic and copies ran while one was open for 0% of the time, Pallas kernels for 30%

profile of v3, /device:TPU:1, one launch (start us, length us, event | category | flops | bytes accessed | tf_op | source)
XLA Modules:
  0.0 160.1 jit_solution(1648548976025247395)
XLA Ops:
  3.8 3.7 %collective-permute-start.2 = (f32[2,160,512]{2,1,0:T(8,128)S(1)}, f32[2,160,512]{2,1,0:T(8,128)S(1)}, u32[]{:S(2)}, u32[]{:S(2)}) collective-permute-start(f32[2,160,512]{2,1,0:T(8,128)S(1)} %get-tuple-element.67), channel_id=1, source_target_pairs={{0,16},{16,32},{32,48},{48,64},{64,80},{80,96},{96,112},{112,128},... | collective-permute-start | bytes 1966088 | tf_op jit(solution)/shard_map/ppermute | solution.py:446
  7.5 5.4 %collective-permute-start.3 = (f32[2,160,512]{2,1,0:T(8,128)S(1)}, f32[2,160,512]{2,1,0:T(8,128)S(1)}, u32[]{:S(2)}, u32[]{:S(2)}) collective-permute-start(f32[2,160,512]{2,1,0:T(8,128)S(1)} %get-tuple-element.58), channel_id=1, source_target_pairs={{0,240},{16,0},{32,16},{48,32},{64,48},{80,64},{96,80},{112,96},{1... | collective-permute-start | bytes 1966088 | tf_op jit(solution)/shard_map/ppermute | solution.py:445
  12.9 4.4 %pack.1 = (f32[2,256,128]{2,1,0:T(8,128)S(1)}, f32[2,256,128]{2,1,0:T(8,128)S(1)}) custom-call(s32[11]{0:T(128)S(1)} %concatenate.9.scal, f32[2,256,512]{2,1,0:T(8,128)} %diag.5, f32[2,256,512]{2,1,0:T(8,128)} %fx.5, f32[2,256,512]{2,1,0:T(8,128)} %fy.5, f32[2,256,512]{2,1,0:T(8,128)} %film.13, f32[2,4,256,512]{3,2,1,0:T(8,128)} %src.17), custom_call_target="tpu_custom_call" | custom-call | bytes 8912896 | tf_op jit(solution)/shard_map/pack/pallas_call | solution.py:426
  20.3 14.6 %collective-permute-done.2.top.rest_0_ = f32[2,160,512]{2,1,0:T(8,128)S(1)} collective-permute-done((f32[2,160,512]{2,1,0:T(8,128)S(1)}, f32[2,160,512]{2,1,0:T(8,128)S(1)}, u32[]{:S(2)}, u32[]{:S(2)}) %collective-permute-start.2) | collective-permute-done | bytes 655392 | tf_op jit(solution)/shard_map/ppermute | solution.py:446
  38.4 5.5 %collective-permute-start.7 = (f32[2,120,512]{2,1,0:T(8,128)S(1)}, f32[2,120,512]{2,1,0:T(8,128)S(1)}, u32[]{:S(2)}, u32[]{:S(2)}) collective-permute-start(f32[2,120,512]{2,1,0:T(8,128)S(1)} %get-tuple-element.76), channel_id=1, source_target_pairs={{0,240},{16,0},{32,16},{48,32},{64,48},{80,64},{96,80},{112,96},{1... | collective-permute-start | bytes 1474568 | tf_op jit(solution)/shard_map/ppermute | solution.py:445
  49.1 5.1 %collective-permute-start.5 = (f32[2,88,128]{2,1,0:T(8,128)S(1)}, f32[2,88,128]{2,1,0:T(8,128)S(1)}, u32[]{:S(2)}, u32[]{:S(2)}) collective-permute-start(f32[2,88,128]{2,1,0:T(8,128)S(1)} %get-tuple-element.69), channel_id=1, source_target_pairs={{0,240},{16,0},{32,16},{48,32},{64,48},{80,64},{96,80},{112,96},{1... | collective-permute-start | bytes 270344 | tf_op jit(solution)/shard_map/ppermute | solution.py:445
  54.3 8.5 %collective-permute-done.4.top_corner = f32[2,88,128]{2,1,0:T(8,128)S(1)} collective-permute-done((f32[2,88,128]{2,1,0:T(8,128)S(1)}, f32[2,88,128]{2,1,0:T(8,128)S(1)}, u32[]{:S(2)}, u32[]{:S(2)}) %collective-permute-start.4) | collective-permute-done | bytes 90144 | tf_op jit(solution)/shard_map/ppermute | solution.py:446
  63.0 4.1 %first0.1 = (f32[256,640]{1,0:T(8,128)S(1)}, f32[48,640]{1,0:T(8,128)S(1)}, f32[48,640]{1,0:T(8,128)S(1)}, f32[256,512]{1,0:T(8,128)S(1)}, f32[3,32,640]{2,1,0:T(8,128)S(1)}, /*index=5*/f32[3,32,640]{2,1,0:T(8,128)S(1)}) custom-call(s32[11]{0:T(128)S(1)} %concatenate.9.scal, bf16[128,1152]{1,0:T(8,128)(2,1)S(1)} %bands.1.mats, ...), custom_call_target="tpu_custom_call" | custom-call | flops 1073741824 | bytes 11337728 | tf_op jit(solution)/shard_map/first0/pallas_call | solution.py:426
  67.1 3.5 %collective-permute-start.10 = (f32[48,640]{1,0:T(8,128)S(1)}, f32[48,640]{1,0:T(8,128)S(1)}, u32[]{:S(2)}, u32[]{:S(2)}) collective-permute-start(f32[48,640]{1,0:T(8,128)S(1)} %get-tuple-element.83), channel_id=1, source_target_pairs={{0,16},{16,32},{32,48},{48,64},{64,80},{80,96},{96,112},{112,128},... | collective-permute-start | bytes 368648 | tf_op jit(solution)/shard_map/ppermute | solution.py:446
  70.6 6.6 %collective-permute-start.11 = (f32[48,640]{1,0:T(8,128)S(1)}, f32[48,640]{1,0:T(8,128)S(1)}, u32[]{:S(2)}, u32[]{:S(2)}) collective-permute-start(f32[48,640]{1,0:T(8,128)S(1)} %get-tuple-element.84), channel_id=1, source_target_pairs={{0,240},{16,0},{32,16},{48,32},{64,48},{80,64},{96,80},{112,96},{1... | collective-permute-start | bytes 368648 | tf_op jit(solution)/shard_map/ppermute | solution.py:445
  77.2 4.1 %first1.1 = (f32[256,640]{1,0:T(8,128)S(1)}, f32[48,640]{1,0:T(8,128)S(1)}, f32[48,640]{1,0:T(8,128)S(1)}, f32[256,512]{1,0:T(8,128)S(1)}, f32[3,32,640]{2,1,0:T(8,128)S(1)}, /*index=5*/f32[3,32,640]{2,1,0:T(8,128)S(1)}) custom-call(s32[11]{0:T(128)S(1)} %concatenate.9.scal, bf16[128,1152]{1,0:T(8,128)(2,1)S(1)} %bands.1.mats, ...), custom_call_target="tpu_custom_call" | custom-call | flops 1073741824 | bytes 11862016 | tf_op jit(solution)/shard_map/first1/pallas_call | solution.py:426
  81.6 5.1 %collective-permute-start.9 = (f32[48,640]{1,0:T(8,128)S(1)}, f32[48,640]{1,0:T(8,128)S(1)}, u32[]{:S(2)}, u32[]{:S(2)}) collective-permute-start(f32[48,640]{1,0:T(8,128)S(1)} %get-tuple-element.79), channel_id=1, source_target_pairs={{0,240},{16,0},{32,16},{48,32},{64,48},{80,64},{96,80},{112,96},{1... | collective-permute-start | bytes 368648 | tf_op jit(solution)/shard_map/ppermute | solution.py:445
  86.7 5.8 %step2case0.1 = (f32[256,640]{1,0:T(8,128)S(1)}, f32[48,640]{1,0:T(8,128)S(1)}, f32[48,640]{1,0:T(8,128)S(1)}, f32[336,640]{1,0:T(8,128)S(1)}, f32[256,512]{1,0:T(8,128)S(1)}) custom-call(s32[11]{0:T(128)S(1)} %concatenate.9.scal, bf16[128,1152]{1,0:T(8,128)(2,1)S(1)} %bands.1.mats, f32[2,3,256,512]{3,2,1,0:T(8,128)S(1)} %get-tuple-element.61.coef, ...), custom_call_target="tpu_custom_call" | custom-call | flops 1610612736 | bytes 17653760 | tf_op jit(solution)/shard_map/step2case0/pallas_call | solution.py:426
  92.6 5.1 %collective-permute-start.15 = (f32[48,640]{1,0:T(8,128)S(1)}, f32[48,640]{1,0:T(8,128)S(1)}, u32[]{:S(2)}, u32[]{:S(2)}) collective-permute-start(f32[48,640]{1,0:T(8,128)S(1)} %get-tuple-element.93), channel_id=1, source_target_pairs={{0,240},{16,0},{32,16},{48,32},{64,48},{80,64},{96,80},{112,96},{1... | collective-permute-start | bytes 368648 | tf_op jit(solution)/shard_map/ppermute | solution.py:445
  97.7 5.8 %step2case1.1 = (f32[256,640]{1,0:T(8,128)S(1)}, f32[48,640]{1,0:T(8,128)S(1)}, f32[48,640]{1,0:T(8,128)S(1)}, f32[336,640]{1,0:T(8,128)S(1)}, f32[256,512]{1,0:T(8,128)S(1)}) custom-call(s32[11]{0:T(128)S(1)} %concatenate.9.scal, bf16[128,1152]{1,0:T(8,128)(2,1)S(1)} %bands.1.mats, f32[2,3,256,512]{3,2,1,0:T(8,128)S(1)} %get-tuple-element.61.coef, ...), custom_call_target="tpu_custom_call" | custom-call | flops 1610612736 | bytes 17653760 | tf_op jit(solution)/shard_map/step2case1/pallas_call | solution.py:426
  103.6 5.1 %collective-permute-start.13 = (f32[48,640]{1,0:T(8,128)S(1)}, f32[48,640]{1,0:T(8,128)S(1)}, u32[]{:S(2)}, u32[]{:S(2)}) collective-permute-start(f32[48,640]{1,0:T(8,128)S(1)} %get-tuple-element.89), channel_id=1, source_target_pairs={{0,240},{16,0},{32,16},{48,32},{64,48},{80,64},{96,80},{112,96},{1... | collective-permute-start | bytes 368648 | tf_op jit(solution)/shard_map/ppermute | solution.py:445
  108.7 5.8 %step1case0.1 = (f32[256,640]{1,0:T(8,128)S(1)}, f32[48,640]{1,0:T(8,128)S(1)}, f32[48,640]{1,0:T(8,128)S(1)}, f32[328,640]{1,0:T(8,128)S(1)}, f32[256,512]{1,0:T(8,128)S(1)}) custom-call(s32[11]{0:T(128)S(1)} %concatenate.9.scal, bf16[128,1152]{1,0:T(8,128)(2,1)S(1)} %bands.1.mats, f32[2,3,256,512]{3,2,1,0:T(8,128)S(1)} %get-tuple-element.61.coef, ...), custom_call_target="tpu_custom_call" | custom-call | flops 1610612736 | bytes 16134144 | tf_op jit(solution)/shard_map/step1case0/pallas_call | solution.py:426
  114.6 5.1 %collective-permute-start.19 = (f32[48,640]{1,0:T(8,128)S(1)}, f32[48,640]{1,0:T(8,128)S(1)}, u32[]{:S(2)}, u32[]{:S(2)}) collective-permute-start(f32[48,640]{1,0:T(8,128)S(1)} %get-tuple-element.103), channel_id=1, source_target_pairs={{0,240},{16,0},{32,16},{48,32},{64,48},{80,64},{96,80},{112,96},{1... | collective-permute-start | bytes 368648 | tf_op jit(solution)/shard_map/ppermute | solution.py:445
  119.7 5.8 %step1case1.1 = (f32[256,640]{1,0:T(8,128)S(1)}, f32[48,640]{1,0:T(8,128)S(1)}, f32[48,640]{1,0:T(8,128)S(1)}, f32[328,640]{1,0:T(8,128)S(1)}, f32[256,512]{1,0:T(8,128)S(1)}) custom-call(s32[11]{0:T(128)S(1)} %concatenate.9.scal, bf16[128,1152]{1,0:T(8,128)(2,1)S(1)} %bands.1.mats, f32[2,3,256,512]{3,2,1,0:T(8,128)S(1)} %get-tuple-element.61.coef, ...), custom_call_target="tpu_custom_call" | custom-call | flops 1610612736 | bytes 16134144 | tf_op jit(solution)/shard_map/step1case1/pallas_call | solution.py:426
  125.6 5.1 %collective-permute-start.17 = (f32[48,640]{1,0:T(8,128)S(1)}, f32[48,640]{1,0:T(8,128)S(1)}, u32[]{:S(2)}, u32[]{:S(2)}) collective-permute-start(f32[48,640]{1,0:T(8,128)S(1)} %get-tuple-element.99), channel_id=1, source_target_pairs={{0,240},{16,0},{32,16},{48,32},{64,48},{80,64},{96,80},{112,96},{1... | collective-permute-start | bytes 368648 | tf_op jit(solution)/shard_map/ppermute | solution.py:445
  130.7 6.8 %step0case0.1 = (f32[2,256,512]{2,1,0:T(8,128)}, f32[2,256,512]{2,1,0:T(8,128)}, f32[256,512]{1,0:T(8,128)S(1)}) custom-call(s32[11]{0:T(128)S(1)} %concatenate.9.scal, bf16[128,1152]{1,0:T(8,128)(2,1)S(1)} %bands.1.mats, f32[2,3,256,512]{3,2,1,0:T(8,128)S(1)} %get-tuple-element.61.coef, f32[2,8,256,128]{3,2,1,0:T(8,128)S(1)} %get-tuple-element.65.side, ...), custom_call_target="tpu_custom_call" | custom-call | flops 1610612736 | bytes 16470016 | tf_op jit(solution)/shard_map/step0case0/pallas_call | solution.py:426
  137.5 6.8 %step0case1.1 = (f32[2,256,512]{2,1,0:T(8,128)}, f32[2,256,512]{2,1,0:T(8,128)}, f32[128,512]{1,0:T(8,128)S(1)}, f32[128,512]{1,0:T(8,128)S(1)}) custom-call(s32[11]{0:T(128)S(1)} %concatenate.9.scal, bf16[128,1152]{1,0:T(8,128)(2,1)S(1)} %bands.1.mats, ...), custom_call_target="tpu_custom_call", output_to_operand_aliasing={{0}: (16, {}), {1}: (17, {})} | custom-call | flops 1610612736 | bytes 18567168 | tf_op jit(solution)/shard_map/step0case1/pallas_call | solution.py:426
  144.3 3.7 %collective-permute-start.20 = (f32[128,512]{1,0:T(8,128)S(1)}, f32[128,512]{1,0:T(8,128)S(1)}, u32[]{:S(2)}, u32[]{:S(2)}) collective-permute-start(f32[128,512]{1,0:T(8,128)S(1)} %get-tuple-element.112), channel_id=1, source_target_pairs={{0,1},{1,0},{2,3},{3,2},{4,5},{5,4},{6,7},{7,6},{8,9},{9,8},{10,11... | collective-permute-start | bytes 786440 | tf_op jit(solution)/shard_map/ppermute | solution.py:457
  149.6 7.2 %collective-permute-done.21 = f32[128,512]{1,0:T(8,128)S(1)} collective-permute-done((f32[128,512]{1,0:T(8,128)S(1)}, f32[128,512]{1,0:T(8,128)S(1)}, u32[]{:S(2)}, u32[]{:S(2)}) %collective-permute-start.21) | collective-permute-done | bytes 262176 | tf_op jit(solution)/shard_map/ppermute | solution.py:458
  (51 shorter events, 20.6 us)
Async XLA Ops:
  3.8 31.1 %collective-permute-start.2 = (f32[2,160,512]{2,1,0:T(8,128)S(1)}, f32[2,160,512]{2,1,0:T(8,128)S(1)}, u32[]{:S(2)}, u32[]{:S(2)}) collective-permute-start(f32[2,160,512]{2,1,0:T(8,128)S(1)} %get-tuple-element.67), channel_id=1, source_target_pairs={{0,16},{16,32},{32,48},{48,64},{64,80},{80,96},{96,112},{112,128},... | collective-permute-start | bytes 1966088 | tf_op jit(solution)/shard_map/ppermute | solution.py:446
  7.5 36.5 %copy-start.4 = (f32[2,256,512]{2,1,0:T(8,128)S(1)}, f32[2,256,512]{2,1,0:T(8,128)}, u32[]{:S(2)}) copy-start(f32[2,256,512]{2,1,0:T(8,128)} %fy.5) | copy-start | bytes 3145732
  7.5 30.9 %collective-permute-start.3 = (f32[2,160,512]{2,1,0:T(8,128)S(1)}, f32[2,160,512]{2,1,0:T(8,128)S(1)}, u32[]{:S(2)}, u32[]{:S(2)}) collective-permute-start(f32[2,160,512]{2,1,0:T(8,128)S(1)} %get-tuple-element.58), channel_id=1, source_target_pairs={{0,240},{16,0},{32,16},{48,32},{64,48},{80,64},{96,80},{112,96},{1... | collective-permute-start | bytes 1966088 | tf_op jit(solution)/shard_map/ppermute | solution.py:445
  17.4 29.4 %collective-permute-start = (f32[2,256,128]{2,1,0:T(8,128)S(1)}, f32[2,256,128]{2,1,0:T(8,128)S(1)}, u32[]{:S(2)}, u32[]{:S(2)}) collective-permute-start(f32[2,256,128]{2,1,0:T(8,128)S(1)} %get-tuple-element.62), channel_id=1, source_target_pairs={{0,4},{4,8},{8,12},{12,0},{1,5},{5,9},{9,13},{13,1},{2,6},{6,10},{... | collective-permute-start | bytes 786440 | tf_op jit(solution)/shard_map/ppermute | solution.py:446
  18.7 28.0 %collective-permute-start.1 = (f32[2,256,128]{2,1,0:T(8,128)S(1)}, f32[2,256,128]{2,1,0:T(8,128)S(1)}, u32[]{:S(2)}, u32[]{:S(2)}) collective-permute-start(f32[2,256,128]{2,1,0:T(8,128)S(1)} %get-tuple-element.60.gate), channel_id=1, source_target_pairs={{0,12},{4,0},{8,4},{12,8},{1,13},{5,1},{9,5},{13,9},{2,14},{6,2},{... | collective-permute-start | bytes 786440 | tf_op jit(solution)/shard_map/ppermute | solution.py:445
  38.4 48.3 %collective-permute-start.7 = (f32[2,120,512]{2,1,0:T(8,128)S(1)}, f32[2,120,512]{2,1,0:T(8,128)S(1)}, u32[]{:S(2)}, u32[]{:S(2)}) collective-permute-start(f32[2,120,512]{2,1,0:T(8,128)S(1)} %get-tuple-element.76), channel_id=1, source_target_pairs={{0,240},{16,0},{32,16},{48,32},{64,48},{80,64},{96,80},{112,96},{1... | collective-permute-start | bytes 1474568 | tf_op jit(solution)/shard_map/ppermute | solution.py:445
  43.9 42.8 %collective-permute-start.6 = (f32[2,96,512]{2,1,0:T(8,128)S(1)}, f32[2,96,512]{2,1,0:T(8,128)S(1)}, u32[]{:S(2)}, u32[]{:S(2)}) collective-permute-start(f32[2,96,512]{2,1,0:T(8,128)S(1)} %get-tuple-element.75), channel_id=1, source_target_pairs={{0,16},{16,32},{32,48},{48,64},{64,80},{80,96},{96,112},{112,128},... | collective-permute-start | bytes 1179656 | tf_op jit(solution)/shard_map/ppermute | solution.py:446
  49.1 13.7 %collective-permute-start.4 = (f32[2,88,128]{2,1,0:T(8,128)S(1)}, f32[2,88,128]{2,1,0:T(8,128)S(1)}, u32[]{:S(2)}, u32[]{:S(2)}) collective-permute-start(f32[2,88,128]{2,1,0:T(8,128)S(1)} %get-tuple-element.68), channel_id=1, source_target_pairs={{0,16},{16,32},{32,48},{48,64},{64,80},{80,96},{96,112},{112,128},... | collective-permute-start | bytes 270344 | tf_op jit(solution)/shard_map/ppermute | solution.py:446
  49.1 13.9 %collective-permute-start.5 = (f32[2,88,128]{2,1,0:T(8,128)S(1)}, f32[2,88,128]{2,1,0:T(8,128)S(1)}, u32[]{:S(2)}, u32[]{:S(2)}) collective-permute-start(f32[2,88,128]{2,1,0:T(8,128)S(1)} %get-tuple-element.69), channel_id=1, source_target_pairs={{0,240},{16,0},{32,16},{48,32},{64,48},{80,64},{96,80},{112,96},{1... | collective-permute-start | bytes 270344 | tf_op jit(solution)/shard_map/ppermute | solution.py:445
  67.1 14.5 %collective-permute-start.10 = (f32[48,640]{1,0:T(8,128)S(1)}, f32[48,640]{1,0:T(8,128)S(1)}, u32[]{:S(2)}, u32[]{:S(2)}) collective-permute-start(f32[48,640]{1,0:T(8,128)S(1)} %get-tuple-element.83), channel_id=1, source_target_pairs={{0,16},{16,32},{32,48},{48,64},{64,80},{80,96},{96,112},{112,128},... | collective-permute-start | bytes 368648 | tf_op jit(solution)/shard_map/ppermute | solution.py:446
  70.6 16.1 %collective-permute-start.11 = (f32[48,640]{1,0:T(8,128)S(1)}, f32[48,640]{1,0:T(8,128)S(1)}, u32[]{:S(2)}, u32[]{:S(2)}) collective-permute-start(f32[48,640]{1,0:T(8,128)S(1)} %get-tuple-element.84), channel_id=1, source_target_pairs={{0,240},{16,0},{32,16},{48,32},{64,48},{80,64},{96,80},{112,96},{1... | collective-permute-start | bytes 368648 | tf_op jit(solution)/shard_map/ppermute | solution.py:445
  81.3 16.3 %collective-permute-start.8 = (f32[48,640]{1,0:T(8,128)S(1)}, f32[48,640]{1,0:T(8,128)S(1)}, u32[]{:S(2)}, u32[]{:S(2)}) collective-permute-start(f32[48,640]{1,0:T(8,128)S(1)} %get-tuple-element.78), channel_id=1, source_target_pairs={{0,16},{16,32},{32,48},{48,64},{64,80},{80,96},{96,112},{112,128},... | collective-permute-start | bytes 368648 | tf_op jit(solution)/shard_map/ppermute | solution.py:446
  81.6 16.1 %collective-permute-start.9 = (f32[48,640]{1,0:T(8,128)S(1)}, f32[48,640]{1,0:T(8,128)S(1)}, u32[]{:S(2)}, u32[]{:S(2)}) collective-permute-start(f32[48,640]{1,0:T(8,128)S(1)} %get-tuple-element.79), channel_id=1, source_target_pairs={{0,240},{16,0},{32,16},{48,32},{64,48},{80,64},{96,80},{112,96},{1... | collective-permute-start | bytes 368648 | tf_op jit(solution)/shard_map/ppermute | solution.py:445
  92.5 16.1 %collective-permute-start.14 = (f32[48,640]{1,0:T(8,128)S(1)}, f32[48,640]{1,0:T(8,128)S(1)}, u32[]{:S(2)}, u32[]{:S(2)}) collective-permute-start(f32[48,640]{1,0:T(8,128)S(1)} %get-tuple-element.92), channel_id=1, source_target_pairs={{0,16},{16,32},{32,48},{48,64},{64,80},{80,96},{96,112},{112,128},... | collective-permute-start | bytes 368648 | tf_op jit(solution)/shard_map/ppermute | solution.py:446
  92.6 16.1 %collective-permute-start.15 = (f32[48,640]{1,0:T(8,128)S(1)}, f32[48,640]{1,0:T(8,128)S(1)}, u32[]{:S(2)}, u32[]{:S(2)}) collective-permute-start(f32[48,640]{1,0:T(8,128)S(1)} %get-tuple-element.93), channel_id=1, source_target_pairs={{0,240},{16,0},{32,16},{48,32},{64,48},{80,64},{96,80},{112,96},{1... | collective-permute-start | bytes 368648 | tf_op jit(solution)/shard_map/ppermute | solution.py:445
  103.5 16.2 %collective-permute-start.12 = (f32[48,640]{1,0:T(8,128)S(1)}, f32[48,640]{1,0:T(8,128)S(1)}, u32[]{:S(2)}, u32[]{:S(2)}) collective-permute-start(f32[48,640]{1,0:T(8,128)S(1)} %get-tuple-element.88), channel_id=1, source_target_pairs={{0,16},{16,32},{32,48},{48,64},{64,80},{80,96},{96,112},{112,128},... | collective-permute-start | bytes 368648 | tf_op jit(solution)/shard_map/ppermute | solution.py:446
  103.6 16.1 %collective-permute-start.13 = (f32[48,640]{1,0:T(8,128)S(1)}, f32[48,640]{1,0:T(8,128)S(1)}, u32[]{:S(2)}, u32[]{:S(2)}) collective-permute-start(f32[48,640]{1,0:T(8,128)S(1)} %get-tuple-element.89), channel_id=1, source_target_pairs={{0,240},{16,0},{32,16},{48,32},{64,48},{80,64},{96,80},{112,96},{1... | collective-permute-start | bytes 368648 | tf_op jit(solution)/shard_map/ppermute | solution.py:445
  114.5 16.2 %collective-permute-start.18 = (f32[48,640]{1,0:T(8,128)S(1)}, f32[48,640]{1,0:T(8,128)S(1)}, u32[]{:S(2)}, u32[]{:S(2)}) collective-permute-start(f32[48,640]{1,0:T(8,128)S(1)} %get-tuple-element.102), channel_id=1, source_target_pairs={{0,16},{16,32},{32,48},{48,64},{64,80},{80,96},{96,112},{112,128},... | collective-permute-start | bytes 368648 | tf_op jit(solution)/shard_map/ppermute | solution.py:446
  114.6 16.1 %collective-permute-start.19 = (f32[48,640]{1,0:T(8,128)S(1)}, f32[48,640]{1,0:T(8,128)S(1)}, u32[]{:S(2)}, u32[]{:S(2)}) collective-permute-start(f32[48,640]{1,0:T(8,128)S(1)} %get-tuple-element.103), channel_id=1, source_target_pairs={{0,240},{16,0},{32,16},{48,32},{64,48},{80,64},{96,80},{112,96},{1... | collective-permute-start | bytes 368648 | tf_op jit(solution)/shard_map/ppermute | solution.py:445
  125.5 11.9 %collective-permute-start.16 = (f32[48,640]{1,0:T(8,128)S(1)}, f32[48,640]{1,0:T(8,128)S(1)}, u32[]{:S(2)}, u32[]{:S(2)}) collective-permute-start(f32[48,640]{1,0:T(8,128)S(1)} %get-tuple-element.98), channel_id=1, source_target_pairs={{0,16},{16,32},{32,48},{48,64},{64,80},{80,96},{96,112},{112,128},... | collective-permute-start | bytes 368648 | tf_op jit(solution)/shard_map/ppermute | solution.py:446
  125.6 11.9 %collective-permute-start.17 = (f32[48,640]{1,0:T(8,128)S(1)}, f32[48,640]{1,0:T(8,128)S(1)}, u32[]{:S(2)}, u32[]{:S(2)}) collective-permute-start(f32[48,640]{1,0:T(8,128)S(1)} %get-tuple-element.99), channel_id=1, source_target_pairs={{0,240},{16,0},{32,16},{48,32},{64,48},{80,64},{96,80},{112,96},{1... | collective-permute-start | bytes 368648 | tf_op jit(solution)/shard_map/ppermute | solution.py:445
  144.3 4.8 %collective-permute-start.20 = (f32[128,512]{1,0:T(8,128)S(1)}, f32[128,512]{1,0:T(8,128)S(1)}, u32[]{:S(2)}, u32[]{:S(2)}) collective-permute-start(f32[128,512]{1,0:T(8,128)S(1)} %get-tuple-element.112), channel_id=1, source_target_pairs={{0,1},{1,0},{2,3},{3,2},{4,5},{5,4},{6,7},{7,6},{8,9},{9,8},{10,11... | collective-permute-start | bytes 786440 | tf_op jit(solution)/shard_map/ppermute | solution.py:457
  149.2 7.6 %collective-permute-start.21 = (f32[128,512]{1,0:T(8,128)S(1)}, f32[128,512]{1,0:T(8,128)S(1)}, u32[]{:S(2)}, u32[]{:S(2)}) collective-permute-start(f32[128,512]{1,0:T(8,128)S(1)} %add.11), channel_id=1, source_target_pairs={{0,2},{1,3},{2,0},{3,1},{4,6},{5,7},{6,4},{7,5},{8,10},{9,11},{10,... | collective-permute-start | bytes 786440 | tf_op jit(solution)/shard_map/ppermute | solution.py:458
  156.8 2.5 %collective-permute-start.22 = (f32[128,512]{1,0:T(8,128)S(1)}, f32[128,512]{1,0:T(8,128)S(1)}, u32[]{:S(2)}, u32[]{:S(2)}) collective-permute-start(f32[128,512]{1,0:T(8,128)S(1)} %add.12), channel_id=1, source_target_pairs={{0,1},{1,0},{2,3},{3,2},{4,5},{5,4},{6,7},{7,6},{8,9},{9,8},{10,11... | collective-permute-start | bytes 786440 | tf_op jit(solution)/shard_map/ppermute | solution.py:459
  (5 other events, 152.4 us)

commit v4 on v3

--- a/solution.py
+++ b/solution.py
@@ -228,8 +228,8 @@
         inner, outer = max(start, HALO), min(start + size, end)
         for row in range(start, min(start + size, HALO), 16):
             chunk(row)
-        if inner < outer:
-            chunks(inner, outer, chunk)
+        for row in range(inner, outer, 16):
+            chunk(row)
         for row in range(max(start, end), start + size, 16):
             chunk(row)
         start += size
@@ -535,7 +535,7 @@
     block = shape(total, cols)
     grad = None
     lams, ends, coefs, films = [None] * 2, [None] * 2, [None] * 2, [rough_adjoint] * 2
-    later = both_ways(*after(edges[2:4], near), "roll")
+    later = both_ways(*after(edges[2:4], (*near, top_corner, bot_corner)), "roll")
     for c in range(2):
         lams[c], up, down, grad, *coefs[c] = call(
             functools.partial(first_kernel, c),

time: 160 us -> 138 us (0.86)
  Pallas kernels: 57 us -> 40 us
  waiting for transfers between devices: 36.5 us -> 31.3 us
    pallas_call x13, Pallas kernels: 57 us -> 40 us  [call(): pl.pallas_call(body, out_shape=tuple(outs), in_specs=[SM] * len(smem) + [...]
    ppermute x10, waiting for transfers between devices: 23.1 us -> 18.2 us  [both_ways(): from_low = lax.ppermute(down, axis, ring(axis, 1))]
    ppermute x10, starting transfers between devices: 49.5 us -> 53.4 us  [both_ways(): from_high = lax.ppermute(up, axis, ring(axis, -1))]
    ppermute x10, starting transfers between devices: 9.2 us -> 5.61 us  [both_ways(): from_low = lax.ppermute(down, axis, ring(axis, 1))]
  transfers between devices with their start and end apart: 23 -> 23, of which waited for: 7 -> 7; matrix products, arithmetic and copies ran while one was open for 0% -> 0% of each run, Pallas kernels for 30% -> 24%
where the time goes in v4:
time: 138 us
  starting transfers between devices  63.9 us (46%)
  Pallas kernels  40 us (29%)
  waiting for transfers between devices  31.3 us (23%)
    ppermute x10, starting transfers between devices, both_ways(): from_high = lax.ppermute(up, axis, ring(axis, -1))  53.4 us
    pallas_call x13, Pallas kernels, call(): pl.pallas_call(body, out_shape=tuple(outs), in_specs=[SM] * len(smem) + [...  40 us
    ppermute x10, waiting for transfers between devices, both_ways(): from_low = lax.ppermute(down, axis, ring(axis, 1))  18.2 us
    ppermute x1, waiting for transfers between devices, case_sum(): mine = mine + lax.ppermute(mine, 'case', swap_chip)  7.2 us
    ppermute x10, starting transfers between devices, both_ways(): from_low = lax.ppermute(down, axis, ring(axis, 1))  5.61 us
    ppermute x10, waiting for transfers between devices, both_ways(): from_high = lax.ppermute(up, axis, ring(axis, -1))  3.51 us
    ppermute x1, starting transfers between devices, case_sum(): mine = mine + lax.ppermute(other, 'case', swap_core)  3.21 us
  transfers between devices with their start and end apart: 23, of which 7 were waited for; matrix products, arithmetic and copies ran while one was open for 0% of the time, Pallas kernels for 24%

profile of v4, /device:TPU:1, one launch (start us, length us, event | category | flops | bytes accessed | tf_op | source)
XLA Modules:
  0.0 137.7 jit_solution(4071886973631090070)
XLA Ops:
  1.4 2.4 %edges.1 = (f32[2,160,512]{2,1,0:T(8,128)S(1)}, f32[2,160,512]{2,1,0:T(8,128)S(1)}, f32[2,120,512]{2,1,0:T(8,128)S(1)}, f32[2,96,512]{2,1,0:T(8,128)S(1)}) custom-call(s32[11]{0:T(128)S(1)} %concatenate.9.scal, f32[2,256,512]{2,1,0:T(8,128)} %diag.5, f32[2,256,512]{2,1,0:T(8,128)} %fx.5, f32[2,256,512]{2,1,0:T(8,128)} %fy.5, f32[2,256,512]{2,1,0:T(8,128)} %film.13, ...), custom_call_target="tpu_custom_call" | custom-call | bytes 10584064 | tf_op jit(solution)/shard_map/edges/pallas_call | solution.py:426
  3.8 3.7 %collective-permute-start.2 = (f32[2,160,512]{2,1,0:T(8,128)S(1)}, f32[2,160,512]{2,1,0:T(8,128)S(1)}, u32[]{:S(2)}, u32[]{:S(2)}) collective-permute-start(f32[2,160,512]{2,1,0:T(8,128)S(1)} %get-tuple-element.67), channel_id=1, source_target_pairs={{0,16},{16,32},{32,48},{48,64},{64,80},{80,96},{96,112},{112,128},... | collective-permute-start | bytes 1966088 | tf_op jit(solution)/shard_map/ppermute | solution.py:446
  7.5 5.4 %collective-permute-start.3 = (f32[2,160,512]{2,1,0:T(8,128)S(1)}, f32[2,160,512]{2,1,0:T(8,128)S(1)}, u32[]{:S(2)}, u32[]{:S(2)}) collective-permute-start(f32[2,160,512]{2,1,0:T(8,128)S(1)} %get-tuple-element.58), channel_id=1, source_target_pairs={{0,240},{16,0},{32,16},{48,32},{64,48},{80,64},{96,80},{112,96},{1... | collective-permute-start | bytes 1966088 | tf_op jit(solution)/shard_map/ppermute | solution.py:445
  12.9 4.4 %pack.1 = (f32[2,256,128]{2,1,0:T(8,128)S(1)}, f32[2,256,128]{2,1,0:T(8,128)S(1)}) custom-call(s32[11]{0:T(128)S(1)} %concatenate.9.scal, f32[2,256,512]{2,1,0:T(8,128)} %diag.5, f32[2,256,512]{2,1,0:T(8,128)} %fx.5, f32[2,256,512]{2,1,0:T(8,128)} %fy.5, f32[2,256,512]{2,1,0:T(8,128)} %film.13, f32[2,4,256,512]{3,2,1,0:T(8,128)} %src.17), custom_call_target="tpu_custom_call" | custom-call | bytes 8912896 | tf_op jit(solution)/shard_map/pack/pallas_call | solution.py:426
  23.1 2.6 %collective-permute-done.from_left = f32[2,256,128]{2,1,0:T(8,128)S(1)} collective-permute-done((f32[2,256,128]{2,1,0:T(8,128)S(1)}, f32[2,256,128]{2,1,0:T(8,128)S(1)}, u32[]{:S(2)}, u32[]{:S(2)}) %collective-permute-start) | collective-permute-done | bytes 262176 | tf_op jit(solution)/shard_map/ppermute | solution.py:446
  28.1 5.1 %collective-permute-start.5 = (f32[2,88,128]{2,1,0:T(8,128)S(1)}, f32[2,88,128]{2,1,0:T(8,128)S(1)}, u32[]{:S(2)}, u32[]{:S(2)}) collective-permute-start(f32[2,88,128]{2,1,0:T(8,128)S(1)} %get-tuple-element.69), channel_id=1, source_target_pairs={{0,240},{16,0},{32,16},{48,32},{64,48},{80,64},{96,80},{112,96},{1... | collective-permute-start | bytes 270344 | tf_op jit(solution)/shard_map/ppermute | solution.py:445
  33.1 5.7 %collective-permute-done.4.top_corner = f32[2,88,128]{2,1,0:T(8,128)S(1)} collective-permute-done((f32[2,88,128]{2,1,0:T(8,128)S(1)}, f32[2,88,128]{2,1,0:T(8,128)S(1)}, u32[]{:S(2)}, u32[]{:S(2)}) %collective-permute-start.4) | collective-permute-done | bytes 90144 | tf_op jit(solution)/shard_map/ppermute | solution.py:446
  38.8 3.5 %collective-permute-done.5.bot_corner = f32[2,88,128]{2,1,0:T(8,128)S(1)} collective-permute-done((f32[2,88,128]{2,1,0:T(8,128)S(1)}, f32[2,88,128]{2,1,0:T(8,128)S(1)}, u32[]{:S(2)}, u32[]{:S(2)}) %collective-permute-start.5) | collective-permute-done | bytes 90144 | tf_op jit(solution)/shard_map/ppermute | solution.py:445
  42.3 5.6 %collective-permute-start.7 = (f32[2,120,512]{2,1,0:T(8,128)S(1)}, f32[2,120,512]{2,1,0:T(8,128)S(1)}, u32[]{:S(2)}, u32[]{:S(2)}) collective-permute-start(f32[2,120,512]{2,1,0:T(8,128)S(1)} %get-tuple-element.76), channel_id=1, source_target_pairs={{0,240},{16,0},{32,16},{48,32},{64,48},{80,64},{96,80},{112,96},{1... | collective-permute-start | bytes 1474568 | tf_op jit(solution)/shard_map/ppermute | solution.py:445
  50.3 5.3 %collective-permute-start.11 = (f32[48,640]{1,0:T(8,128)S(1)}, f32[48,640]{1,0:T(8,128)S(1)}, u32[]{:S(2)}, u32[]{:S(2)}) collective-permute-start(f32[48,640]{1,0:T(8,128)S(1)} %get-tuple-element.84), channel_id=1, source_target_pairs={{0,240},{16,0},{32,16},{48,32},{64,48},{80,64},{96,80},{112,96},{1... | collective-permute-start | bytes 368648 | tf_op jit(solution)/shard_map/ppermute | solution.py:445
  58.1 10.0 %collective-permute-done.10.lam_top = f32[48,640]{1,0:T(8,128)S(1)} collective-permute-done((f32[48,640]{1,0:T(8,128)S(1)}, f32[48,640]{1,0:T(8,128)S(1)}, u32[]{:S(2)}, u32[]{:S(2)}) %collective-permute-start.10) | collective-permute-done | bytes 122912 | tf_op jit(solution)/shard_map/ppermute | solution.py:446
  68.1 10.2 %collective-permute-start.9 = (f32[48,640]{1,0:T(8,128)S(1)}, f32[48,640]{1,0:T(8,128)S(1)}, u32[]{:S(2)}, u32[]{:S(2)}) collective-permute-start(f32[48,640]{1,0:T(8,128)S(1)} %get-tuple-element.79), channel_id=1, source_target_pairs={{0,240},{16,0},{32,16},{48,32},{64,48},{80,64},{96,80},{112,96},{1... | collective-permute-start | bytes 368648 | tf_op jit(solution)/shard_map/ppermute | solution.py:445
  78.3 3.6 %step2case0.1 = (f32[256,640]{1,0:T(8,128)S(1)}, f32[48,640]{1,0:T(8,128)S(1)}, f32[48,640]{1,0:T(8,128)S(1)}, f32[336,640]{1,0:T(8,128)S(1)}, f32[256,512]{1,0:T(8,128)S(1)}) custom-call(s32[11]{0:T(128)S(1)} %concatenate.9.scal, bf16[128,1152]{1,0:T(8,128)(2,1)S(1)} %bands.1.mats, f32[2,3,256,512]{3,2,1,0:T(8,128)S(1)} %get-tuple-element.61.coef, ...), custom_call_target="tpu_custom_call" | custom-call | flops 1610612736 | bytes 17653760 | tf_op jit(solution)/shard_map/step2case0/pallas_call | solution.py:426
  82.0 5.1 %collective-permute-start.15 = (f32[48,640]{1,0:T(8,128)S(1)}, f32[48,640]{1,0:T(8,128)S(1)}, u32[]{:S(2)}, u32[]{:S(2)}) collective-permute-start(f32[48,640]{1,0:T(8,128)S(1)} %get-tuple-element.93), channel_id=1, source_target_pairs={{0,240},{16,0},{32,16},{48,32},{64,48},{80,64},{96,80},{112,96},{1... | collective-permute-start | bytes 368648 | tf_op jit(solution)/shard_map/ppermute | solution.py:445
  87.1 3.6 %step2case1.1 = (f32[256,640]{1,0:T(8,128)S(1)}, f32[48,640]{1,0:T(8,128)S(1)}, f32[48,640]{1,0:T(8,128)S(1)}, f32[336,640]{1,0:T(8,128)S(1)}, f32[256,512]{1,0:T(8,128)S(1)}) custom-call(s32[11]{0:T(128)S(1)} %concatenate.9.scal, bf16[128,1152]{1,0:T(8,128)(2,1)S(1)} %bands.1.mats, f32[2,3,256,512]{3,2,1,0:T(8,128)S(1)} %get-tuple-element.61.coef, ...), custom_call_target="tpu_custom_call" | custom-call | flops 1610612736 | bytes 17653760 | tf_op jit(solution)/shard_map/step2case1/pallas_call | solution.py:426
  90.7 5.1 %collective-permute-start.13 = (f32[48,640]{1,0:T(8,128)S(1)}, f32[48,640]{1,0:T(8,128)S(1)}, u32[]{:S(2)}, u32[]{:S(2)}) collective-permute-start(f32[48,640]{1,0:T(8,128)S(1)} %get-tuple-element.89), channel_id=1, source_target_pairs={{0,240},{16,0},{32,16},{48,32},{64,48},{80,64},{96,80},{112,96},{1... | collective-permute-start | bytes 368648 | tf_op jit(solution)/shard_map/ppermute | solution.py:445
  95.8 3.6 %step1case0.1 = (f32[256,640]{1,0:T(8,128)S(1)}, f32[48,640]{1,0:T(8,128)S(1)}, f32[48,640]{1,0:T(8,128)S(1)}, f32[328,640]{1,0:T(8,128)S(1)}, f32[256,512]{1,0:T(8,128)S(1)}) custom-call(s32[11]{0:T(128)S(1)} %concatenate.9.scal, bf16[128,1152]{1,0:T(8,128)(2,1)S(1)} %bands.1.mats, f32[2,3,256,512]{3,2,1,0:T(8,128)S(1)} %get-tuple-element.61.coef, ...), custom_call_target="tpu_custom_call" | custom-call | flops 1610612736 | bytes 16134144 | tf_op jit(solution)/shard_map/step1case0/pallas_call | solution.py:426
  99.5 5.1 %collective-permute-start.19 = (f32[48,640]{1,0:T(8,128)S(1)}, f32[48,640]{1,0:T(8,128)S(1)}, u32[]{:S(2)}, u32[]{:S(2)}) collective-permute-start(f32[48,640]{1,0:T(8,128)S(1)} %get-tuple-element.103), channel_id=1, source_target_pairs={{0,240},{16,0},{32,16},{48,32},{64,48},{80,64},{96,80},{112,96},{1... | collective-permute-start | bytes 368648 | tf_op jit(solution)/shard_map/ppermute | solution.py:445
  104.6 3.6 %step1case1.1 = (f32[256,640]{1,0:T(8,128)S(1)}, f32[48,640]{1,0:T(8,128)S(1)}, f32[48,640]{1,0:T(8,128)S(1)}, f32[328,640]{1,0:T(8,128)S(1)}, f32[256,512]{1,0:T(8,128)S(1)}) custom-call(s32[11]{0:T(128)S(1)} %concatenate.9.scal, bf16[128,1152]{1,0:T(8,128)(2,1)S(1)} %bands.1.mats, f32[2,3,256,512]{3,2,1,0:T(8,128)S(1)} %get-tuple-element.61.coef, ...), custom_call_target="tpu_custom_call" | custom-call | flops 1610612736 | bytes 16134144 | tf_op jit(solution)/shard_map/step1case1/pallas_call | solution.py:426
  108.2 5.1 %collective-permute-start.17 = (f32[48,640]{1,0:T(8,128)S(1)}, f32[48,640]{1,0:T(8,128)S(1)}, u32[]{:S(2)}, u32[]{:S(2)}) collective-permute-start(f32[48,640]{1,0:T(8,128)S(1)} %get-tuple-element.99), channel_id=1, source_target_pairs={{0,240},{16,0},{32,16},{48,32},{64,48},{80,64},{96,80},{112,96},{1... | collective-permute-start | bytes 368648 | tf_op jit(solution)/shard_map/ppermute | solution.py:445
  113.3 4.5 %step0case0.1 = (f32[2,256,512]{2,1,0:T(8,128)}, f32[2,256,512]{2,1,0:T(8,128)}, f32[256,512]{1,0:T(8,128)S(1)}) custom-call(s32[11]{0:T(128)S(1)} %concatenate.9.scal, bf16[128,1152]{1,0:T(8,128)(2,1)S(1)} %bands.1.mats, f32[2,3,256,512]{3,2,1,0:T(8,128)S(1)} %get-tuple-element.61.coef, f32[2,8,256,128]{3,2,1,0:T(8,128)S(1)} %get-tuple-element.65.side, ...), custom_call_target="tpu_custom_call" | custom-call | flops 1610612736 | bytes 16470016 | tf_op jit(solution)/shard_map/step0case0/pallas_call | solution.py:426
  117.8 4.6 %step0case1.1 = (f32[2,256,512]{2,1,0:T(8,128)}, f32[2,256,512]{2,1,0:T(8,128)}, f32[128,512]{1,0:T(8,128)S(1)}, f32[128,512]{1,0:T(8,128)S(1)}) custom-call(s32[11]{0:T(128)S(1)} %concatenate.9.scal, bf16[128,1152]{1,0:T(8,128)(2,1)S(1)} %bands.1.mats, ...), custom_call_target="tpu_custom_call", output_to_operand_aliasing={{0}: (16, {}), {1}: (17, {})} | custom-call | flops 1610612736 | bytes 18567168 | tf_op jit(solution)/shard_map/step0case1/pallas_call | solution.py:426
  122.4 3.2 %collective-permute-start.20 = (f32[128,512]{1,0:T(8,128)S(1)}, f32[128,512]{1,0:T(8,128)S(1)}, u32[]{:S(2)}, u32[]{:S(2)}) collective-permute-start(f32[128,512]{1,0:T(8,128)S(1)} %get-tuple-element.112), channel_id=1, source_target_pairs={{0,1},{1,0},{2,3},{3,2},{4,5},{5,4},{6,7},{7,6},{8,9},{9,8},{10,11... | collective-permute-start | bytes 786440 | tf_op jit(solution)/shard_map/ppermute | solution.py:457
  127.2 7.2 %collective-permute-done.21 = f32[128,512]{1,0:T(8,128)S(1)} collective-permute-done((f32[128,512]{1,0:T(8,128)S(1)}, f32[128,512]{1,0:T(8,128)S(1)}, u32[]{:S(2)}, u32[]{:S(2)}) %collective-permute-start.21) | collective-permute-done | bytes 262176 | tf_op jit(solution)/shard_map/ppermute | solution.py:458
  (51 shorter events, 19.0 us)
Async XLA Ops:
  3.8 38.4 %collective-permute-start.2 = (f32[2,160,512]{2,1,0:T(8,128)S(1)}, f32[2,160,512]{2,1,0:T(8,128)S(1)}, u32[]{:S(2)}, u32[]{:S(2)}) collective-permute-start(f32[2,160,512]{2,1,0:T(8,128)S(1)} %get-tuple-element.67), channel_id=1, source_target_pairs={{0,16},{16,32},{32,48},{48,64},{64,80},{80,96},{96,112},{112,128},... | collective-permute-start | bytes 1966088 | tf_op jit(solution)/shard_map/ppermute | solution.py:446
  7.5 12.8 %copy-start.4 = (f32[2,256,512]{2,1,0:T(8,128)S(1)}, f32[2,256,512]{2,1,0:T(8,128)}, u32[]{:S(2)}) copy-start(f32[2,256,512]{2,1,0:T(8,128)} %fy.5) | copy-start | bytes 3145732
  7.5 34.8 %collective-permute-start.3 = (f32[2,160,512]{2,1,0:T(8,128)S(1)}, f32[2,160,512]{2,1,0:T(8,128)S(1)}, u32[]{:S(2)}, u32[]{:S(2)}) collective-permute-start(f32[2,160,512]{2,1,0:T(8,128)S(1)} %get-tuple-element.58), channel_id=1, source_target_pairs={{0,240},{16,0},{32,16},{48,32},{64,48},{80,64},{96,80},{112,96},{1... | collective-permute-start | bytes 1966088 | tf_op jit(solution)/shard_map/ppermute | solution.py:445
  17.4 8.3 %collective-permute-start = (f32[2,256,128]{2,1,0:T(8,128)S(1)}, f32[2,256,128]{2,1,0:T(8,128)S(1)}, u32[]{:S(2)}, u32[]{:S(2)}) collective-permute-start(f32[2,256,128]{2,1,0:T(8,128)S(1)} %get-tuple-element.62), channel_id=1, source_target_pairs={{0,4},{4,8},{8,12},{12,0},{1,5},{5,9},{9,13},{13,1},{2,6},{6,10},{... | collective-permute-start | bytes 786440 | tf_op jit(solution)/shard_map/ppermute | solution.py:446
  18.7 6.9 %collective-permute-start.1 = (f32[2,256,128]{2,1,0:T(8,128)S(1)}, f32[2,256,128]{2,1,0:T(8,128)S(1)}, u32[]{:S(2)}, u32[]{:S(2)}) collective-permute-start(f32[2,256,128]{2,1,0:T(8,128)S(1)} %get-tuple-element.60.gate), channel_id=1, source_target_pairs={{0,12},{4,0},{8,4},{12,8},{1,13},{5,1},{9,5},{13,9},{2,14},{6,2},{... | collective-permute-start | bytes 786440 | tf_op jit(solution)/shard_map/ppermute | solution.py:445
  28.0 10.8 %collective-permute-start.4 = (f32[2,88,128]{2,1,0:T(8,128)S(1)}, f32[2,88,128]{2,1,0:T(8,128)S(1)}, u32[]{:S(2)}, u32[]{:S(2)}) collective-permute-start(f32[2,88,128]{2,1,0:T(8,128)S(1)} %get-tuple-element.68), channel_id=1, source_target_pairs={{0,16},{16,32},{32,48},{48,64},{64,80},{80,96},{96,112},{112,128},... | collective-permute-start | bytes 270344 | tf_op jit(solution)/shard_map/ppermute | solution.py:446
  28.1 14.2 %collective-permute-start.5 = (f32[2,88,128]{2,1,0:T(8,128)S(1)}, f32[2,88,128]{2,1,0:T(8,128)S(1)}, u32[]{:S(2)}, u32[]{:S(2)}) collective-permute-start(f32[2,88,128]{2,1,0:T(8,128)S(1)} %get-tuple-element.69), channel_id=1, source_target_pairs={{0,240},{16,0},{32,16},{48,32},{64,48},{80,64},{96,80},{112,96},{1... | collective-permute-start | bytes 270344 | tf_op jit(solution)/shard_map/ppermute | solution.py:445
  42.3 36.0 %collective-permute-start.7 = (f32[2,120,512]{2,1,0:T(8,128)S(1)}, f32[2,120,512]{2,1,0:T(8,128)S(1)}, u32[]{:S(2)}, u32[]{:S(2)}) collective-permute-start(f32[2,120,512]{2,1,0:T(8,128)S(1)} %get-tuple-element.76), channel_id=1, source_target_pairs={{0,240},{16,0},{32,16},{48,32},{64,48},{80,64},{96,80},{112,96},{1... | collective-permute-start | bytes 1474568 | tf_op jit(solution)/shard_map/ppermute | solution.py:445
  47.9 30.4 %collective-permute-start.6 = (f32[2,96,512]{2,1,0:T(8,128)S(1)}, f32[2,96,512]{2,1,0:T(8,128)S(1)}, u32[]{:S(2)}, u32[]{:S(2)}) collective-permute-start(f32[2,96,512]{2,1,0:T(8,128)S(1)} %get-tuple-element.75), channel_id=1, source_target_pairs={{0,16},{16,32},{32,48},{48,64},{64,80},{80,96},{96,112},{112,128},... | collective-permute-start | bytes 1179656 | tf_op jit(solution)/shard_map/ppermute | solution.py:446
  50.2 17.9 %collective-permute-start.10 = (f32[48,640]{1,0:T(8,128)S(1)}, f32[48,640]{1,0:T(8,128)S(1)}, u32[]{:S(2)}, u32[]{:S(2)}) collective-permute-start(f32[48,640]{1,0:T(8,128)S(1)} %get-tuple-element.83), channel_id=1, source_target_pairs={{0,16},{16,32},{32,48},{48,64},{64,80},{80,96},{96,112},{112,128},... | collective-permute-start | bytes 368648 | tf_op jit(solution)/shard_map/ppermute | solution.py:446
  50.3 28.0 %collective-permute-start.11 = (f32[48,640]{1,0:T(8,128)S(1)}, f32[48,640]{1,0:T(8,128)S(1)}, u32[]{:S(2)}, u32[]{:S(2)}) collective-permute-start(f32[48,640]{1,0:T(8,128)S(1)} %get-tuple-element.84), channel_id=1, source_target_pairs={{0,240},{16,0},{32,16},{48,32},{64,48},{80,64},{96,80},{112,96},{1... | collective-permute-start | bytes 368648 | tf_op jit(solution)/shard_map/ppermute | solution.py:445
  58.0 29.0 %collective-permute-start.8 = (f32[48,640]{1,0:T(8,128)S(1)}, f32[48,640]{1,0:T(8,128)S(1)}, u32[]{:S(2)}, u32[]{:S(2)}) collective-permute-start(f32[48,640]{1,0:T(8,128)S(1)} %get-tuple-element.78), channel_id=1, source_target_pairs={{0,16},{16,32},{32,48},{48,64},{64,80},{80,96},{96,112},{112,128},... | collective-permute-start | bytes 368648 | tf_op jit(solution)/shard_map/ppermute | solution.py:446
  68.1 18.9 %collective-permute-start.9 = (f32[48,640]{1,0:T(8,128)S(1)}, f32[48,640]{1,0:T(8,128)S(1)}, u32[]{:S(2)}, u32[]{:S(2)}) collective-permute-start(f32[48,640]{1,0:T(8,128)S(1)} %get-tuple-element.79), channel_id=1, source_target_pairs={{0,240},{16,0},{32,16},{48,32},{64,48},{80,64},{96,80},{112,96},{1... | collective-permute-start | bytes 368648 | tf_op jit(solution)/shard_map/ppermute | solution.py:445
  81.9 13.9 %collective-permute-start.14 = (f32[48,640]{1,0:T(8,128)S(1)}, f32[48,640]{1,0:T(8,128)S(1)}, u32[]{:S(2)}, u32[]{:S(2)}) collective-permute-start(f32[48,640]{1,0:T(8,128)S(1)} %get-tuple-element.92), channel_id=1, source_target_pairs={{0,16},{16,32},{32,48},{48,64},{64,80},{80,96},{96,112},{112,128},... | collective-permute-start | bytes 368648 | tf_op jit(solution)/shard_map/ppermute | solution.py:446
  82.0 13.8 %collective-permute-start.15 = (f32[48,640]{1,0:T(8,128)S(1)}, f32[48,640]{1,0:T(8,128)S(1)}, u32[]{:S(2)}, u32[]{:S(2)}) collective-permute-start(f32[48,640]{1,0:T(8,128)S(1)} %get-tuple-element.93), channel_id=1, source_target_pairs={{0,240},{16,0},{32,16},{48,32},{64,48},{80,64},{96,80},{112,96},{1... | collective-permute-start | bytes 368648 | tf_op jit(solution)/shard_map/ppermute | solution.py:445
  90.6 13.9 %collective-permute-start.12 = (f32[48,640]{1,0:T(8,128)S(1)}, f32[48,640]{1,0:T(8,128)S(1)}, u32[]{:S(2)}, u32[]{:S(2)}) collective-permute-start(f32[48,640]{1,0:T(8,128)S(1)} %get-tuple-element.88), channel_id=1, source_target_pairs={{0,16},{16,32},{32,48},{48,64},{64,80},{80,96},{96,112},{112,128},... | collective-permute-start | bytes 368648 | tf_op jit(solution)/shard_map/ppermute | solution.py:446
  90.7 13.8 %collective-permute-start.13 = (f32[48,640]{1,0:T(8,128)S(1)}, f32[48,640]{1,0:T(8,128)S(1)}, u32[]{:S(2)}, u32[]{:S(2)}) collective-permute-start(f32[48,640]{1,0:T(8,128)S(1)} %get-tuple-element.89), channel_id=1, source_target_pairs={{0,240},{16,0},{32,16},{48,32},{64,48},{80,64},{96,80},{112,96},{1... | collective-permute-start | bytes 368648 | tf_op jit(solution)/shard_map/ppermute | solution.py:445
  99.4 13.9 %collective-permute-start.18 = (f32[48,640]{1,0:T(8,128)S(1)}, f32[48,640]{1,0:T(8,128)S(1)}, u32[]{:S(2)}, u32[]{:S(2)}) collective-permute-start(f32[48,640]{1,0:T(8,128)S(1)} %get-tuple-element.102), channel_id=1, source_target_pairs={{0,16},{16,32},{32,48},{48,64},{64,80},{80,96},{96,112},{112,128},... | collective-permute-start | bytes 368648 | tf_op jit(solution)/shard_map/ppermute | solution.py:446
  99.5 13.8 %collective-permute-start.19 = (f32[48,640]{1,0:T(8,128)S(1)}, f32[48,640]{1,0:T(8,128)S(1)}, u32[]{:S(2)}, u32[]{:S(2)}) collective-permute-start(f32[48,640]{1,0:T(8,128)S(1)} %get-tuple-element.103), channel_id=1, source_target_pairs={{0,240},{16,0},{32,16},{48,32},{64,48},{80,64},{96,80},{112,96},{1... | collective-permute-start | bytes 368648 | tf_op jit(solution)/shard_map/ppermute | solution.py:445
  108.1 9.6 %collective-permute-start.16 = (f32[48,640]{1,0:T(8,128)S(1)}, f32[48,640]{1,0:T(8,128)S(1)}, u32[]{:S(2)}, u32[]{:S(2)}) collective-permute-start(f32[48,640]{1,0:T(8,128)S(1)} %get-tuple-element.98), channel_id=1, source_target_pairs={{0,16},{16,32},{32,48},{48,64},{64,80},{80,96},{96,112},{112,128},... | collective-permute-start | bytes 368648 | tf_op jit(solution)/shard_map/ppermute | solution.py:446
  108.2 9.6 %collective-permute-start.17 = (f32[48,640]{1,0:T(8,128)S(1)}, f32[48,640]{1,0:T(8,128)S(1)}, u32[]{:S(2)}, u32[]{:S(2)}) collective-permute-start(f32[48,640]{1,0:T(8,128)S(1)} %get-tuple-element.99), channel_id=1, source_target_pairs={{0,240},{16,0},{32,16},{48,32},{64,48},{80,64},{96,80},{112,96},{1... | collective-permute-start | bytes 368648 | tf_op jit(solution)/shard_map/ppermute | solution.py:445
  122.4 4.4 %collective-permute-start.20 = (f32[128,512]{1,0:T(8,128)S(1)}, f32[128,512]{1,0:T(8,128)S(1)}, u32[]{:S(2)}, u32[]{:S(2)}) collective-permute-start(f32[128,512]{1,0:T(8,128)S(1)} %get-tuple-element.112), channel_id=1, source_target_pairs={{0,1},{1,0},{2,3},{3,2},{4,5},{5,4},{6,7},{7,6},{8,9},{9,8},{10,11... | collective-permute-start | bytes 786440 | tf_op jit(solution)/shard_map/ppermute | solution.py:457
  126.8 7.6 %collective-permute-start.21 = (f32[128,512]{1,0:T(8,128)S(1)}, f32[128,512]{1,0:T(8,128)S(1)}, u32[]{:S(2)}, u32[]{:S(2)}) collective-permute-start(f32[128,512]{1,0:T(8,128)S(1)} %add.11), channel_id=1, source_target_pairs={{0,2},{1,3},{2,0},{3,1},{4,6},{5,7},{6,4},{7,5},{8,10},{9,11},{10,... | collective-permute-start | bytes 786440 | tf_op jit(solution)/shard_map/ppermute | solution.py:458
  134.4 2.5 %collective-permute-start.22 = (f32[128,512]{1,0:T(8,128)S(1)}, f32[128,512]{1,0:T(8,128)S(1)}, u32[]{:S(2)}, u32[]{:S(2)}) collective-permute-start(f32[128,512]{1,0:T(8,128)S(1)} %add.12), channel_id=1, source_target_pairs={{0,1},{1,0},{2,3},{3,2},{4,5},{5,4},{6,7},{7,6},{8,9},{9,8},{10,11... | collective-permute-start | bytes 786440 | tf_op jit(solution)/shard_map/ppermute | solution.py:459
  (5 other events, 53.8 us)

commit v5 on v2

--- a/solution.py
+++ b/solution.py
@@ -519,10 +519,7 @@
     film = rough_adjoint
     for step in range(STEPS - 2, -1, -1):
         lam_top, lam_bot = both_ways(up, down, "roll")
-        if step == STEPS - 2:
-            up_c, down_c = after((up_c, down_c), (lam_top, lam_bot))
-            top_c, bot_c = both_ways(up_c, down_c, "roll")
-        src_top, src_bot = (top_b, bot_b) if step == 2 else (top_c, bot_c)
+        src_top, src_bot = (top_b, bot_b) if step == 2 else last
         films = shape(cases, total + 2 * COEF + 8 * step, wide)
         half = shape(total // 2, cols)
         if step:
@@ -546,6 +543,8 @@
         )
         if step:
             lam, up, down, film, grad = result
+            if step == STEPS - 2:
+                last = both_ways(*after((up_c, down_c), (lam,)), "roll")
         else:
             lam, film, mine, other = result
     return lam, film, case_sum(mine, other, core)

time: 133 us -> 144 us (1.083)
  waiting for transfers between devices: 46.3 us -> 60.4 us
  starting transfers between devices: 48.6 us -> 45.7 us
    ppermute x8, waiting for transfers between devices: 17.6 us -> 35 us  [both_ways(): from_low = lax.ppermute(down, axis, ring(axis, 1))]
    ppermute x8, starting transfers between devices: 39.8 us -> 35.5 us  [both_ways(): from_high = lax.ppermute(up, axis, ring(axis, -1))]
    ppermute x8, waiting for transfers between devices: 20.1 us -> 16.8 us  [both_ways(): from_high = lax.ppermute(up, axis, ring(axis, -1))]
  transfers between devices with their start and end apart: 19 -> 19, of which waited for: 12 -> 12; matrix products, arithmetic and copies ran while one was open for 0% -> 0% of each run, Pallas kernels for 12% -> 7%
where the time goes in v5:
time: 144 us
  waiting for transfers between devices  60.4 us (42%)
  starting transfers between devices  45.7 us (32%)
  Pallas kernels  35.6 us (25%)
    pallas_call x9, Pallas kernels, call(): pl.pallas_call(body, out_shape=tuple(outs), in_specs=[SM] * len(smem) + [...  35.6 us
    ppermute x8, starting transfers between devices, both_ways(): from_high = lax.ppermute(up, axis, ring(axis, -1))  35.5 us
    ppermute x8, waiting for transfers between devices, both_ways(): from_low = lax.ppermute(down, axis, ring(axis, 1))  35 us
    ppermute x8, waiting for transfers between devices, both_ways(): from_high = lax.ppermute(up, axis, ring(axis, -1))  16.8 us
    ppermute x1, waiting for transfers between devices, case_sum(): mine = mine + lax.ppermute(mine, 'case', swap_chip)  6.3 us
    ppermute x8, starting transfers between devices, both_ways(): from_low = lax.ppermute(down, axis, ring(axis, 1))  6.25 us
  transfers between devices with their start and end apart: 19, of which 12 were waited for; matrix products, arithmetic and copies ran while one was open for 0% of the time, Pallas kernels for 7%

profile of v5, /device:TPU:1, one launch (start us, length us, event | category | flops | bytes accessed | tf_op | source)
XLA Modules:
  0.0 144.2 jit_solution(16870311022766044815)
XLA Ops:
  1.4 2.3 %edges.1 = (f32[2,160,512]{2,1,0:T(8,128)S(1)}, f32[2,160,512]{2,1,0:T(8,128)S(1)}, f32[2,56,512]{2,1,0:T(8,128)S(1)}, f32[2,32,512]{2,1,0:T(8,128)S(1)}, f32[2,...) custom-call(s32[11]{0:T(128)S(1)} %concatenate.9.scal, f32[2,256,512]{2,1,0:T(8,128)} %diag.5, f32[2,256,512]{2,1,0:T(8,128)} %fx.5, ...), custom_call_target="tpu_custom_call" | custom-call | bytes 10584064 | tf_op jit(solution)/shard_map/edges/pallas_call | solution.py:401
  3.7 3.7 %collective-permute-start.2 = (f32[2,160,512]{2,1,0:T(8,128)S(1)}, f32[2,160,512]{2,1,0:T(8,128)S(1)}, u32[]{:S(2)}, u32[]{:S(2)}) collective-permute-start(f32[2,160,512]{2,1,0:T(8,128)S(1)} %get-tuple-element.49), channel_id=1, source_target_pairs={{0,16},{16,32},{32,48},{48,64},{64,80},{80,96},{96,112},{112,128},... | collective-permute-start | bytes 1966088 | tf_op jit(solution)/shard_map/ppermute | solution.py:420
  7.4 5.4 %collective-permute-start.3 = (f32[2,160,512]{2,1,0:T(8,128)S(1)}, f32[2,160,512]{2,1,0:T(8,128)S(1)}, u32[]{:S(2)}, u32[]{:S(2)}) collective-permute-start(f32[2,160,512]{2,1,0:T(8,128)S(1)} %get-tuple-element.50), channel_id=1, source_target_pairs={{0,240},{16,0},{32,16},{48,32},{64,48},{80,64},{96,80},{112,96},{1... | collective-permute-start | bytes 1966088 | tf_op jit(solution)/shard_map/ppermute | solution.py:419
  12.8 4.7 %pack.1 = (f32[2,256,128]{2,1,0:T(8,128)S(1)}, f32[2,256,128]{2,1,0:T(8,128)S(1)}) custom-call(s32[11]{0:T(128)S(1)} %concatenate.9.scal, f32[2,256,512]{2,1,0:T(8,128)} %diag.5, f32[2,256,512]{2,1,0:T(8,128)} %fx.5, f32[2,256,512]{2,1,0:T(8,128)} %fy.5, f32[2,256,512]{2,1,0:T(8,128)} %film.9, f32[2,4,256,512]{3,2,1,0:T(8,128)} %src.11), custom_call_target="tpu_custom_call" | custom-call | bytes 8912896 | tf_op jit(solution)/shard_map/pack/pallas_call | solution.py:401
  23.2 2.6 %collective-permute-done.from_left = f32[2,256,128]{2,1,0:T(8,128)S(1)} collective-permute-done((f32[2,256,128]{2,1,0:T(8,128)S(1)}, f32[2,256,128]{2,1,0:T(8,128)S(1)}, u32[]{:S(2)}, u32[]{:S(2)}) %collective-permute-start) | collective-permute-done | bytes 262176 | tf_op jit(solution)/shard_map/ppermute | solution.py:420
  28.2 5.1 %collective-permute-start.5 = (f32[2,88,128]{2,1,0:T(8,128)S(1)}, f32[2,88,128]{2,1,0:T(8,128)S(1)}, u32[]{:S(2)}, u32[]{:S(2)}) collective-permute-start(f32[2,88,128]{2,1,0:T(8,128)S(1)} %get-tuple-element.52), channel_id=1, source_target_pairs={{0,240},{16,0},{32,16},{48,32},{64,48},{80,64},{96,80},{112,96},{1... | collective-permute-start | bytes 270344 | tf_op jit(solution)/shard_map/ppermute | solution.py:419
  33.3 5.4 %collective-permute-done.4.top_corner = f32[2,88,128]{2,1,0:T(8,128)S(1)} collective-permute-done((f32[2,88,128]{2,1,0:T(8,128)S(1)}, f32[2,88,128]{2,1,0:T(8,128)S(1)}, u32[]{:S(2)}, u32[]{:S(2)}) %collective-permute-start.4) | collective-permute-done | bytes 90144 | tf_op jit(solution)/shard_map/ppermute | solution.py:420
  38.7 3.5 %collective-permute-done.5.bot_corner = f32[2,88,128]{2,1,0:T(8,128)S(1)} collective-permute-done((f32[2,88,128]{2,1,0:T(8,128)S(1)}, f32[2,88,128]{2,1,0:T(8,128)S(1)}, u32[]{:S(2)}, u32[]{:S(2)}) %collective-permute-start.5) | collective-permute-done | bytes 90144 | tf_op jit(solution)/shard_map/ppermute | solution.py:419
  42.2 3.8 %first.1 = (f32[2,256,640]{2,1,0:T(8,128)S(1)}, f32[2,48,640]{2,1,0:T(8,128)S(1)}, f32[2,48,640]{2,1,0:T(8,128)S(1)}, f32[256,512]{1,0:T(8,128)S(1)}, f32[2,3,32...) custom-call(s32[11]{0:T(128)S(1)} %concatenate.9.scal, bf16[128,1152]{1,0:T(8,128)(2,1)S(1)} %bands.1.mats, ...), custom_call_target="tpu_custom_call" | custom-call | flops 2147483648 | bytes 12730368 | tf_op jit(solution)/shard_map/first/pallas_call | solution.py:401
  46.3 5.4 %collective-permute-start.9 = (f32[2,48,640]{2,1,0:T(8,128)S(1)}, f32[2,48,640]{2,1,0:T(8,128)S(1)}, u32[]{:S(2)}, u32[]{:S(2)}) collective-permute-start(f32[2,48,640]{2,1,0:T(8,128)S(1)} %get-tuple-element.63), channel_id=1, source_target_pairs={{0,240},{16,0},{32,16},{48,32},{64,48},{80,64},{96,80},{112,96},{1... | collective-permute-start | bytes 737288 | tf_op jit(solution)/shard_map/ppermute | solution.py:419
  51.7 2.9 %collective-permute-start.7 = (f32[2,56,512]{2,1,0:T(8,128)S(1)}, f32[2,56,512]{2,1,0:T(8,128)S(1)}, u32[]{:S(2)}, u32[]{:S(2)}) collective-permute-start(f32[2,56,512]{2,1,0:T(8,128)S(1)} %get-tuple-element.60), channel_id=1, source_target_pairs={{0,240},{16,0},{32,16},{48,32},{64,48},{80,64},{96,80},{112,96},{1... | collective-permute-start | bytes 688136 | tf_op jit(solution)/shard_map/ppermute | solution.py:419
  54.7 9.7 %collective-permute-done.6.src_top = f32[2,32,512]{2,1,0:T(8,128)S(1)} collective-permute-done((f32[2,32,512]{2,1,0:T(8,128)S(1)}, f32[2,32,512]{2,1,0:T(8,128)S(1)}, u32[]{:S(2)}, u32[]{:S(2)}) %collective-permute-start.6) | collective-permute-done | bytes 131104 | tf_op jit(solution)/shard_map/ppermute | solution.py:420
  64.4 3.1 %collective-permute-done.7.src_bot = f32[2,56,512]{2,1,0:T(8,128)S(1)} collective-permute-done((f32[2,56,512]{2,1,0:T(8,128)S(1)}, f32[2,56,512]{2,1,0:T(8,128)S(1)}, u32[]{:S(2)}, u32[]{:S(2)}) %collective-permute-start.7) | collective-permute-done | bytes 229408 | tf_op jit(solution)/shard_map/ppermute | solution.py:419
  67.6 6.2 %step2.1 = (f32[2,256,640]{2,1,0:T(8,128)S(1)}, f32[2,48,640]{2,1,0:T(8,128)S(1)}, f32[2,48,640]{2,1,0:T(8,128)S(1)}, f32[2,336,640]{2,1,0:T(8,128)S(1)}, f32[256,512]{1,0:T(8,128)S(1)}) custom-call(s32[11]{0:T(128)S(1)} %concatenate.9.scal, bf16[128,1152]{1,0:T(8,128)(2,1)S(1)} %bands.1.mats, f32[2,3,256,512]{3,2,1,0:T(8,128)S(1)} %get-tuple-element.43.coef, ...), custom_call_target="tpu_custom_call" | custom-call | flops 3221225472 | bytes 20283392 | tf_op jit(solution)/shard_map/step2/pallas_call | solution.py:401
  74.4 5.1 %collective-permute-start.11 = (f32[2,64,512]{2,1,0:T(8,128)S(1)}, f32[2,64,512]{2,1,0:T(8,128)S(1)}, u32[]{:S(2)}, u32[]{:S(2)}) collective-permute-start(f32[2,64,512]{2,1,0:T(8,128)S(1)} %get-tuple-element.67), channel_id=1, source_target_pairs={{0,240},{16,0},{32,16},{48,32},{64,48},{80,64},{96,80},{112,96},{1... | collective-permute-start | bytes 786440 | tf_op jit(solution)/shard_map/ppermute | solution.py:419
  79.5 5.1 %collective-permute-start.13 = (f32[2,48,640]{2,1,0:T(8,128)S(1)}, f32[2,48,640]{2,1,0:T(8,128)S(1)}, u32[]{:S(2)}, u32[]{:S(2)}) collective-permute-start(f32[2,48,640]{2,1,0:T(8,128)S(1)} %get-tuple-element.69), channel_id=1, source_target_pairs={{0,240},{16,0},{32,16},{48,32},{64,48},{80,64},{96,80},{112,96},{1... | collective-permute-start | bytes 737288 | tf_op jit(solution)/shard_map/ppermute | solution.py:419
  84.6 11.6 %collective-permute-done.12.lam_top = f32[2,48,640]{2,1,0:T(8,128)S(1)} collective-permute-done((f32[2,48,640]{2,1,0:T(8,128)S(1)}, f32[2,48,640]{2,1,0:T(8,128)S(1)}, u32[]{:S(2)}, u32[]{:S(2)}) %collective-permute-start.12) | collective-permute-done | bytes 245792 | tf_op jit(solution)/shard_map/ppermute | solution.py:420
  96.3 6.0 %collective-permute-done.13.lam_bot = f32[2,48,640]{2,1,0:T(8,128)S(1)} collective-permute-done((f32[2,48,640]{2,1,0:T(8,128)S(1)}, f32[2,48,640]{2,1,0:T(8,128)S(1)}, u32[]{:S(2)}, u32[]{:S(2)}) %collective-permute-start.13) | collective-permute-done | bytes 245792 | tf_op jit(solution)/shard_map/ppermute | solution.py:419
  102.3 6.2 %step1.1 = (f32[2,256,640]{2,1,0:T(8,128)S(1)}, f32[2,48,640]{2,1,0:T(8,128)S(1)}, f32[2,48,640]{2,1,0:T(8,128)S(1)}, f32[2,328,640]{2,1,0:T(8,128)S(1)}, f32[256,512]{1,0:T(8,128)S(1)}) custom-call(s32[11]{0:T(128)S(1)} %concatenate.9.scal, bf16[128,1152]{1,0:T(8,128)(2,1)S(1)} %bands.1.mats, f32[2,3,256,512]{3,2,1,0:T(8,128)S(1)} %get-tuple-element.43.coef, ...), custom_call_target="tpu_custom_call" | custom-call | flops 3221225472 | bytes 19767296 | tf_op jit(solution)/shard_map/step1/pallas_call | solution.py:401
  108.6 5.1 %collective-permute-start.15 = (f32[2,48,640]{2,1,0:T(8,128)S(1)}, f32[2,48,640]{2,1,0:T(8,128)S(1)}, u32[]{:S(2)}, u32[]{:S(2)}) collective-permute-start(f32[2,48,640]{2,1,0:T(8,128)S(1)} %get-tuple-element.74), channel_id=1, source_target_pairs={{0,240},{16,0},{32,16},{48,32},{64,48},{80,64},{96,80},{112,96},{1... | collective-permute-start | bytes 737288 | tf_op jit(solution)/shard_map/ppermute | solution.py:419
  113.7 5.6 %collective-permute-done.14.lam_top = f32[2,48,640]{2,1,0:T(8,128)S(1)} collective-permute-done((f32[2,48,640]{2,1,0:T(8,128)S(1)}, f32[2,48,640]{2,1,0:T(8,128)S(1)}, u32[]{:S(2)}, u32[]{:S(2)}) %collective-permute-start.14) | collective-permute-done | bytes 245792 | tf_op jit(solution)/shard_map/ppermute | solution.py:420
  119.2 4.1 %collective-permute-done.15.lam_bot = f32[2,48,640]{2,1,0:T(8,128)S(1)} collective-permute-done((f32[2,48,640]{2,1,0:T(8,128)S(1)}, f32[2,48,640]{2,1,0:T(8,128)S(1)}, u32[]{:S(2)}, u32[]{:S(2)}) %collective-permute-start.15) | collective-permute-done | bytes 245792 | tf_op jit(solution)/shard_map/ppermute | solution.py:419
  123.3 7.4 %step0.1 = (f32[2,256,512]{2,1,0:T(8,128)}, f32[2,256,512]{2,1,0:T(8,128)}, f32[128,512]{1,0:T(8,128)S(1)}, f32[128,512]{1,0:T(8,128)S(1)}) custom-call(s32[11]{0:T(128)S(1)} %concatenate.9.scal, bf16[128,1152]{1,0:T(8,128)(2,1)S(1)} %bands.1.mats, f32[2,3,256,512]{3,2,1,0:T(8,128)S(1)} %get-tuple-element.43.coef, ...), custom_call_target="tpu_custom_call" | custom-call | flops 3221225472 | bytes 18341888 | tf_op jit(solution)/shard_map/step0/pallas_call | solution.py:401
  134.5 6.3 %collective-permute-done.17 = f32[128,512]{1,0:T(8,128)S(1)} collective-permute-done((f32[128,512]{1,0:T(8,128)S(1)}, f32[128,512]{1,0:T(8,128)S(1)}, u32[]{:S(2)}, u32[]{:S(2)}) %collective-permute-start.17) | collective-permute-done | bytes 262176 | tf_op jit(solution)/shard_map/ppermute | solution.py:432
  (39 shorter events, 17.1 us)
Async XLA Ops:
  3.7 38.4 %collective-permute-start.2 = (f32[2,160,512]{2,1,0:T(8,128)S(1)}, f32[2,160,512]{2,1,0:T(8,128)S(1)}, u32[]{:S(2)}, u32[]{:S(2)}) collective-permute-start(f32[2,160,512]{2,1,0:T(8,128)S(1)} %get-tuple-element.49), channel_id=1, source_target_pairs={{0,16},{16,32},{32,48},{48,64},{64,80},{80,96},{96,112},{112,128},... | collective-permute-start | bytes 1966088 | tf_op jit(solution)/shard_map/ppermute | solution.py:420
  7.4 13.1 %copy-start.1 = (f32[2,256,512]{2,1,0:T(8,128)S(1)}, f32[2,256,512]{2,1,0:T(8,128)}, u32[]{:S(2)}) copy-start(f32[2,256,512]{2,1,0:T(8,128)} %film.9) | copy-start | bytes 3145732
  7.4 13.1 %copy-start.2 = (f32[2,256,512]{2,1,0:T(8,128)S(1)}, f32[2,256,512]{2,1,0:T(8,128)}, u32[]{:S(2)}) copy-start(f32[2,256,512]{2,1,0:T(8,128)} %diag.5) | copy-start | bytes 3145732
  7.4 13.1 %copy-start.3 = (f32[2,256,512]{2,1,0:T(8,128)S(1)}, f32[2,256,512]{2,1,0:T(8,128)}, u32[]{:S(2)}) copy-start(f32[2,256,512]{2,1,0:T(8,128)} %fx.5) | copy-start | bytes 3145732
  7.4 13.1 %copy-start.4 = (f32[2,256,512]{2,1,0:T(8,128)S(1)}, f32[2,256,512]{2,1,0:T(8,128)}, u32[]{:S(2)}) copy-start(f32[2,256,512]{2,1,0:T(8,128)} %fy.5) | copy-start | bytes 3145732
  7.4 34.8 %collective-permute-start.3 = (f32[2,160,512]{2,1,0:T(8,128)S(1)}, f32[2,160,512]{2,1,0:T(8,128)S(1)}, u32[]{:S(2)}, u32[]{:S(2)}) collective-permute-start(f32[2,160,512]{2,1,0:T(8,128)S(1)} %get-tuple-element.50), channel_id=1, source_target_pairs={{0,240},{16,0},{32,16},{48,32},{64,48},{80,64},{96,80},{112,96},{1... | collective-permute-start | bytes 1966088 | tf_op jit(solution)/shard_map/ppermute | solution.py:419
  12.8 7.6 %copy-start = (f32[2,4,256,512]{3,2,1,0:T(8,128)S(1)}, f32[2,4,256,512]{3,2,1,0:T(8,128)}, u32[]{:S(2)}) copy-start(f32[2,4,256,512]{3,2,1,0:T(8,128)} %src.11) | copy-start | bytes 12582916
  17.5 8.3 %collective-permute-start = (f32[2,256,128]{2,1,0:T(8,128)S(1)}, f32[2,256,128]{2,1,0:T(8,128)S(1)}, u32[]{:S(2)}, u32[]{:S(2)}) collective-permute-start(f32[2,256,128]{2,1,0:T(8,128)S(1)} %get-tuple-element.44), channel_id=1, source_target_pairs={{0,4},{4,8},{8,12},{12,0},{1,5},{5,9},{9,13},{13,1},{2,6},{6,10},{... | collective-permute-start | bytes 786440 | tf_op jit(solution)/shard_map/ppermute | solution.py:420
  18.9 6.9 %collective-permute-start.1 = (f32[2,256,128]{2,1,0:T(8,128)S(1)}, f32[2,256,128]{2,1,0:T(8,128)S(1)}, u32[]{:S(2)}, u32[]{:S(2)}) collective-permute-start(f32[2,256,128]{2,1,0:T(8,128)S(1)} %get-tuple-element.42.gate), channel_id=1, source_target_pairs={{0,12},{4,0},{8,4},{12,8},{1,13},{5,1},{9,5},{13,9},{2,14},{6,2},{... | collective-permute-start | bytes 786440 | tf_op jit(solution)/shard_map/ppermute | solution.py:419
  28.1 10.6 %collective-permute-start.4 = (f32[2,88,128]{2,1,0:T(8,128)S(1)}, f32[2,88,128]{2,1,0:T(8,128)S(1)}, u32[]{:S(2)}, u32[]{:S(2)}) collective-permute-start(f32[2,88,128]{2,1,0:T(8,128)S(1)} %get-tuple-element.51), channel_id=1, source_target_pairs={{0,16},{16,32},{32,48},{48,64},{64,80},{80,96},{96,112},{112,128},... | collective-permute-start | bytes 270344 | tf_op jit(solution)/shard_map/ppermute | solution.py:420
  28.2 14.0 %collective-permute-start.5 = (f32[2,88,128]{2,1,0:T(8,128)S(1)}, f32[2,88,128]{2,1,0:T(8,128)S(1)}, u32[]{:S(2)}, u32[]{:S(2)}) collective-permute-start(f32[2,88,128]{2,1,0:T(8,128)S(1)} %get-tuple-element.52), channel_id=1, source_target_pairs={{0,240},{16,0},{32,16},{48,32},{64,48},{80,64},{96,80},{112,96},{1... | collective-permute-start | bytes 270344 | tf_op jit(solution)/shard_map/ppermute | solution.py:419
  46.0 21.6 %collective-permute-start.8 = (f32[2,48,640]{2,1,0:T(8,128)S(1)}, f32[2,48,640]{2,1,0:T(8,128)S(1)}, u32[]{:S(2)}, u32[]{:S(2)}) collective-permute-start(f32[2,48,640]{2,1,0:T(8,128)S(1)} %get-tuple-element.62), channel_id=1, source_target_pairs={{0,16},{16,32},{32,48},{48,64},{64,80},{80,96},{96,112},{112,128},... | collective-permute-start | bytes 737288 | tf_op jit(solution)/shard_map/ppermute | solution.py:420
  46.3 21.2 %collective-permute-start.9 = (f32[2,48,640]{2,1,0:T(8,128)S(1)}, f32[2,48,640]{2,1,0:T(8,128)S(1)}, u32[]{:S(2)}, u32[]{:S(2)}) collective-permute-start(f32[2,48,640]{2,1,0:T(8,128)S(1)} %get-tuple-element.63), channel_id=1, source_target_pairs={{0,240},{16,0},{32,16},{48,32},{64,48},{80,64},{96,80},{112,96},{1... | collective-permute-start | bytes 737288 | tf_op jit(solution)/shard_map/ppermute | solution.py:419
  51.7 15.9 %collective-permute-start.7 = (f32[2,56,512]{2,1,0:T(8,128)S(1)}, f32[2,56,512]{2,1,0:T(8,128)S(1)}, u32[]{:S(2)}, u32[]{:S(2)}) collective-permute-start(f32[2,56,512]{2,1,0:T(8,128)S(1)} %get-tuple-element.60), channel_id=1, source_target_pairs={{0,240},{16,0},{32,16},{48,32},{64,48},{80,64},{96,80},{112,96},{1... | collective-permute-start | bytes 688136 | tf_op jit(solution)/shard_map/ppermute | solution.py:419
  54.6 9.8 %collective-permute-start.6 = (f32[2,32,512]{2,1,0:T(8,128)S(1)}, f32[2,32,512]{2,1,0:T(8,128)S(1)}, u32[]{:S(2)}, u32[]{:S(2)}) collective-permute-start(f32[2,32,512]{2,1,0:T(8,128)S(1)} %get-tuple-element.59), channel_id=1, source_target_pairs={{0,16},{16,32},{32,48},{48,64},{64,80},{80,96},{96,112},{112,128},... | collective-permute-start | bytes 393224 | tf_op jit(solution)/shard_map/ppermute | solution.py:420
  73.8 28.5 %collective-permute-start.10 = (f32[2,64,512]{2,1,0:T(8,128)S(1)}, f32[2,64,512]{2,1,0:T(8,128)S(1)}, u32[]{:S(2)}, u32[]{:S(2)}) collective-permute-start(f32[2,64,512]{2,1,0:T(8,128)S(1)} %get-tuple-element.66), channel_id=1, source_target_pairs={{0,16},{16,32},{32,48},{48,64},{64,80},{80,96},{96,112},{112,128},... | collective-permute-start | bytes 786440 | tf_op jit(solution)/shard_map/ppermute | solution.py:420
  74.4 27.9 %collective-permute-start.11 = (f32[2,64,512]{2,1,0:T(8,128)S(1)}, f32[2,64,512]{2,1,0:T(8,128)S(1)}, u32[]{:S(2)}, u32[]{:S(2)}) collective-permute-start(f32[2,64,512]{2,1,0:T(8,128)S(1)} %get-tuple-element.67), channel_id=1, source_target_pairs={{0,240},{16,0},{32,16},{48,32},{64,48},{80,64},{96,80},{112,96},{1... | collective-permute-start | bytes 786440 | tf_op jit(solution)/shard_map/ppermute | solution.py:419
  79.5 16.7 %collective-permute-start.12 = (f32[2,48,640]{2,1,0:T(8,128)S(1)}, f32[2,48,640]{2,1,0:T(8,128)S(1)}, u32[]{:S(2)}, u32[]{:S(2)}) collective-permute-start(f32[2,48,640]{2,1,0:T(8,128)S(1)} %get-tuple-element.68), channel_id=1, source_target_pairs={{0,16},{16,32},{32,48},{48,64},{64,80},{80,96},{96,112},{112,128},... | collective-permute-start | bytes 737288 | tf_op jit(solution)/shard_map/ppermute | solution.py:420
  79.5 22.8 %collective-permute-start.13 = (f32[2,48,640]{2,1,0:T(8,128)S(1)}, f32[2,48,640]{2,1,0:T(8,128)S(1)}, u32[]{:S(2)}, u32[]{:S(2)}) collective-permute-start(f32[2,48,640]{2,1,0:T(8,128)S(1)} %get-tuple-element.69), channel_id=1, source_target_pairs={{0,240},{16,0},{32,16},{48,32},{64,48},{80,64},{96,80},{112,96},{1... | collective-permute-start | bytes 737288 | tf_op jit(solution)/shard_map/ppermute | solution.py:419
  108.5 10.7 %collective-permute-start.14 = (f32[2,48,640]{2,1,0:T(8,128)S(1)}, f32[2,48,640]{2,1,0:T(8,128)S(1)}, u32[]{:S(2)}, u32[]{:S(2)}) collective-permute-start(f32[2,48,640]{2,1,0:T(8,128)S(1)} %get-tuple-element.73), channel_id=1, source_target_pairs={{0,16},{16,32},{32,48},{48,64},{64,80},{80,96},{96,112},{112,128},... | collective-permute-start | bytes 737288 | tf_op jit(solution)/shard_map/ppermute | solution.py:420
  108.6 14.7 %collective-permute-start.15 = (f32[2,48,640]{2,1,0:T(8,128)S(1)}, f32[2,48,640]{2,1,0:T(8,128)S(1)}, u32[]{:S(2)}, u32[]{:S(2)}) collective-permute-start(f32[2,48,640]{2,1,0:T(8,128)S(1)} %get-tuple-element.74), channel_id=1, source_target_pairs={{0,240},{16,0},{32,16},{48,32},{64,48},{80,64},{96,80},{112,96},{1... | collective-permute-start | bytes 737288 | tf_op jit(solution)/shard_map/ppermute | solution.py:419
  130.7 2.5 %collective-permute-start.16 = (f32[128,512]{1,0:T(8,128)S(1)}, f32[128,512]{1,0:T(8,128)S(1)}, u32[]{:S(2)}, u32[]{:S(2)}) collective-permute-start(f32[128,512]{1,0:T(8,128)S(1)} %get-tuple-element.80), channel_id=1, source_target_pairs={{0,1},{1,0},{2,3},{3,2},{4,5},{5,4},{6,7},{7,6},{8,9},{9,8},{10,11... | collective-permute-start | bytes 786440 | tf_op jit(solution)/shard_map/ppermute | solution.py:431
  133.2 7.6 %collective-permute-start.17 = (f32[128,512]{1,0:T(8,128)S(1)}, f32[128,512]{1,0:T(8,128)S(1)}, u32[]{:S(2)}, u32[]{:S(2)}) collective-permute-start(f32[128,512]{1,0:T(8,128)S(1)} %add.11), channel_id=1, source_target_pairs={{0,2},{1,3},{2,0},{3,1},{4,6},{5,7},{6,4},{7,5},{8,10},{9,11},{10,... | collective-permute-start | bytes 786440 | tf_op jit(solution)/shard_map/ppermute | solution.py:432
  140.9 2.5 %collective-permute-start.18 = (f32[128,512]{1,0:T(8,128)S(1)}, f32[128,512]{1,0:T(8,128)S(1)}, u32[]{:S(2)}, u32[]{:S(2)}) collective-permute-start(f32[128,512]{1,0:T(8,128)S(1)} %add.12), channel_id=1, source_target_pairs={{0,1},{1,0},{2,3},{3,2},{4,5},{5,4},{6,7},{7,6},{8,9},{9,8},{10,11... | collective-permute-start | bytes 786440 | tf_op jit(solution)/shard_map/ppermute | solution.py:433
  (1 other events, 2.6 us)
